TPU v7x, 32 devices: a whole 2x2x4 slice. The times are simulated.
32 devices in a mesh: ep: 8 (over z, x), ws: 4 (over y, core).
Axes of the slice: x: 2, y: 2, z: 4, core: 2. Of those that a mesh axis runs over, the one named last changes fastest.
Arguments:
- x_in: bfloat16 [4096, 2048], P(('ep', 'ws')), may hold values from -6 to 6
- gain_attn: bfloat16 [2048], P(('ep', 'ws')), may hold values from 0.5 to 1.5
- gain_ffn: bfloat16 [2048], P(('ep', 'ws')), may hold values from 0.5 to 1.5
- key_value_weight: bfloat16 [2048, 4096], P(None, ('ep', 'ws')), may hold values from -0.125 to 0.125
- w_query: bfloat16 [8, 2048, 2048], P('ep', None, 'ws'), may hold values from -0.125 to 0.125
- w_output: bfloat16 [8, 2048, 2048], P('ep', 'ws'), may hold values from -0.5 to 0.5
- w_in: bfloat16 [8, 2048, 2, 5632], P('ep', None, None, 'ws'), may hold values from -0.125 to 0.125
- w_out: bfloat16 [8, 5632, 2048], P('ep', 'ws'), may hold values from -0.078125 to 0.078125
- gate_attn: float32 [4096, 2], P(('ep', 'ws')), may hold values from 0.3 to 1
- gate_ffn: float32 [4096, 2], P(('ep', 'ws')), may hold values from 0.3 to 1
- route_attn: int32 [4096, 2], P(('ep', 'ws')), may hold values from 0 to 7, as said below
- slot_attn: int32 [4096, 2], P(('ep', 'ws')), may hold values from 0 to 127, as said below
- route_ffn: int32 [4096, 2], P(('ep', 'ws')), may hold values from 0 to 7, as said below
- slot_ffn: int32 [4096, 2], P(('ep', 'ws')), may hold values from 0 to 127, as said below
- cotangent: bfloat16 [4096, 2048], P(('ep', 'ws')), may hold values from -6 to 6
Outputs:
- out: bfloat16 [4096, 2048], P(('ep', 'ws'))
- grad_input: float32 [4096, 2048], P(('ep', 'ws'))
- grad_gain_attn: float32 [2048], P(('ep', 'ws'))
- grad_gain_ffn: float32 [2048], P(('ep', 'ws'))
- grad_w_kv: float32 [2048, 4096], P(None, ('ep', 'ws'))
- grad_w_query: float32 [8, 2048, 2048], P('ep', None, 'ws')
- grad_w_output: float32 [8, 2048, 2048], P('ep', 'ws')
- grad_w_in: float32 [8, 2048, 2, 5632], P('ep', None, None, 'ws')
- grad_w_out: float32 [8, 5632, 2048], P('ep', 'ws')
Inputs may be any that keep to these rules, and one draw needn't show every extreme that they name: `route_attn`: each token names 2 different experts. `route_ffn`: each token names 2 different experts. `slot_attn`: a pair's rank, in an order drawn for each device's 128 tokens, among that device's pairs of the same expert. `slot_ffn`: a pair's rank, in an order drawn for each device's 128 tokens, among that device's pairs of the same expert.
All inputs are finite; a program needn't handle non-finite values.
Results may differ from a plain program's by a relative error of at most 0.018.
Values may be sent and summed in bfloat16 or wider, within the bound.
A program may use at most 384 MiB of HBM per device.

v0:
```python
import jax
import jax.numpy as jnp
from jax import lax
from jax.sharding import PartitionSpec as P

KEY_VALUE_HEADS = 16
HEAD_SIZE = 128
MIXTURE_EXPERTS = 8
CHOSEN_EXPERTS = 2
BLOCK = 256
CAP = 36


EPS = 1e-06
very_negative = -1e30


def dispatch(send):
    return lax.all_to_all(send, "ep", split_axis=0, concat_axis=0, tiled=True)


def combine(back):
    return lax.all_to_all(back, "ep", split_axis=0, concat_axis=0, tiled=True)


def slot_table(routes, slots):
    valid = slots < CAP
    target = jnp.where(valid, routes * CAP + slots, -1).reshape(-1)
    places = lax.broadcasted_iota(jnp.int32, (MIXTURE_EXPERTS * CAP, target.shape[0]), 0)
    table = (places == target[None, :]).astype(jnp.bfloat16)
    per_token = jnp.sum(table.reshape(MIXTURE_EXPERTS * CAP, -1, CHOSEN_EXPERTS), -1)
    return (table, per_token, jnp.maximum(target, 0), valid.reshape(-1, 1))


def expert_pick(slot_values, index, valid):
    return jnp.where(valid, jnp.take(slot_values, index, axis=0), jnp.zeros((), slot_values.dtype))


def spread(rows, group):
    width = rows.shape[-1]
    copies = jnp.broadcast_to(
        rows.reshape(MIXTURE_EXPERTS, 1, CAP, width), (MIXTURE_EXPERTS, group, CAP, width)
    )
    return copies.reshape(MIXTURE_EXPERTS * group, CAP, width)


def split_heads(rows, group):
    width = rows.shape[-1] // group
    return (
        rows.reshape(MIXTURE_EXPERTS, CAP, group, width)
        .transpose(0, 2, 1, 3)
        .reshape(MIXTURE_EXPERTS * group, CAP, width)
    )


def join_heads(back, group):
    width = back.shape[-1]
    return (
        back.reshape(MIXTURE_EXPERTS, group, CAP, width)
        .transpose(0, 2, 1, 3)
        .reshape(MIXTURE_EXPERTS * CAP, group * width)
    )


def sum_groups(back, group):
    width = back.shape[-1]
    return jnp.sum(back.reshape(MIXTURE_EXPERTS, group, CAP, width).astype(jnp.float32), 1).reshape(
        MIXTURE_EXPERTS * CAP, width
    )


def norm_back(grad, unit, inverse, gain):
    gain_grad = jnp.sum(grad * unit, 0)
    scaled = grad * gain
    return (inverse * (scaled - unit * jnp.mean(scaled * unit, -1, keepdims=True)), gain_grad)


def scores_of(query_rows, key_rows, allowed):
    attention_scores = jnp.einsum(
        "tkhd,shd->htks", query_rows, key_rows, preferred_element_type=jnp.float32
    ) * HEAD_SIZE ** (-0.5)
    return jnp.where(allowed, attention_scores, very_negative)


def local(
    x_in,
    gain_attn,
    gain_ffn,
    key_value_weight,
    w_query,
    w_output,
    w_in,
    w_out,
    gate_attn,
    gate_ffn,
    route_attn,
    slot_attn,
    route_ffn,
    slot_ffn,
    cotangent,
):
    n_ep = lax.axis_size("ep")
    group = n_ep // MIXTURE_EXPERTS
    local_tokens = x_in.shape[0]
    width = x_in.shape[1]
    key_value_width = KEY_VALUE_HEADS * HEAD_SIZE
    shared = (
        lax.all_gather(key_value_weight, ("ep", "ws"), axis=1, tiled=True),
        lax.all_gather(gain_attn, ("ep", "ws"), axis=0, tiled=True),
        lax.all_gather(gain_ffn, ("ep", "ws"), axis=0, tiled=True),
    )
    kv_full = shared[0]
    gain_one = shared[1].astype(jnp.float32)
    gain_two = shared[2].astype(jnp.float32)
    gathered = (
        lax.all_gather(w_query, "ws", axis=2, tiled=True),
        lax.all_gather(w_output, "ws", axis=1, tiled=True),
        lax.all_gather(w_in, "ws", axis=3, tiled=True),
        lax.all_gather(w_out, "ws", axis=1, tiled=True),
    )
    query_full, output_full, first_full, second_full = (
        gathered[0][0],
        gathered[1][0],
        gathered[2][0],
        gathered[3][0],
    )
    inputs = x_in.astype(jnp.float32)
    inverse_one = lax.rsqrt(jnp.mean(inputs * inputs, -1, keepdims=True) + EPS)
    unit_one = inputs * inverse_one
    normed = (unit_one * gain_one).astype(jnp.bfloat16)
    key_value_rows = jnp.dot(normed, kv_full, preferred_element_type=jnp.float32).astype(
        jnp.bfloat16
    )
    key_value_sequence = lax.all_gather(key_value_rows, "ws", axis=0, tiled=True)
    key_rows = key_value_sequence[:, :key_value_width].reshape(-1, KEY_VALUE_HEADS, HEAD_SIZE)
    value_rows = key_value_sequence[:, key_value_width:].reshape(-1, KEY_VALUE_HEADS, HEAD_SIZE)
    key_count = key_rows.shape[0]
    attn_table, attn_tokens, attention_index, attention_valid = slot_table(route_attn, slot_attn)
    ffn_table, ffn_tokens, ffn_index, ffn_valid = slot_table(route_ffn, slot_ffn)
    rows_normed = jnp.dot(attn_tokens, normed, preferred_element_type=jnp.float32).astype(
        jnp.bfloat16
    )
    owner_normed = dispatch(spread(rows_normed, group)).reshape(-1, width)
    owner_query = jnp.dot(owner_normed, query_full, preferred_element_type=jnp.float32).astype(
        jnp.bfloat16
    )
    query_backward = join_heads(combine(owner_query.reshape(n_ep, CAP, -1)), group)
    query_rows = expert_pick(query_backward, attention_index, attention_valid).reshape(
        local_tokens, CHOSEN_EXPERTS, KEY_VALUE_HEADS, HEAD_SIZE
    )
    positions = (lax.axis_index("ws") * local_tokens + jnp.arange(local_tokens)) // BLOCK
    key_blocks = jnp.arange(key_count) // BLOCK
    allowed = (key_blocks[None, :] <= positions[:, None])[None, :, None, :]
    attention_scores = scores_of(query_rows, key_rows, allowed)
    log_total = jax.scipy.special.logsumexp(attention_scores, axis=-1, keepdims=True)
    probs_low = jnp.exp(attention_scores - log_total).astype(jnp.bfloat16)
    mixed_output = jnp.einsum(
        "htks,shd->tkhd", probs_low, value_rows, preferred_element_type=jnp.float32
    ).astype(jnp.bfloat16)
    mixed_output = mixed_output.reshape(local_tokens * CHOSEN_EXPERTS, -1)
    rows_mixed = jnp.dot(attn_table, mixed_output, preferred_element_type=jnp.float32).astype(
        jnp.bfloat16
    )
    owner_mixed = dispatch(split_heads(rows_mixed, group)).reshape(-1, query_full.shape[1])
    owner_attn = jnp.dot(owner_mixed, output_full, preferred_element_type=jnp.float32).astype(
        jnp.bfloat16
    )
    attn_slots = sum_groups(combine(owner_attn.reshape(n_ep, CAP, -1)), group)
    attn_pairs = expert_pick(attn_slots, attention_index, attention_valid).reshape(
        local_tokens, CHOSEN_EXPERTS, -1
    )
    hidden_state = inputs + jnp.sum(gate_attn[:, :, None] * attn_pairs, 1)
    inverse_two = lax.rsqrt(jnp.mean(hidden_state * hidden_state, -1, keepdims=True) + EPS)
    unit_two = hidden_state * inverse_two
    normed_two = (unit_two * gain_two).astype(jnp.bfloat16)
    rows_two = jnp.dot(ffn_tokens, normed_two, preferred_element_type=jnp.float32).astype(
        jnp.bfloat16
    )
    expert_rows = dispatch(spread(rows_two, group)).reshape(-1, width)
    pre_act = jnp.einsum("rd,djf->rjf", expert_rows, first_full, preferred_element_type=jnp.float32)
    gate_pre = pre_act[:, 0]
    up_pre = pre_act[:, 1]
    activated = (jax.nn.silu(gate_pre) * up_pre).astype(jnp.bfloat16)
    owner_ffn = jnp.dot(activated, second_full, preferred_element_type=jnp.float32).astype(
        jnp.bfloat16
    )
    ffn_slots = sum_groups(combine(owner_ffn.reshape(n_ep, CAP, -1)), group)
    ffn_pairs = expert_pick(ffn_slots, ffn_index, ffn_valid).reshape(
        local_tokens, CHOSEN_EXPERTS, -1
    )
    result = hidden_state + jnp.sum(gate_ffn[:, :, None] * ffn_pairs, 1)
    grad_out = cotangent.astype(jnp.float32)
    grad_ffn_pairs = (
        (gate_ffn[:, :, None] * grad_out[:, None, :])
        .astype(jnp.bfloat16)
        .reshape(local_tokens * CHOSEN_EXPERTS, -1)
    )
    grad_ffn_slots = jnp.dot(ffn_table, grad_ffn_pairs, preferred_element_type=jnp.float32).astype(
        jnp.bfloat16
    )
    expert_grad = dispatch(spread(grad_ffn_slots, group)).reshape(-1, width)
    grad_act = jnp.dot(expert_grad, second_full.T, preferred_element_type=jnp.float32)
    sigmoid_gate = jax.nn.sigmoid(gate_pre)
    grad_up = grad_act * gate_pre * sigmoid_gate
    grad_gate = grad_act * up_pre * sigmoid_gate * (1.0 + gate_pre * (1.0 - sigmoid_gate))
    grad_pre = jnp.stack([grad_gate, grad_up], 1).astype(jnp.bfloat16)
    grad_second = jnp.dot(activated.T, expert_grad, preferred_element_type=jnp.float32)
    grad_first = jnp.einsum(
        "rd,rjf->djf", expert_rows, grad_pre, preferred_element_type=jnp.float32
    )
    back_two = jnp.einsum(
        "rjf,djf->rd", grad_pre, first_full, preferred_element_type=jnp.float32
    ).astype(jnp.bfloat16)
    back_slots = sum_groups(combine(back_two.reshape(n_ep, CAP, -1)), group)
    grad_normed_two = jnp.sum(
        expert_pick(back_slots, ffn_index, ffn_valid).reshape(local_tokens, CHOSEN_EXPERTS, -1), 1
    )
    grad_hidden_norm, grad_gain_two = norm_back(grad_normed_two, unit_two, inverse_two, gain_two)
    grad_hidden = grad_out + grad_hidden_norm
    grad_attn_pairs = (
        (gate_attn[:, :, None] * grad_hidden[:, None, :])
        .astype(jnp.bfloat16)
        .reshape(local_tokens * CHOSEN_EXPERTS, -1)
    )
    grad_attn_slots = jnp.dot(
        attn_table, grad_attn_pairs, preferred_element_type=jnp.float32
    ).astype(jnp.bfloat16)
    owner_grad_attn = dispatch(spread(grad_attn_slots, group)).reshape(-1, width)
    back_mixed = jnp.dot(owner_grad_attn, output_full.T, preferred_element_type=jnp.float32).astype(
        jnp.bfloat16
    )
    grad_output = jnp.dot(owner_mixed.T, owner_grad_attn, preferred_element_type=jnp.float32)
    mixed_backward = join_heads(combine(back_mixed.reshape(n_ep, CAP, -1)), group)
    mixed_gradient = expert_pick(mixed_backward, attention_index, attention_valid).reshape(
        local_tokens, CHOSEN_EXPERTS, KEY_VALUE_HEADS, HEAD_SIZE
    )
    probs_again = jnp.exp(scores_of(query_rows, key_rows, allowed) - log_total)
    grad_probs = jnp.einsum(
        "tkhd,shd->htks", mixed_gradient, value_rows, preferred_element_type=jnp.float32
    )
    centred = jnp.sum(probs_again * grad_probs, -1, keepdims=True)
    grad_scores = (probs_again * (grad_probs - centred)).astype(jnp.bfloat16)
    grad_queries = jnp.einsum(
        "htks,shd->tkhd", grad_scores, key_rows, preferred_element_type=jnp.float32
    ) * HEAD_SIZE ** (-0.5)
    grad_queries = grad_queries.astype(jnp.bfloat16).reshape(local_tokens * CHOSEN_EXPERTS, -1)
    grad_keys = jnp.einsum(
        "htks,tkhd->shd", grad_scores, query_rows, preferred_element_type=jnp.float32
    ) * HEAD_SIZE ** (-0.5)
    grad_values = jnp.einsum(
        "htks,tkhd->shd", probs_low, mixed_gradient, preferred_element_type=jnp.float32
    )
    grad_kv_terms = jnp.concatenate(
        [grad_keys.reshape(key_count, -1), grad_values.reshape(key_count, -1)], 1
    )
    grad_query_slots = jnp.dot(attn_table, grad_queries, preferred_element_type=jnp.float32).astype(
        jnp.bfloat16
    )
    owner_grad_query = dispatch(split_heads(grad_query_slots, group)).reshape(
        -1, query_full.shape[1]
    )
    back_normed = jnp.dot(
        owner_grad_query, query_full.T, preferred_element_type=jnp.float32
    ).astype(jnp.bfloat16)
    grad_query = jnp.dot(owner_normed.T, owner_grad_query, preferred_element_type=jnp.float32)
    normed_back = sum_groups(combine(back_normed.reshape(n_ep, CAP, -1)), group)
    grad_normed = jnp.sum(
        expert_pick(normed_back, attention_index, attention_valid).reshape(
            local_tokens, CHOSEN_EXPERTS, -1
        ),
        1,
    )
    grad_keyval = lax.psum_scatter(grad_kv_terms, "ws", scatter_dimension=0, tiled=True).astype(
        jnp.bfloat16
    )
    grad_normed = grad_normed + jnp.dot(grad_keyval, kv_full.T, preferred_element_type=jnp.float32)
    grad_kv = jnp.dot(normed.T, grad_keyval, preferred_element_type=jnp.float32)
    grad_input_norm, grad_gain_one = norm_back(grad_normed, unit_one, inverse_one, gain_one)
    shared_grads = (
        lax.psum_scatter(grad_kv, ("ep", "ws"), scatter_dimension=1, tiled=True),
        lax.psum_scatter(grad_gain_one, ("ep", "ws"), scatter_dimension=0, tiled=True),
        lax.psum_scatter(grad_gain_two, ("ep", "ws"), scatter_dimension=0, tiled=True),
    )
    grad_kv_shard, gain_one_shard, gain_two_shard = (
        shared_grads[0],
        shared_grads[1],
        shared_grads[2],
    )
    grad_input = grad_hidden + grad_input_norm
    block_grads = (
        lax.psum_scatter(
            grad_query[None].astype(jnp.bfloat16), "ws", scatter_dimension=2, tiled=True
        ).astype(jnp.float32),
        lax.psum_scatter(
            grad_output[None].astype(jnp.bfloat16), "ws", scatter_dimension=1, tiled=True
        ).astype(jnp.float32),
        lax.psum_scatter(
            grad_first[None].astype(jnp.bfloat16), "ws", scatter_dimension=3, tiled=True
        ).astype(jnp.float32),
        lax.psum_scatter(
            grad_second[None].astype(jnp.bfloat16), "ws", scatter_dimension=1, tiled=True
        ).astype(jnp.float32),
    )
    return (
        result.astype(jnp.bfloat16),
        grad_input,
        gain_one_shard,
        gain_two_shard,
        grad_kv_shard,
        block_grads[0],
        block_grads[1],
        block_grads[2],
        block_grads[3],
    )


def solution(mesh):
    placed = (
        P(("ep", "ws"), None),
        P(("ep", "ws")),
        P(("ep", "ws")),
        P(None, ("ep", "ws")),
        P("ep", None, "ws"),
        P("ep", "ws", None),
        P("ep", None, None, "ws"),
        P("ep", "ws", None),
        P(("ep", "ws"), None),
        P(("ep", "ws"), None),
        P(("ep", "ws"), None),
        P(("ep", "ws"), None),
        P(("ep", "ws"), None),
        P(("ep", "ws"), None),
        P(("ep", "ws"), None),
    )
    return jax.shard_map(
        local,
        mesh=mesh,
        in_specs=placed,
        out_specs=(
            P(("ep", "ws"), None),
            P(("ep", "ws"), None),
            P(("ep", "ws")),
            P(("ep", "ws")),
            P(None, ("ep", "ws")),
            P("ep", None, "ws"),
            P("ep", "ws", None),
            P("ep", None, None, "ws"),
            P("ep", "ws", None),
        ),
        check_vma=False,
    )
```

profile of v0, /device:TPU:1, one launch (start us, length us, event | category | flops | bytes accessed | tf_op | source)
XLA Modules:
  0.0 2069.6 jit_solution(1595892979517082909)
XLA Ops:
  9.3 43.5 %all-reduce.5 = (bf16[2048]{0:T(1024)(128)(2,1)S(1)}, bf16[2048]{0:T(1024)(128)(2,1)S(1)}) all-reduce(bf16[2048]{0:T(1024)(128)(2,1)S(1)} %dynamic-update-slice, bf16[2048]{0:T(1024)(128)(2,1)S(1)} %dynamic-update-slice.1), channel_id=1, replica_groups=mesh['ep'=8,'ws'=4] {'ep','ws'}, use_global_device_ids=true, to_apply=%add | all-reduce | flops 4096 | bytes 16384
  53.0 107.8 %all-gather.7.cloned.1.call-done = bf16[2048,4096]{1,0:T(8,128)(2,1)} async-done(((bf16[2048,128]{1,0:T(8,128)(2,1)}), bf16[2048,4096]{1,0:T(8,128)(2,1)}) %all-gather.7.cloned.1.call-update) | async-done | bytes 16777232 | tf_op jit(solution)/shard_map/all_gather | solution.py:108
  185.2 34.6 %all_to_all.60 = bf16[8,36,2048]{2,1,0:T(8,128)(2,1)S(1)} all-to-all(bf16[8,36,2048]{2,1,0:T(8,128)(2,1)} %reshape_reshape.12), channel_id=1, replica_groups=mesh['ep'=8,'ws'=4] {'ep'}, dimensions={0} | all-to-all | bytes 2359296 | tf_op jit(solution)/shard_map/all_to_all | solution.py:19
  236.4 29.1 %all-to-all-done.1 = bf16[8,36,2048]{2,1,0:T(8,128)(2,1)} async-done(((bf16[8,36,2048]{2,1,0:T(8,128)(2,1)}), bf16[8,36,2048]{2,1,0:T(8,128)(2,1)}, u32[]{:S(2)}, u32[]{:S(2)}) %all-to-all-start.1) | async-done | bytes 1179680 | tf_op jit(solution)/shard_map/all_to_all | solution.py:23
  293.7 35.6 %all_to_all.61 = bf16[8,36,2048]{2,1,0:T(8,128)(2,1)S(1)} all-to-all(bf16[8,36,2048]{2,1,0:T(8,128)(2,1)} %reshape_transpose_reshape.13), channel_id=1, replica_groups=mesh['ep'=8,'ws'=4] {'ep'}, dimensions={0} | all-to-all | bytes 2359296 | tf_op jit(solution)/shard_map/all_to_all | solution.py:19
  355.8 22.7 %all-to-all-done.3 = bf16[8,36,2048]{2,1,0:T(8,128)(2,1)} async-done(((bf16[8,36,2048]{2,1,0:T(8,128)(2,1)}), bf16[8,36,2048]{2,1,0:T(8,128)(2,1)}, u32[]{:S(2)}, u32[]{:S(2)}) %all-to-all-start.3) | async-done | bytes 1179680 | tf_op jit(solution)/shard_map/all_to_all | solution.py:23
  421.2 28.4 %all-to-all-done.4 = bf16[8,36,2048]{2,1,0:T(8,128)(2,1)S(1)} async-done(((bf16[8,36,2048]{2,1,0:T(8,128)(2,1)}), bf16[8,36,2048]{2,1,0:T(8,128)(2,1)S(1)}, u32[]{:S(2)}, u32[]{:S(2)}) %all-to-all-start.4) | async-done | bytes 1179680 | tf_op jit(solution)/shard_map/all_to_all | solution.py:19
  449.9 140.7 %all-gather.15.cloned.1.call-done = bf16[1,2048,2,5632]{3,1,2,0:T(8,128)(2,1)} async-done(((bf16[1,2048,2,1408]{3,1,2,0:T(8,128)(2,1)}), bf16[1,2048,2,5632]{3,1,2,0:T(8,128)(2,1)}) %all-gather.15.cloned.1.call-update) | async-done | bytes 46137360 | tf_op jit(solution)/shard_map/all_gather | solution.py:118
  590.6 28.9 %fusion.2 = f32[288,2,5632]{2,0,1:T(8,128)} fusion(bf16[288,2048,1]{1,0,2:T(8,128)(2,1)S(1)} %reshape.398, bf16[1,2048,2,5632]{3,1,2,0:T(8,128)(2,1)} %all-gather.15.cloned.1.call-done), kind=kOutput, calls=%fused_computation.8 | convolution fusion | flops 13287555072 | bytes 60293120 | tf_op jit(solution)/shard_map/rd,djf->rjf/dot_general | solution.py:180
  626.4 108.9 %all-gather.17.cloned.1.call-done = bf16[1,5632,2048]{2,1,0:T(8,128)(2,1)} async-done(((bf16[1,1408,2048]{2,1,0:T(8,128)(2,1)}), bf16[1,5632,2048]{2,1,0:T(8,128)(2,1)}) %all-gather.17.cloned.1.call-update) | async-done | bytes 23068688 | tf_op jit(solution)/shard_map/all_gather | solution.py:119
  735.3 25.4 %fusion.32 = (bf16[288,1,5632]{2,0,1:T(8,128)(2,1)}, bf16[288,1,5632]{2,0,1:T(8,128)(2,1)}) fusion(f32[288,2,5632]{2,0,1:T(8,128)} %fusion.2, bf16[288,2048]{1,0:T(8,128)(2,1)S(1)} %copy-done.28, bf16[1,5632,2048]{2,1,0:T(8,128)(2,1)} %all-gather.17.cloned.1.call-done), kind=kOutput, calls=%fused_computation.56 | convolution fusion | flops 6664863744 | bytes 43712512 | tf_op jit(solution)/shard_map/dot_general | solution.py:202
  828.7 25.2 %all-to-all-done.5 = bf16[8,36,2048]{2,1,0:T(8,128)(2,1)} async-done(((bf16[8,36,2048]{2,1,0:T(8,128)(2,1)}), bf16[8,36,2048]{2,1,0:T(8,128)(2,1)}, u32[]{:S(2)}, u32[]{:S(2)}) %all-to-all-start.5) | async-done | bytes 1179680 | tf_op jit(solution)/shard_map/all_to_all | solution.py:23
  888.4 35.1 %all_to_all.62 = bf16[8,36,2048]{2,1,0:T(8,128)(2,1)S(1)} all-to-all(bf16[8,36,2048]{2,1,0:T(8,128)(2,1)S(1)} %reshape_reshape.15), channel_id=1, replica_groups=mesh['ep'=8,'ws'=4] {'ep'}, dimensions={0} | all-to-all | bytes 2359296 | tf_op jit(solution)/shard_map/all_to_all | solution.py:19
  932.4 34.7 %all_to_all.63 = bf16[8,36,2048]{2,1,0:T(8,128)(2,1)} all-to-all(bf16[8,36,2048]{2,1,0:T(8,128)(2,1)S(1)} %reshape.308), channel_id=1, replica_groups=mesh['ep'=8,'ws'=4] {'ep'}, dimensions={0} | all-to-all | bytes 2359296 | tf_op jit(solution)/shard_map/all_to_all | solution.py:23
  1015.4 33.9 %all_to_all.64 = bf16[8,36,2048]{2,1,0:T(8,128)(2,1)S(1)} all-to-all(bf16[8,36,2048]{2,1,0:T(8,128)(2,1)S(1)} %reshape_transpose_reshape.15), channel_id=1, replica_groups=mesh['ep'=8,'ws'=4] {'ep'}, dimensions={0} | all-to-all | bytes 2359296 | tf_op jit(solution)/shard_map/all_to_all | solution.py:19
  1077.1 33.7 %convert_bitcast_fusion = bf16[1,2048,2,5632]{3,1,2,0:T(8,128)(2,1)} fusion(bf16[288,2048,1]{1,0,2:T(8,128)(2,1)S(1)} %copy-done.23, bf16[288,1,5632]{2,0,1:T(8,128)(2,1)} %get-tuple-element.58, bf16[288,1,5632]{2,0,1:T(8,128)(2,1)} %get-tuple-element.57), kind=kOutput, calls=%fused_computation.10 | convolution fusion | flops 13323599872 | bytes 53805056 | tf_op jit(solution)/shard_map/rd,rjf->djf/dot_general | solution.py:208
  1110.8 113.6 %copy.116 = bf16[1,2048,2,5632]{1,2,0,3:T(2,128)(2,1)} copy(bf16[1,2048,2,5632]{3,1,2,0:T(8,128)(2,1)} %convert_bitcast_fusion) | data formatting | bytes 92274688
  1224.4 37.8 %copy.124 = bf16[704,8,2,2048]{3,1,2,0:T(8,128)(2,1)} copy(bf16[704,8,2,2048]{3,2,1,0:T(2,128)(2,1)} %bitcast.182) | data formatting | bytes 92274688
  1293.4 29.7 %all-to-all-done.11 = bf16[8,36,2048]{2,1,0:T(8,128)(2,1)} async-done(((bf16[8,36,2048]{2,1,0:T(8,128)(2,1)}), bf16[8,36,2048]{2,1,0:T(8,128)(2,1)}, u32[]{:S(2)}, u32[]{:S(2)}) %all-to-all-start.11) | async-done | bytes 1179680 | tf_op jit(solution)/shard_map/all_to_all | solution.py:23
  1353.6 38.9 %all-reduce.4 = (f32[2048]{0:T(1024)S(1)}, f32[2048]{0:T(1024)S(1)}) all-reduce(f32[2048]{0:T(1024)S(1)} %get-tuple-element.49, f32[2048]{0:T(1024)S(1)} %copy-done.36), channel_id=3, replica_groups=mesh['ep'=8,'ws'=4] {'ep','ws'}, use_global_device_ids=true, to_apply=%region_15.18.clone | all-reduce | flops 4096 | bytes 32768
  1417.4 284.1 %reduce-scatter.19.cloned.1.call-done = bf16[1408,4096]{1,0:T(8,128)(2,1)} async-done(((bf16[5632,4096]{1,0:T(8,128)(2,1)}), bf16[1408,4096]{1,0:T(8,128)(2,1)}) %reduce-scatter.19.cloned.1.call-update) | async-done | bytes 11534352
  1721.2 29.0 %copy.117 = bf16[1,2048,2,1408]{3,1,2,0:T(8,128)(2,1)} copy(bf16[1,2048,2,1408]{1,2,0,3:T(2,128)(2,1)} %bitcast.183) | data formatting | bytes 23068672
  1750.2 23.6 %copy.101 = f32[1,2048,2,1408]{3,2,1,0:T(2,128)} copy(bf16[1,2048,2,1408]{3,1,2,0:T(8,128)(2,1)} %copy.117) | data formatting | bytes 34603008
  1773.8 288.8 %reduce-scatter.11.cloned.1.call-done = f32[2048,128]{1,0:T(8,128)} async-done(((f32[2048,4096]{1,0:T(8,128)}), f32[2048,128]{1,0:T(8,128)}) %reduce-scatter.11.cloned.1.call-update) | async-done | bytes 1048592 | tf_op jit(solution)/shard_map/reduce_scatter | solution.py:280
  (286 shorter events, 440.4 us)
Async XLA Ops:
  7.2 153.6 %all-gather.7.cloned.1.call-start = ((), (), s32[]{:S(2)}) async-start(), calls=%async_computation.18 | async-start | bytes 17301504 | tf_op jit(solution)/shard_map/all_gather | solution.py:108
  7.9 213.2 %all-gather.11.cloned.1.call-start = ((), (), s32[]{:S(2)}) async-start(), calls=%async_computation.20 | async-start | bytes 10485760 | tf_op jit(solution)/shard_map/all_gather | solution.py:116
  8.7 262.1 %all-gather.9.cloned.1.call-start = ((), (), s32[]{:S(2)}) async-start(), calls=%async_computation.19 | async-start | bytes 5242880 | tf_op jit(solution)/shard_map/all_gather | solution.py:134
  52.8 130.6 %copy-start.29 = (f32[2048]{0:T(1024)}, f32[2048]{0:T(1024)S(1)}, u32[]{:S(2)}) copy-start(f32[2048]{0:T(1024)S(1)} %convert_element_type.154) | copy-start | bytes 24580
  53.0 130.5 %copy-start.34 = (f32[128]{0:T(128)}, f32[128]{0:T(128)S(1)}, u32[]{:S(2)}) copy-start(f32[128]{0:T(128)S(1)} %add_rsqrt_fusion.1) | copy-start | bytes 1540
  170.1 160.4 %all-gather.13.cloned.1.call-start = ((), (), s32[]{:S(2)}) async-start(), calls=%async_computation.21 | async-start | bytes 10485760 | tf_op jit(solution)/shard_map/all_gather | solution.py:117
  170.7 419.9 %all-gather.15.cloned.1.call-start = ((), (), s32[]{:S(2)}) async-start(), calls=%async_computation.22 | async-start | bytes 57671680 | tf_op jit(solution)/shard_map/all_gather | solution.py:118
  182.7 552.6 %all-gather.17.cloned.1.call-start = ((), (), s32[]{:S(2)}) async-start(), calls=%async_computation.23 | async-start | bytes 28835840 | tf_op jit(solution)/shard_map/all_gather | solution.py:119
  230.8 34.7 %all-to-all-start.1 = ((bf16[8,36,2048]{2,1,0:T(8,128)(2,1)}), bf16[8,36,2048]{2,1,0:T(8,128)(2,1)}, u32[]{:S(2)}, u32[]{:S(2)}) async-start(bf16[8,36,2048]{2,1,0:T(8,128)(2,1)} %reshape.287), calls=%async_computation.1 | async-start | bytes 2621440 | tf_op jit(solution)/shard_map/all_to_all | solution.py:23
  236.2 732.3 %copy-start.37 = (s32[1024]{0:T(1024)}, s32[1024]{0:T(1024)S(1)}, u32[]{:S(2)}) copy-start(s32[1024]{0:T(1024)S(1)} %pad_clamp_fusion.1) | copy-start | bytes 12292
  343.3 35.2 %all-to-all-start.3 = ((bf16[8,36,2048]{2,1,0:T(8,128)(2,1)}), bf16[8,36,2048]{2,1,0:T(8,128)(2,1)}, u32[]{:S(2)}, u32[]{:S(2)}) async-start(bf16[8,36,2048]{2,1,0:T(8,128)(2,1)} %reshape.292), calls=%async_computation.3 | async-start | bytes 2621440 | tf_op jit(solution)/shard_map/all_to_all | solution.py:23
  378.5 35.2 %all-to-all-start.6 = ((bf16[8,36,2048]{2,1,0:T(8,128)(2,1)}), bf16[8,36,2048]{2,1,0:T(8,128)(2,1)}, u32[]{:S(2)}, u32[]{:S(2)}) async-start(bf16[8,36,2048]{2,1,0:T(8,128)(2,1)} %reshape_reshape.14), calls=%async_computation.6 | async-start | bytes 2621440 | tf_op jit(solution)/shard_map/all_to_all | solution.py:19
  413.7 35.9 %all-to-all-start.4 = ((bf16[8,36,2048]{2,1,0:T(8,128)(2,1)}), bf16[8,36,2048]{2,1,0:T(8,128)(2,1)S(1)}, u32[]{:S(2)}, u32[]{:S(2)}) async-start(bf16[8,36,2048]{2,1,0:T(8,128)(2,1)} %reshape_reshape.13), calls=%async_computation.4 | async-start | bytes 2621440 | tf_op jit(solution)/shard_map/all_to_all | solution.py:19
  449.9 169.6 %copy-start.22 = (bf16[288,2048,1]{1,0,2:T(8,128)(2,1)}, bf16[288,2048,1]{1,0,2:T(8,128)(2,1)S(1)}, u32[]{:S(2)}) copy-start(bf16[288,2048,1]{1,0,2:T(8,128)(2,1)S(1)} %reshape.398) | copy-start | bytes 3538948
  619.5 115.8 %copy-start.28 = (bf16[288,2048]{1,0:T(8,128)(2,1)S(1)}, bf16[288,2048]{1,0:T(8,128)(2,1)}, u32[]{:S(2)}) copy-start(bf16[288,2048]{1,0:T(8,128)(2,1)} %reshape.302) | copy-start | bytes 3538948
  783.1 36.2 %all-to-all-start.7 = ((bf16[8,36,2048]{2,1,0:T(8,128)(2,1)}), bf16[8,36,2048]{2,1,0:T(8,128)(2,1)S(1)}, u32[]{:S(2)}, u32[]{:S(2)}) async-start(bf16[8,36,2048]{2,1,0:T(8,128)(2,1)} %reshape.303), calls=%async_computation.7 | async-start | bytes 2621440 | tf_op jit(solution)/shard_map/all_to_all | solution.py:23
  819.3 34.6 %all-to-all-start.5 = ((bf16[8,36,2048]{2,1,0:T(8,128)(2,1)}), bf16[8,36,2048]{2,1,0:T(8,128)(2,1)}, u32[]{:S(2)}, u32[]{:S(2)}) async-start(bf16[8,36,2048]{2,1,0:T(8,128)(2,1)} %reshape.297), calls=%async_computation.5 | async-start | bytes 2621440 | tf_op jit(solution)/shard_map/all_to_all | solution.py:23
  823.6 438.7 %reduce-scatter.9.cloned.1.call-start = ((), (), s32[]{:S(2)}) async-start(), calls=%async_computation.24 | async-start | bytes 10485760 | tf_op jit(solution)/shard_map/reduce_scatter | solution.py:273
  995.5 340.3 %reduce-scatter.15.cloned.1.call-start = ((), (), s32[]{:S(2)}) async-start(), calls=%async_computation.27 | async-start | bytes 10485760 | tf_op jit(solution)/shard_map/reduce_scatter | solution.py:294
  1004.6 392.1 %reduce-scatter.13.cloned.1.call-start = ((), (), s32[]{:S(2)}) async-start(), calls=%async_computation.26 | async-start | bytes 10485760 | tf_op jit(solution)/shard_map/reduce_scatter | solution.py:291
  1057.2 345.6 %reduce-scatter.17.cloned.1.call-start = ((), (), s32[]{:S(2)}) async-start(), calls=%async_computation.28 | async-start | bytes 28835840 | tf_op jit(solution)/shard_map/reduce_scatter | solution.py:300
  1075.8 625.7 %reduce-scatter.19.cloned.1.call-start = ((), (), s32[]{:S(2)}) async-start(), calls=%async_computation.29 | async-start | bytes 57671680
  1262.2 800.3 %reduce-scatter.11.cloned.1.call-start = ((), (), s32[]{:S(2)}) async-start(), calls=%async_computation.25 | async-start | bytes 34603008 | tf_op jit(solution)/shard_map/reduce_scatter | solution.py:280
  1289.0 34.2 %all-to-all-start.11 = ((bf16[8,36,2048]{2,1,0:T(8,128)(2,1)}), bf16[8,36,2048]{2,1,0:T(8,128)(2,1)}, u32[]{:S(2)}, u32[]{:S(2)}) async-start(bf16[8,36,2048]{2,1,0:T(8,128)(2,1)} %reshape.312), calls=%async_computation.11 | async-start | bytes 2621440 | tf_op jit(solution)/shard_map/all_to_all | solution.py:23
  (50 other events, 463.9 us)
Sparse Core Ops, SparseCore 0:
  10.9 149.9 all-gather.6
  162.4 56.4 all-gather.10
  221.0 34.4 all-gather.8
  256.9 58.2 all-gather.12
  317.2 273.3 all-gather.14
  592.0 143.1 all-gather.16
  995.6 70.2 reduce-scatter.8
  1068.5 71.3 reduce-scatter.14
  1142.5 71.2 reduce-scatter.12
  1216.8 163.8 reduce-scatter.16
  1383.3 318.1 reduce-scatter.18
  1704.3 358.2 reduce-scatter.10
where the time goes:
time: 2080 us; the launch traced here: 2070 us
  waiting for transfers between devices  1100 us (53%)
  local copies, waits for them, and re-layouts  336 us (16%)
  blocking collectives  256 us (12%)
  matrix products  252 us (12%)
  other arithmetic  76 us (4%)
  starting transfers between devices  34.5 us (2%)
    reduce_scatter x1, waiting for transfers between devices, local(): lax.psum_scatter(grad_kv, ('ep', 'ws'), scatter_dimension=1, tiled=True)  289 us
    unnamed x13, waiting for transfers between devices  287 us
    unnamed x129, local copies, waits for them, and re-layouts  261 us
    all_gather x1, waiting for transfers between devices, local(): lax.all_gather(w_in, 'ws', axis=3, tiled=True)  141 us
    all_to_all x4, blocking collectives, dispatch(): return lax.all_to_all(send, 'ep', split_axis=0, concat_axis=0, tiled=True)  139 us
    all_to_all x5, waiting for transfers between devices, combine(): return lax.all_to_all(back, 'ep', split_axis=0, concat_axis=0, tiled=True)  124 us
    all_gather x1, waiting for transfers between devices, local(): lax.all_gather(w_out, 'ws', axis=1, tiled=True)  109 us
    all_gather x1, waiting for transfers between devices, local(): lax.all_gather(key_value_weight, ('ep', 'ws'), axis=1, tiled=True)  108 us
  transfers between devices with their start and end apart: 19, of which 12 were waited for; matrix products, arithmetic and copies ran while one was open for 26% of the time, Pallas kernels for 0%

commit v1 on v0

v1 whole, which is shorter than its diff:
```python
import jax
import jax.numpy as jnp
from jax import lax
from jax.sharding import PartitionSpec as P

KEY_VALUE_HEADS = 16
HEAD_SIZE = 128
MIXTURE_EXPERTS = 8
CHOSEN_EXPERTS = 2
BLOCK = 256
CAP = 36
ROWS = 40

EPS = 1e-06
very_negative = -1e30
f32 = jnp.float32
bf16 = jnp.bfloat16


def dot(a, b):
    return jnp.dot(a, b, preferred_element_type=f32)


def dot_t(a, b):
    return lax.dot_general(a, b, (((1,), (1,)), ((), ())), preferred_element_type=f32)


def t_dot(a, b):
    return lax.dot_general(a, b, (((0,), (0,)), ((), ())), preferred_element_type=f32)


def exchange(send):
    return lax.all_to_all(send, "ep", split_axis=0, concat_axis=0, tiled=True)


def spread(rows, group):
    width = rows.shape[-1]
    blocks = rows.reshape(MIXTURE_EXPERTS, 1, ROWS, width)
    return jnp.broadcast_to(blocks, (MIXTURE_EXPERTS, group, ROWS, width)).reshape(
        MIXTURE_EXPERTS * group, ROWS, width
    )


def dispatch(rows, group):
    got = exchange(spread(rows, group))
    return lax.all_gather(got, "ws", axis=1, tiled=False)


def combine(partial, group, n_ep, n_ws):
    width = partial.shape[-1]
    part = partial.reshape(n_ep, n_ws, ROWS, width).transpose(1, 0, 2, 3)
    part = part.reshape(n_ws * n_ep * ROWS, width)
    own = lax.psum_scatter(part, "ws", scatter_dimension=0, tiled=True)
    own = own.reshape(n_ep, ROWS, width)
    back = exchange(own)
    if group == 1:
        return back.reshape(MIXTURE_EXPERTS * ROWS, width)
    total = jnp.sum(back.reshape(MIXTURE_EXPERTS, group, ROWS, width).astype(f32), 1)
    return total.astype(bf16).reshape(MIXTURE_EXPERTS * ROWS, width)


def slot_tables(routes, slots):
    target = jnp.where(slots < CAP, routes * ROWS + slots, -1)
    places = lax.broadcasted_iota(jnp.int32, (MIXTURE_EXPERTS * ROWS, target.shape[0]), 0)
    return [(places == target[None, :, k]).astype(bf16) for k in range(CHOSEN_EXPERTS)]


def norm_back(grad, unit, inverse, gain):
    gain_grad = jnp.sum(grad * unit, 0)
    scaled = grad * gain
    return (inverse * (scaled - unit * jnp.mean(scaled * unit, -1, keepdims=True)), gain_grad)


def heads_of(rows):
    return rows.reshape(rows.shape[0], -1, HEAD_SIZE)


def local(
    x_in,
    gain_attn,
    gain_ffn,
    key_value_weight,
    w_query,
    w_output,
    w_in,
    w_out,
    gate_attn,
    gate_ffn,
    route_attn,
    slot_attn,
    route_ffn,
    slot_ffn,
    cotangent,
):
    n_ep = lax.axis_size("ep")
    n_ws = lax.axis_size("ws")
    group = n_ep // MIXTURE_EXPERTS
    local_tokens, width = x_in.shape
    key_value_width = KEY_VALUE_HEADS * HEAD_SIZE
    part = w_query.shape[2]
    own_width = group * part
    sequence = n_ws * local_tokens
    place = lax.axis_index("ws")
    scale = HEAD_SIZE ** (-0.5)

    gain_one = lax.all_gather(gain_attn, ("ep", "ws"), axis=0, tiled=True).astype(f32)
    gain_two = lax.all_gather(gain_ffn, ("ep", "ws"), axis=0, tiled=True).astype(f32)
    plain = group == 1 and key_value_weight.shape[1] == HEAD_SIZE
    if plain:
        half = n_ep // 2
        there = [
            (e * n_ws + w, (w + n_ws * (e // half)) * n_ws + e % half)
            for e in range(n_ep)
            for w in range(n_ws)
        ]
        mine = lax.ppermute(key_value_weight, ("ep", "ws"), there)
        kv_own = lax.all_gather(mine, "ep", axis=1, tiled=True)
    else:
        whole = lax.all_gather(key_value_weight, ("ep", "ws"), axis=1, tiled=True)
        whole = whole.reshape(width, 2 * group, n_ws, part)
        kv_own = lax.dynamic_index_in_dim(whole, place, 2, keepdims=False).reshape(width, -1)

    inputs = x_in.astype(f32)
    inverse_one = lax.rsqrt(jnp.mean(inputs * inputs, -1, keepdims=True) + EPS)
    unit_one = inputs * inverse_one
    normed = (unit_one * gain_one).astype(bf16)
    attn_pairs = slot_tables(route_attn, slot_attn)
    ffn_pairs = slot_tables(route_ffn, slot_ffn)
    attn_tokens = attn_pairs[0] + attn_pairs[1]
    ffn_tokens = ffn_pairs[0] + ffn_pairs[1]

    normed_sequence = lax.all_gather(normed, "ws", axis=0, tiled=True)
    rows_one = dispatch(dot(attn_tokens, normed).astype(bf16), group).reshape(-1, width)
    kv = dot(normed_sequence, kv_own).astype(bf16)
    keys = kv[:, :own_width].reshape(sequence, -1, HEAD_SIZE)
    values = kv[:, own_width:].reshape(sequence, -1, HEAD_SIZE)

    owner_query = dot(rows_one, w_query[0]).astype(bf16)
    queries = exchange(owner_query.reshape(n_ep, n_ws * ROWS, part))
    queries = queries.reshape(MIXTURE_EXPERTS, group, n_ws, ROWS, part)

    def by_block(rows):
        rows = rows.reshape(MIXTURE_EXPERTS, group, n_ws, ROWS, part)
        return [
            rows[:, :, w].transpose(0, 2, 1, 3).reshape(-1, own_width // HEAD_SIZE, HEAD_SIZE)
            for w in range(n_ws)
        ]

    def to_experts(pieces):
        rows = jnp.stack(
            [
                piece.reshape(MIXTURE_EXPERTS, ROWS, group, part).transpose(0, 2, 1, 3)
                for piece in pieces
            ],
            2,
        )
        return rows.reshape(n_ep, n_ws * ROWS, part)

    spans = [(w * local_tokens // BLOCK + 1) * BLOCK for w in range(n_ws)]
    kept = []
    mixed_pieces = []
    for q, span in zip(by_block(queries), spans):
        scores = (
            jnp.einsum("rhd,shd->hrs", q, keys[:span], preferred_element_type=f32) * scale
        )
        probs = jax.nn.softmax(scores, axis=-1)
        mixed = jnp.einsum(
            "hrs,shd->rhd", probs.astype(bf16), values[:span], preferred_element_type=f32
        )
        kept.append((q, probs))
        mixed_pieces.append(mixed.astype(bf16))
    owner_mixed = exchange(to_experts(mixed_pieces)).reshape(-1, part)
    attn_slots = combine(dot(owner_mixed, w_output[0]).astype(bf16), group, n_ep, n_ws)

    def weighted(pairs, gates, slot_values):
        return sum(gates[:, k : k + 1] * t_dot(pairs[k], slot_values) for k in range(2))

    def to_slots(pairs, gates, values):
        return sum(
            dot(pairs[k], (gates[:, k : k + 1] * values).astype(bf16)) for k in range(2)
        ).astype(bf16)

    hidden_state = inputs + weighted(attn_pairs, gate_attn, attn_slots)
    inverse_two = lax.rsqrt(jnp.mean(hidden_state * hidden_state, -1, keepdims=True) + EPS)
    unit_two = hidden_state * inverse_two
    normed_two = (unit_two * gain_two).astype(bf16)

    grad_out = cotangent.astype(f32)
    expert_grad = dispatch(to_slots(ffn_pairs, gate_ffn, grad_out), group).reshape(-1, width)
    expert_rows = dispatch(dot(ffn_tokens, normed_two).astype(bf16), group).reshape(-1, width)
    gate_weight, up_weight = w_in[0, :, 0], w_in[0, :, 1]
    gate_pre = dot(expert_rows, gate_weight)
    up_pre = dot(expert_rows, up_weight)
    sigmoid_gate = jax.nn.sigmoid(gate_pre)
    silu_gate = gate_pre * sigmoid_gate
    activated = (silu_gate * up_pre).astype(bf16)
    grad_act = dot_t(expert_grad, w_out[0])
    grad_up = (grad_act * silu_gate).astype(bf16)
    grad_gate = (
        grad_act * up_pre * sigmoid_gate * (1.0 + gate_pre * (1.0 - sigmoid_gate))
    ).astype(bf16)
    back_two = (dot_t(grad_gate, gate_weight) + dot_t(grad_up, up_weight)).astype(bf16)
    back_slots = combine(back_two, group, n_ep, n_ws)
    ffn_slots = combine(dot(activated, w_out[0]).astype(bf16), group, n_ep, n_ws)
    result = hidden_state + weighted(ffn_pairs, gate_ffn, ffn_slots)
    grad_second = t_dot(activated, expert_grad)
    grad_first = jnp.stack([t_dot(expert_rows, grad_gate), t_dot(expert_rows, grad_up)], 1)

    grad_normed_two = t_dot(ffn_tokens, back_slots)
    grad_hidden_norm, grad_gain_two = norm_back(grad_normed_two, unit_two, inverse_two, gain_two)
    grad_hidden = grad_out + grad_hidden_norm
    owner_grad = dispatch(to_slots(attn_pairs, gate_attn, grad_hidden), group).reshape(-1, width)
    grad_output = t_dot(owner_mixed, owner_grad)
    back_mixed = dot_t(owner_grad, w_output[0]).astype(bf16)
    mixed_grads = exchange(back_mixed.reshape(n_ep, n_ws * ROWS, part))

    grad_keys, grad_values, query_pieces = 0.0, 0.0, []
    for (q, probs), grad, span in zip(kept, by_block(mixed_grads), spans):
        grad_probs = jnp.einsum("rhd,shd->hrs", grad, values[:span], preferred_element_type=f32)
        centred = jnp.sum(probs * grad_probs, -1, keepdims=True)
        grad_scores = (probs * (grad_probs - centred)).astype(bf16)
        grad_q = (
            jnp.einsum("hrs,shd->rhd", grad_scores, keys[:span], preferred_element_type=f32)
            * scale
        )
        query_pieces.append(grad_q.astype(bf16))
        pad = ((0, sequence - span), (0, 0), (0, 0))
        piece = jnp.einsum("hrs,rhd->shd", grad_scores, q, preferred_element_type=f32) * scale
        grad_keys = grad_keys + jnp.pad(piece, pad)
        piece = jnp.einsum(
            "hrs,rhd->shd", probs.astype(bf16), grad, preferred_element_type=f32
        )
        grad_values = grad_values + jnp.pad(piece, pad)
    grad_kv_rows = jnp.concatenate(
        [grad_keys.reshape(sequence, -1), grad_values.reshape(sequence, -1)], 1
    ).astype(bf16)
    owner_grad_query = exchange(to_experts(query_pieces)).reshape(-1, part)
    grad_query = t_dot(rows_one, owner_grad_query)
    back_normed = dot_t(owner_grad_query, w_query[0]).astype(bf16)
    normed_back = combine(back_normed, group, n_ep, n_ws)

    grad_kv = t_dot(normed_sequence, grad_kv_rows)
    if plain:
        pieces = grad_kv.reshape(width, n_ep, HEAD_SIZE).transpose(1, 0, 2).astype(bf16)
        piece = lax.psum_scatter(pieces, "ep", scatter_dimension=0, tiled=False)
        grad_kv_shard = lax.ppermute(piece, ("ep", "ws"), [(b, a) for a, b in there]).astype(f32)
    else:
        mask = (jnp.arange(n_ws) == place)[None, None, :, None]
        pieces = jnp.where(mask, grad_kv.reshape(width, 2 * group, 1, part), 0.0)
        pieces = pieces.reshape(width, 2 * key_value_width).astype(bf16)
        grad_kv_shard = lax.psum_scatter(
            pieces, ("ep", "ws"), scatter_dimension=1, tiled=True
        ).astype(f32)
    from_kv = lax.psum_scatter(
        dot_t(grad_kv_rows, kv_own).astype(bf16), "ws", scatter_dimension=0, tiled=True
    )
    grad_normed = t_dot(attn_tokens, normed_back) + from_kv.astype(f32)
    grad_input_norm, grad_gain_one = norm_back(grad_normed, unit_one, inverse_one, gain_one)
    grad_input = grad_hidden + grad_input_norm
    gain_shards = lax.psum_scatter(
        jnp.stack([grad_gain_one, grad_gain_two], 0), ("ep", "ws"), scatter_dimension=1, tiled=True
    )
    return (
        result.astype(bf16),
        grad_input,
        gain_shards[0],
        gain_shards[1],
        grad_kv_shard,
        grad_query[None],
        grad_output[None],
        grad_first[None],
        grad_second[None],
    )


def solution(mesh):
    both = ("ep", "ws")
    rows, vector, columns = P(both, None), P(both), P(None, both)
    return jax.shard_map(
        local,
        mesh=mesh,
        in_specs=(
            rows,
            vector,
            vector,
            columns,
            P("ep", None, "ws"),
            P("ep", "ws", None),
            P("ep", None, None, "ws"),
            P("ep", "ws", None),
            rows,
            rows,
            rows,
            rows,
            rows,
            rows,
            rows,
        ),
        out_specs=(
            rows,
            rows,
            vector,
            vector,
            columns,
            P("ep", None, "ws"),
            P("ep", "ws", None),
            P("ep", None, None, "ws"),
            P("ep", "ws", None),
        ),
        check_vma=False,
    )
```

time: 2080 us -> 1250 us (0.60)
  waiting for transfers between devices: 1100 us -> 482 us
  local copies, waits for them, and re-layouts: 336 us -> 115 us
  blocking collectives: 256 us -> 320 us
  other arithmetic: 76 us -> 34.5 us
    unnamed x129 -> x194, local copies, waits for them, and re-layouts: 261 us -> 50.6 us
    all_gather x6, waiting for transfers between devices: 357 us -> 150 us  [the longest x1 84.5 us: local(): kv_own = lax.all_gather(mine, 'ep', axis=1, tiled=True)]
    reduce_scatter x5 -> x6, waiting for transfers between devices: 289 us -> 113 us  [the longest x4 102 us: combine(): own = lax.psum_scatter(part, 'ws', scatter_dimension=0, tiled=True)]
    unnamed x13 -> x14, waiting for transfers between devices: 287 us -> 131 us
    all_to_all x5 -> x8, blocking collectives: 174 us -> 279 us  [exchange(): return lax.all_to_all(send, 'ep', split_axis=0, concat_axis=0, tiled=True)]
    all_to_all x7 -> x4, waiting for transfers between devices: 166 us -> 70.9 us  [exchange(): return lax.all_to_all(send, 'ep', split_axis=0, concat_axis=0, tiled=True)]
    unnamed x2 -> x1, blocking collectives: 82.4 us -> 40.9 us
    convert_element_type x7 -> x8, other arithmetic: 36.5 us -> 4.01 us  [the longest x4 1.74 us: local(): grad_scores = (probs * (grad_probs - centred)).astype(bf16)]
  transfers between devices with their start and end apart: 19 -> 19, of which waited for: 12 -> 12; matrix products, arithmetic and copies ran while one was open for 26% -> 21% of each run, Pallas kernels for 0% -> 0%
where the time goes in v1:
time: 1250 us; the launch traced here: 1230 us
  waiting for transfers between devices  482 us (39%)
  blocking collectives  320 us (26%)
  matrix products  236 us (19%)
  local copies, waits for them, and re-layouts  115 us (9%)
  other arithmetic  34.5 us (3%)
  starting transfers between devices  30.5 us (2%)
  between operations  15.4 us (1%)
    all_to_all x8, blocking collectives, exchange(): return lax.all_to_all(send, 'ep', split_axis=0, concat_axis=0, tiled=True)  279 us
    unnamed x14, waiting for transfers between devices  131 us
    reduce_scatter x4, waiting for transfers between devices, combine(): own = lax.psum_scatter(part, 'ws', scatter_dimension=0, tiled=True)  102 us
    all_gather x1, waiting for transfers between devices, local(): kv_own = lax.all_gather(mine, 'ep', axis=1, tiled=True)  84.5 us
    all_to_all x4, waiting for transfers between devices, exchange(): return lax.all_to_all(send, 'ep', split_axis=0, concat_axis=0, tiled=True)  70.9 us
    dot_general x6, matrix products, dot_t(): lax.dot_general(a, b, (((1,), (1,)), ((), ())), preferred_element_type=f32)  63.8 us
    dot_general x12, matrix products, t_dot(): lax.dot_general(a, b, (((0,), (0,)), ((), ())), preferred_element_type=f32)  63.2 us
    dot_general x12, matrix products, dot(): return jnp.dot(a, b, preferred_element_type=f32)  56.6 us
  transfers between devices with their start and end apart: 19, of which 12 were waited for; matrix products, arithmetic and copies ran while one was open for 21% of the time, Pallas kernels for 0%

profile of v1, /device:TPU:1, one launch (start us, length us, event | category | flops | bytes accessed | tf_op | source)
XLA Modules:
  0.0 1233.6 jit_solution(14797323896688899517)
XLA Ops:
  11.1 40.9 %all-reduce.6 = (bf16[2048]{0:T(1024)(128)(2,1)S(1)}, bf16[2048]{0:T(1024)(128)(2,1)}) all-reduce(bf16[2048]{0:T(1024)(128)(2,1)S(1)} %dynamic-update-slice, bf16[2048]{0:T(1024)(128)(2,1)S(1)} %dynamic-update-slice.1), channel_id=1, replica_groups=mesh['ep'=8,'ws'=4] {'ep','ws'}, use_global_device_ids=true, to_apply=%add.4 | all-reduce | flops 4096 | bytes 16384
  54.3 34.5 %all_to_all.60 = bf16[8,40,2048]{2,1,0:T(8,128)(2,1)} all-to-all(bf16[8,40,2048]{2,1,0:T(8,128)(2,1)S(1)} %bitcast.308), channel_id=1, replica_groups=mesh['ep'=8,'ws'=4] {'ep'}, dimensions={0} | all-to-all | bytes 2621440 | tf_op jit(solution)/shard_map/all_to_all | solution.py:33
  107.8 27.8 %all-gather.15.cloned.1.call-done = bf16[8,160,2048]{2,1,0:T(8,128)(2,1)} async-done(((bf16[8,40,2048]{2,1,0:T(8,128)(2,1)}), bf16[8,160,2048]{2,1,0:T(8,128)(2,1)}) %all-gather.15.cloned.1.call-update) | async-done | bytes 5242896 | tf_op jit(solution)/shard_map/all_gather | solution.py:46
  160.9 84.5 %all-gather.13.cloned.1.call-done = bf16[2048,1024]{1,0:T(8,128)(2,1)} async-done(((bf16[2048,128]{1,0:T(8,128)(2,1)}), bf16[2048,1024]{1,0:T(8,128)(2,1)}) %all-gather.13.cloned.1.call-update) | async-done | bytes 4194320 | tf_op jit(solution)/shard_map/all_gather | solution.py:117
  293.5 33.6 %all_to_all.61 = bf16[8,160,512]{2,1,0:T(8,128)(2,1)S(1)} all-to-all(bf16[8,160,512]{2,1,0:T(8,128)(2,1)S(1)} %bitcast.306), channel_id=1, replica_groups=mesh['ep'=8,'ws'=4] {'ep'}, dimensions={0} | all-to-all | bytes 2621440 | tf_op jit(solution)/shard_map/all_to_all | solution.py:33
  333.1 51.5 %reduce-scatter.10.cloned.1.call-done = bf16[320,2048]{1,0:T(8,128)(2,1)} async-done(((bf16[1280,2048]{1,0:T(8,128)(2,1)}), bf16[320,2048]{1,0:T(8,128)(2,1)}) %reduce-scatter.10.cloned.1.call-update) | async-done | bytes 1310736 | tf_op jit(solution)/shard_map/reduce_scatter | solution.py:53
  390.0 30.2 %all-to-all-done.3 = bf16[8,40,2048]{2,1,0:T(8,128)(2,1)S(1)} async-done(((bf16[8,40,2048]{2,1,0:T(8,128)(2,1)}), bf16[8,40,2048]{2,1,0:T(8,128)(2,1)S(1)}, u32[]{:S(2)}, u32[]{:S(2)}) %all-to-all-start.3) | async-done | bytes 1310752 | tf_op jit(solution)/shard_map/all_to_all | solution.py:33
  424.0 35.1 %all_to_all.62 = bf16[8,40,2048]{2,1,0:T(8,128)(2,1)} all-to-all(bf16[8,40,2048]{2,1,0:T(8,128)(2,1)S(1)} %bitcast.309), channel_id=1, replica_groups=mesh['ep'=8,'ws'=4] {'ep'}, dimensions={0} | all-to-all | bytes 2621440 | tf_op jit(solution)/shard_map/all_to_all | solution.py:33
  461.5 34.7 %all_to_all.63 = bf16[8,40,2048]{2,1,0:T(8,128)(2,1)} all-to-all(bf16[8,40,2048]{2,1,0:T(8,128)(2,1)S(1)} %bitcast.298), channel_id=1, replica_groups=mesh['ep'=8,'ws'=4] {'ep'}, dimensions={0} | all-to-all | bytes 2621440 | tf_op jit(solution)/shard_map/all_to_all | solution.py:33
  496.3 23.2 %fusion.209 = (bf16[1,2048,1,1408]{3,2,1,0:T(2,128)(2,1)}, bf16[1,2048,1,1408]{3,2,1,0:T(2,128)(2,1)}) fusion(bf16[1,2048,2,1408]{3,2,1,0:T(2,128)(2,1)} %param.21), kind=kLoop, calls=%fused_computation.268 | loop fusion | bytes 23068672 | tf_op jit(solution)/shard_map/slice | solution.py:191
  519.5 15.0 %fusion.22 = f32[1280,1408]{1,0:T(8,128)} fusion(bf16[1280,2048]{1,0:T(8,128)(2,1)} %bitcast.332, bf16[1,2048,1,1408]{3,2,1,0:T(2,128)(2,1)} %get-tuple-element.54), kind=kOutput, calls=%fused_computation.54 | convolution fusion | flops 7381975040 | bytes 18219008 | tf_op jit(solution)/shard_map/dot_general | solution.py:21
  544.8 19.9 %multiply_convert_fusion = (bf16[1280,1408]{1,0:T(8,128)(2,1)}, bf16[1280,1408]{1,0:T(8,128)(2,1)}, bf16[1280,1408]{1,0:T(8,128)(2,1)}) fusion(f32[1280,1408]{1,0:T(8,128)} %fusion.22, f32[1280,1408]{1,0:T(8,128)} %fusion.23, bf16[1280,2048]{1,0:T(8,128)(2,1)} %bitcast.330, bf16[1,1408,2048]{2,1,0:T(8,128)(2,1)} %param.22), kind=kOutput, calls=%fused_computation.12 | convolution fusion | flops 7409008640 | bytes 36241408 | tf_op jit(solution)/shard_map/dot_general | solution.py:25
  564.7 15.0 %fusion.21 = f32[1280,2048]{1,0:T(8,128)} fusion(bf16[1280,1408]{1,0:T(8,128)(2,1)} %get-tuple-element.52, bf16[1,2048,1,1408]{3,2,1,0:T(2,128)(2,1)} %get-tuple-element.54), kind=kOutput, calls=%fused_computation.53 | convolution fusion | flops 7381975040 | bytes 19857408 | tf_op jit(solution)/shard_map/dot_general | solution.py:25
  579.7 14.5 %add_convert_fusion = bf16[1280,2048]{1,0:T(8,128)(2,1)S(1)} fusion(f32[1280,2048]{1,0:T(8,128)} %fusion.21, bf16[1280,1408]{1,0:T(8,128)(2,1)S(1)} %copy-done.86, bf16[1,2048,1,1408]{3,2,1,0:T(2,128)(2,1)} %get-tuple-element.55), kind=kOutput, calls=%fused_computation.5 | convolution fusion | flops 7387217920 | bytes 25100288 | tf_op jit(solution)/shard_map/dot_general | solution.py:25
  597.1 50.5 %reduce-scatter.14.cloned.1.call-done = bf16[320,2048]{1,0:T(8,128)(2,1)} async-done(((bf16[1280,2048]{1,0:T(8,128)(2,1)}), bf16[320,2048]{1,0:T(8,128)(2,1)}) %reduce-scatter.14.cloned.1.call-update) | async-done | bytes 1310736 | tf_op jit(solution)/shard_map/reduce_scatter | solution.py:53
  647.6 36.1 %all_to_all.64 = bf16[8,40,2048]{2,1,0:T(8,128)(2,1)S(1)} all-to-all(bf16[8,40,2048]{2,1,0:T(8,128)(2,1)} %bitcast.319), channel_id=1, replica_groups=mesh['ep'=8,'ws'=4] {'ep'}, dimensions={0} | all-to-all | bytes 2621440 | tf_op jit(solution)/shard_map/all_to_all | solution.py:33
  686.3 34.6 %all_to_all.65 = bf16[8,40,2048]{2,1,0:T(8,128)(2,1)} all-to-all(bf16[8,40,2048]{2,1,0:T(8,128)(2,1)S(1)} %bitcast.310), channel_id=1, replica_groups=mesh['ep'=8,'ws'=4] {'ep'}, dimensions={0} | all-to-all | bytes 2621440 | tf_op jit(solution)/shard_map/all_to_all | solution.py:33
  735.3 25.8 %all-gather.21.cloned.1.call-done = bf16[8,160,2048]{2,1,0:T(8,128)(2,1)} async-done(((bf16[8,40,2048]{2,1,0:T(8,128)(2,1)}), bf16[8,160,2048]{2,1,0:T(8,128)(2,1)}) %all-gather.21.cloned.1.call-update) | async-done | bytes 5242896 | tf_op jit(solution)/shard_map/all_gather | solution.py:46
  766.5 36.1 %all_to_all.66 = bf16[8,160,512]{2,1,0:T(8,128)(2,1)S(1)} all-to-all(bf16[8,160,512]{2,1,0:T(8,128)(2,1)S(1)} %bitcast.320), channel_id=1, replica_groups=mesh['ep'=8,'ws'=4] {'ep'}, dimensions={0} | all-to-all | bytes 2621440 | tf_op jit(solution)/shard_map/all_to_all | solution.py:33
  824.8 34.7 %all_to_all.67 = bf16[8,160,512]{2,1,0:T(8,128)(2,1)S(1)} all-to-all(bf16[8,160,512]{2,1,0:T(8,128)(2,1)S(1)} %bitcast.307), channel_id=1, replica_groups=mesh['ep'=8,'ws'=4] {'ep'}, dimensions={0} | all-to-all | bytes 2621440 | tf_op jit(solution)/shard_map/all_to_all | solution.py:33
  951.5 40.6 %all-to-all-done.5 = bf16[8,40,2048]{2,1,0:T(8,128)(2,1)S(1)} async-done(((bf16[8,40,2048]{2,1,0:T(8,128)(2,1)}), bf16[8,40,2048]{2,1,0:T(8,128)(2,1)S(1)}, u32[]{:S(2)}, u32[]{:S(2)}) %all-to-all-start.5) | async-done | bytes 1310752 | tf_op jit(solution)/shard_map/all_to_all | solution.py:33
  996.5 16.5 %maximum_bitcast_fusion = f32[1,2048,2,1408]{3,1,2,0:T(8,128)} fusion(f32[2048,1,1408]{2,0,1:T(8,128)} %convolution_bitcast_fusion.1, f32[2048,1,1408]{2,0,1:T(8,128)} %convolution_bitcast_fusion.2), kind=kLoop, calls=%fused_computation.4 | loop fusion | flops 5767168 | bytes 46137344 | tf_op jit(solution)/shard_map/broadcast_in_dim | solution.py:271
  1013.0 38.7 %copy.189 = f32[1,2048,2,1408]{3,2,1,0:T(2,128)} copy(f32[1,2048,2,1408]{3,1,2,0:T(8,128)} %maximum_bitcast_fusion) | data formatting | bytes 46137344
  1094.7 130.0 %reduce-scatter.22.cloned.1.call-done = f32[64,2]{1,0:T(8,128)} async-done(((f32[2048,2]{1,0:T(8,128)}), f32[64,2]{1,0:T(8,128)}) %reduce-scatter.22.cloned.1.call-update) | async-done | bytes 528
  (348 shorter events, 314.1 us)
Async XLA Ops:
  7.2 319.9 %copy-start = (bf16[1,512,2048]{2,1,0:T(8,128)(2,1)S(1)}, bf16[1,512,2048]{2,1,0:T(8,128)(2,1)}, u32[]{:S(2)}) copy-start(bf16[1,512,2048]{2,1,0:T(8,128)(2,1)} %param.20) | copy-start | bytes 6291460
  7.2 128.4 %all-gather.15.cloned.1.call-start = ((), (), s32[]{:S(2)}) async-start(), calls=%async_computation.27 | async-start | bytes 6553600 | tf_op jit(solution)/shard_map/all_gather | solution.py:46
  9.3 675.8 %copy-start.59 = (s32[128]{0:T(128)}, s32[128]{0:T(128)S(1)}, u32[]{:S(2)}) copy-start(s32[128]{0:T(128)S(1)} %get-tuple-element.76) | copy-start | bytes 1540
  9.3 676.4 %copy-start.63 = (s32[128]{0:T(128)}, s32[128]{0:T(128)S(1)}, u32[]{:S(2)}) copy-start(s32[128]{0:T(128)S(1)} %get-tuple-element.77) | copy-start | bytes 1540
  88.9 72.0 %all-gather.11.cloned.1.call-start = ((), (), s32[]{:S(2)}) async-start(), calls=%async_computation.19 | async-start | bytes 2621440 | tf_op jit(solution)/shard_map/all_gather | solution.py:132
  89.6 155.8 %all-gather.13.cloned.1.call-start = ((), (), s32[]{:S(2)}) async-start(), calls=%async_computation.20 | async-start | bytes 4718592 | tf_op jit(solution)/shard_map/all_gather | solution.py:117
  89.7 17.3 %collective-permute-start = (bf16[2048,128]{1,0:T(8,128)(2,1)S(1)}, bf16[2048,128]{1,0:T(8,128)(2,1)S(1)}, u32[]{:S(2)}, u32[]{:S(2)}) collective-permute-start(bf16[2048,128]{1,0:T(8,128)(2,1)S(1)} %copy-done.83), channel_id=1, source_target_pairs={{0,0},{1,4},{2,8},{3,12},{4,1},{5,5},{6,9},{7,13},{8,2},{9,6},{10,... | collective-permute-start | bytes 1572872 | tf_op jit(solution)/shard_map/ppermute | solution.py:116
  142.7 109.8 %all-to-all-start.1 = ((bf16[8,160,512]{2,1,0:T(8,128)(2,1)}), bf16[8,160,512]{2,1,0:T(8,128)(2,1)S(1)}, u32[]{:S(2)}, u32[]{:S(2)}) async-start(bf16[8,160,512]{2,1,0:T(8,128)(2,1)} %bitcast.318), calls=%async_computation.1 | async-start | bytes 2621440 | tf_op jit(solution)/shard_map/all_to_all | solution.py:33
  148.5 236.1 %reduce-scatter.10.cloned.1.call-start = ((), (), s32[]{:S(2)}) async-start(), calls=%async_computation.21 | async-start | bytes 6553600 | tf_op jit(solution)/shard_map/reduce_scatter | solution.py:53
  384.6 35.6 %all-to-all-start.3 = ((bf16[8,40,2048]{2,1,0:T(8,128)(2,1)}), bf16[8,40,2048]{2,1,0:T(8,128)(2,1)S(1)}, u32[]{:S(2)}, u32[]{:S(2)}) async-start(bf16[8,40,2048]{2,1,0:T(8,128)(2,1)} %bitcast.317), calls=%async_computation.4 | async-start | bytes 2621440 | tf_op jit(solution)/shard_map/all_to_all | solution.py:33
  389.8 129.6 %all-gather.17.cloned.1.call-start = ((), (), s32[]{:S(2)}) async-start(), calls=%async_computation.28 | async-start | bytes 6553600 | tf_op jit(solution)/shard_map/all_gather | solution.py:46
  390.0 293.7 %copy-start.57 = (s32[128]{0:T(128)}, s32[128]{0:T(128)S(1)}, u32[]{:S(2)}) copy-start(s32[128]{0:T(128)S(1)} %get-tuple-element.73) | copy-start | bytes 1540
  390.0 293.6 %copy-start.61 = (s32[128]{0:T(128)}, s32[128]{0:T(128)S(1)}, u32[]{:S(2)}) copy-start(s32[128]{0:T(128)S(1)} %get-tuple-element.72) | copy-start | bytes 1540
  459.1 85.7 %all-gather.19.cloned.1.call-start = ((), (), s32[]{:S(2)}) async-start(), calls=%async_computation.29 | async-start | bytes 6553600 | tf_op jit(solution)/shard_map/all_gather | solution.py:46
  496.2 151.3 %reduce-scatter.14.cloned.1.call-start = ((), (), s32[]{:S(2)}) async-start(), calls=%async_computation.23 | async-start | bytes 6553600 | tf_op jit(solution)/shard_map/reduce_scatter | solution.py:53
  597.0 164.1 %all-gather.21.cloned.1.call-start = ((), (), s32[]{:S(2)}) async-start(), calls=%async_computation.30 | async-start | bytes 6553600 | tf_op jit(solution)/shard_map/all_gather | solution.py:46
  721.0 205.9 %reduce-scatter.12.cloned.1.call-start = ((), (), s32[]{:S(2)}) async-start(), calls=%async_computation.22 | async-start | bytes 6553600 | tf_op jit(solution)/shard_map/reduce_scatter | solution.py:53
  735.3 256.8 %reduce-scatter.16.cloned.1.call-start = ((), (), s32[]{:S(2)}) async-start(), calls=%async_computation.24 | async-start | bytes 6553600 | tf_op jit(solution)/shard_map/reduce_scatter | solution.py:53
  865.4 193.2 %reduce-scatter.20.cloned.1.call-start = ((), (), s32[]{:S(2)}) async-start(), calls=%async_computation.26 | async-start | bytes 4718592 | tf_op jit(solution)/shard_map/reduce_scatter | solution.py:245
  926.9 65.2 %all-to-all-start.5 = ((bf16[8,40,2048]{2,1,0:T(8,128)(2,1)}), bf16[8,40,2048]{2,1,0:T(8,128)(2,1)S(1)}, u32[]{:S(2)}, u32[]{:S(2)}) async-start(bf16[8,40,2048]{2,1,0:T(8,128)(2,1)} %bitcast.313), calls=%async_computation.7 | async-start | bytes 2621440 | tf_op jit(solution)/shard_map/all_to_all | solution.py:33
  931.9 155.2 %reduce-scatter.18.cloned.1.call-start = ((), (), s32[]{:S(2)}) async-start(), calls=%async_computation.25 | async-start | bytes 2621440 | tf_op jit(solution)/shard_map/reduce_scatter | solution.py:254
  992.1 95.0 %all-to-all-start.11 = ((bf16[8,40,2048]{2,1,0:T(8,128)(2,1)}), bf16[8,40,2048]{2,1,0:T(8,128)(2,1)}, u32[]{:S(2)}, u32[]{:S(2)}) async-start(bf16[8,40,2048]{2,1,0:T(8,128)(2,1)} %bitcast.314), calls=%async_computation.15 | async-start | bytes 2621440 | tf_op jit(solution)/shard_map/all_to_all | solution.py:33
  996.4 228.3 %reduce-scatter.22.cloned.1.call-start = ((), (), s32[]{:S(2)}) async-start(), calls=%async_computation.31 | async-start | bytes 1081344
  1058.7 16.5 %collective-permute-start.1 = (bf16[2048,128]{1,0:T(8,128)(2,1)}, bf16[2048,128]{1,0:T(8,128)(2,1)S(1)}, u32[]{:S(2)}, u32[]{:S(2)}) collective-permute-start(bf16[2048,128]{1,0:T(8,128)(2,1)} %bitcast.338), channel_id=1, source_target_pairs={{0,0},{4,1},{8,2},{12,3},{1,4},{5,5},{9,6},{13,7},{2,8},{6,9},{10,... | collective-permute-start | bytes 1572872 | tf_op jit(solution)/shard_map/ppermute | solution.py:246
  (87 other events, 1595.6 us)
Sparse Core Ops, SparseCore 0:
  89.0 46.5 all-gather.14
  137.7 23.0 all-gather.10
  163.5 81.8 all-gather.12
  333.2 51.4 reduce-scatter.9
  459.2 40.1 all-gather.16
  500.9 40.3 all-gather.18
  597.1 50.3 reduce-scatter.13
  721.1 39.9 all-gather.20
  764.2 50.7 reduce-scatter.11
  865.6 50.4 reduce-scatter.15
  920.2 127.9 reduce-scatter.19
  1050.7 36.3 reduce-scatter.17
  1091.8 132.8 reduce-scatter.21

commit v2 on v1

--- a/solution.py
+++ b/solution.py
@@ -1,6 +1,10 @@
+import functools
+
 import jax
 import jax.numpy as jnp
 from jax import lax
+from jax.experimental import pallas as pl
+from jax.experimental.pallas import tpu as pltpu
 from jax.sharding import PartitionSpec as P
 
 KEY_VALUE_HEADS = 16
@@ -15,6 +19,10 @@
 very_negative = -1e30
 f32 = jnp.float32
 bf16 = jnp.bfloat16
+MESH = pl.DeviceIdType.MESH
+ANY = pl.BlockSpec(memory_space=pl.ANY)
+VM = pl.BlockSpec(memory_space=pltpu.VMEM)
+DMA = pltpu.SemaphoreType.DMA
 
 
 def dot(a, b):
@@ -29,7 +37,303 @@
     return lax.dot_general(a, b, (((0,), (0,)), ((), ())), preferred_element_type=f32)
 
 
+def flip(index, bits):
+    out, bit = index, 1
+    while bit <= bits:
+        if bits & bit:
+            out = out + bit - 2 * bit * ((index // bit) % 2)
+        bit *= 2
+    return out
+
+
+def far_first(n):
+    return sorted(range(1, n), key=lambda k: (-((k // 2).bit_length()), k))
+
+
+def greet(partners):
+    barrier = pltpu.get_barrier_semaphore()
+    for partner in partners:
+        pl.semaphore_signal(barrier, inc=1, device_id=partner, device_id_type=MESH)
+    pl.semaphore_wait(barrier, len(partners))
+
+
+def remote(src, dst, send, recv, device):
+    return pltpu.make_async_remote_copy(
+        src_ref=src, dst_ref=dst, send_sem=send, recv_sem=recv, device_id=device, device_id_type=MESH
+    )
+
+
+def dispatch_kernel(n, rows, out, own, load_sem, ep_s, ep_r, y_s, y_r, c_s, c_r, x_s, x_r):
+    e, w = lax.axis_index("ep"), lax.axis_index("ws")
+    twin, other = flip(w, 1), flip(w, 2)
+    hops = range(1, n)
+    sources = [e] + [flip(e, k) for k in hops]
+    greet([(s, w) for s in sources[1:]] + [(e, twin), (e, other)])
+    first = []
+    for i, s in enumerate(sources[1:]):
+        first.append(remote(rows.at[s], out.at[e, w], ep_s.at[i], ep_r.at[i], (s, w)))
+        first[-1].start()
+    load = pltpu.make_async_copy(rows.at[e], own, load_sem.at[0])
+    load.start()
+    over_y, to_twin, relayed = [], [], []
+
+    def relay(j):
+        over_y[j].wait_recv()
+        block = out.at[sources[j], other]
+        relayed.append(remote(block, block, x_s.at[j], x_r.at[j], (e, twin)))
+        relayed[-1].start()
+
+    for j, s in enumerate(sources):
+        place = out.at[s, w]
+        block = rows.at[e] if j == 0 else place
+        if j:
+            first[j - 1].wait_recv()
+        over_y.append(remote(block, place, y_s.at[j], y_r.at[j], (e, other)))
+        over_y[-1].start()
+        to_twin.append(remote(block, place, c_s.at[j], c_r.at[j], (e, twin)))
+        to_twin[-1].start()
+        if j == 0:
+            load.wait()
+            store = pltpu.make_async_copy(own, out.at[e, w], load_sem.at[1])
+            store.start()
+        else:
+            relay(j - 1)
+    relay(n - 1)
+    store.wait()
+    for copy in first + over_y:
+        copy.wait_send()
+    for copy in to_twin + relayed:
+        copy.wait()
+
+
+def dispatch_call(rows, n_ws):
+    n, count, width = rows.shape
+    return pl.pallas_call(
+        functools.partial(dispatch_kernel, n),
+        out_shape=jax.ShapeDtypeStruct((n, n_ws, count, width), rows.dtype),
+        in_specs=[ANY],
+        out_specs=ANY,
+        scratch_shapes=[
+            pltpu.VMEM((count, width), rows.dtype),
+            DMA((2,)),
+            DMA((n - 1,)),
+            DMA((n - 1,)),
+        ]
+        + [DMA((n,)) for _ in range(6)],
+        compiler_params=pltpu.CompilerParams(collective_id=0, has_side_effects=True),
+        name="dispatch",
+    )(rows)
+
+
+def combine_kernel(
+    n, part, out, mine, core, sum_y, from_y, total, load_sem, c_s, c_r, y_s, y_r, ep_s, ep_r, own_sem
+):
+    e, w = lax.axis_index("ep"), lax.axis_index("ws")
+    twin, other, last = flip(w, 1), flip(w, 2), flip(w, 3)
+    hops = far_first(n)
+    targets = [flip(e, k) for k in hops] + [e]
+    greet([(s, w) for s in targets[:-1]] + [(e, twin), (e, other)])
+    loads, cores = {}, {}
+    for half, near, far in ((1, other, last), (0, w, twin)):
+        for j, s in enumerate(targets):
+            cores[half, j] = remote(
+                part.at[s, far], core.at[half, j], c_s.at[half, j], c_r.at[half, j], (e, twin)
+            )
+            cores[half, j].start()
+            loads[half, j] = pltpu.make_async_copy(
+                part.at[s, near], mine.at[half, j], load_sem.at[half, j]
+            )
+            loads[half, j].start()
+    over_y, back = [], []
+
+    def send_y(j):
+        over_y.append(remote(sum_y.at[j], from_y.at[j], y_s.at[j], y_r.at[j], (e, other)))
+        over_y[-1].start()
+
+    def send_back(j):
+        back.append(remote(total.at[j], out.at[e], ep_s.at[j], ep_r.at[j], (targets[j], w)))
+        back[-1].start()
+
+    for j in range(n):
+        loads[1, j].wait()
+        cores[1, j].wait_recv()
+        sum_y[j] = (mine[1, j].astype(f32) + core[1, j].astype(f32)).astype(bf16)
+        if j:
+            send_y(j - 1)
+    loads[0, 0].wait()
+    cores[0, 0].wait_recv()
+    send_y(n - 1)
+    for j in range(n):
+        if j:
+            loads[0, j].wait()
+            cores[0, j].wait_recv()
+        over_y[j].wait_recv()
+        total[j] = (
+            mine[0, j].astype(f32) + core[0, j].astype(f32) + from_y[j].astype(f32)
+        ).astype(bf16)
+        if j:
+            send_back(j - 1)
+    for copy in over_y + list(cores.values()):
+        copy.wait_send()
+    keep = pltpu.make_async_copy(total.at[n - 1], out.at[e], own_sem)
+    keep.start()
+    for copy in back:
+        copy.wait()
+    keep.wait()
+
+
+def combine_call(part):
+    n, n_ws, count, width = part.shape
+    block = (n, count, width)
+    return pl.pallas_call(
+        functools.partial(combine_kernel, n),
+        out_shape=jax.ShapeDtypeStruct(block, part.dtype),
+        in_specs=[ANY],
+        out_specs=ANY,
+        scratch_shapes=[
+            pltpu.VMEM((2,) + block, part.dtype),
+            pltpu.VMEM((2,) + block, part.dtype),
+            pltpu.VMEM(block, part.dtype),
+            pltpu.VMEM(block, part.dtype),
+            pltpu.VMEM(block, part.dtype),
+            DMA((2, n)),
+            DMA((2, n)),
+            DMA((2, n)),
+            DMA((n,)),
+            DMA((n,)),
+            DMA((n - 1,)),
+            DMA((n - 1,)),
+            DMA,
+        ],
+        compiler_params=pltpu.CompilerParams(collective_id=1, has_side_effects=True),
+        name="combine",
+    )(part)
+
+
+def exchange_kernel(n, rows, out, own, load_sem, ep_s, ep_r):
+    e, w = lax.axis_index("ep"), lax.axis_index("ws")
+    targets = [flip(e, k) for k in far_first(n)]
+    greet([(s, w) for s in targets])
+    copies = []
+    for i, s in enumerate(targets):
+        copies.append(remote(rows.at[s], out.at[e], ep_s.at[i], ep_r.at[i], (s, w)))
+        copies[-1].start()
+    load = pltpu.make_async_copy(rows.at[e], own, load_sem.at[0])
+    load.start()
+    load.wait()
+    store = pltpu.make_async_copy(own, out.at[e], load_sem.at[1])
+    store.start()
+    store.wait()
+    for copy in copies:
+        copy.wait()
+
+
+def exchange_call(rows):
+    n = rows.shape[0]
+    return pl.pallas_call(
+        functools.partial(exchange_kernel, n),
+        out_shape=jax.ShapeDtypeStruct(rows.shape, rows.dtype),
+        in_specs=[ANY],
+        out_specs=ANY,
+        scratch_shapes=[
+            pltpu.VMEM(rows.shape[1:], rows.dtype),
+            DMA((2,)),
+            DMA((n - 1,)),
+            DMA((n - 1,)),
+        ],
+        compiler_params=pltpu.CompilerParams(collective_id=2, has_side_effects=True),
+        name="exchange",
+    )(rows)
+
+
+def gather_kernel(n, n_ws, own, out, load_sem, w_s, w_r, ep_s, ep_r):
+    e, w = lax.axis_index("ep"), lax.axis_index("ws")
+    beside = [flip(w, k) for k in range(1, n_ws)]
+    across = [flip(e, k) for k in far_first(n)]
+    greet([(e, p) for p in beside] + [(s, w) for s in across])
+    keep = pltpu.make_async_copy(own, out.at[e, w], load_sem)
+    keep.start()
+    first = []
+    for i, p in enumerate(beside):
+        first.append(remote(own, out.at[e, w], w_s.at[i], w_r.at[i], (e, p)))
+        first[-1].start()
+    keep.wait()
+    for copy in first:
+        copy.wait()
+    second = []
+    for i, s in enumerate(across):
+        second.append(remote(out.at[e], out.at[e], ep_s.at[i], ep_r.at[i], (s, w)))
+        second[-1].start()
+    for copy in second:
+        copy.wait()
+
+
+def gather_call(own, n, n_ws):
+    return pl.pallas_call(
+        functools.partial(gather_kernel, n, n_ws),
+        out_shape=jax.ShapeDtypeStruct((n, n_ws) + own.shape, own.dtype),
+        in_specs=[VM],
+        out_specs=VM,
+        scratch_shapes=[DMA, DMA((n_ws - 1,)), DMA((n_ws - 1,)), DMA((n - 1,)), DMA((n - 1,))],
+        compiler_params=pltpu.CompilerParams(collective_id=3, has_side_effects=True),
+        name="gather_gains",
+    )(own)
+
+
+def reduce_kernel(n, n_ws, parts, out, held, all_parts, load_sem, w_s, w_r, ep_s, ep_r):
+    e, w = lax.axis_index("ep"), lax.axis_index("ws")
+    beside = [flip(w, k) for k in range(1, n_ws)]
+    across = [flip(e, k) for k in far_first(n)]
+    greet([(e, p) for p in beside] + [(s, w) for s in across])
+    keep = pltpu.make_async_copy(parts.at[:, w], held.at[:, w], load_sem.at[0])
+    keep.start()
+    first = []
+    for i, p in enumerate(beside):
+        first.append(remote(parts.at[:, p], held.at[:, w], w_s.at[i], w_r.at[i], (e, p)))
+        first[-1].start()
+    keep.wait()
+    for copy in first:
+        copy.wait()
+    keep = pltpu.make_async_copy(held.at[e], all_parts.at[e], load_sem.at[1])
+    keep.start()
+    second = []
+    for i, s in enumerate(across):
+        second.append(remote(held.at[s], all_parts.at[e], ep_s.at[i], ep_r.at[i], (s, w)))
+        second[-1].start()
+    keep.wait()
+    for copy in second:
+        copy.wait()
+    out[...] = jnp.sum(jnp.sum(all_parts[...], 0), 0)
+
+
+def reduce_call(parts):
+    n, n_ws = parts.shape[:2]
+    return pl.pallas_call(
+        functools.partial(reduce_kernel, n, n_ws),
+        out_shape=jax.ShapeDtypeStruct(parts.shape[2:], parts.dtype),
+        in_specs=[VM],
+        out_specs=VM,
+        scratch_shapes=[
+            pltpu.VMEM(parts.shape, parts.dtype),
+            pltpu.VMEM(parts.shape, parts.dtype),
+            DMA((2,)),
+            DMA((n_ws - 1,)),
+            DMA((n_ws - 1,)),
+            DMA((n - 1,)),
+            DMA((n - 1,)),
+        ],
+        compiler_params=pltpu.CompilerParams(collective_id=4, has_side_effects=True),
+        name="reduce_gains",
+    )(parts)
+
+
+def small(n_ep):
+    return n_ep == MIXTURE_EXPERTS and lax.axis_size("ws") == 4
+
+
 def exchange(send):
+    if small(send.shape[0]):
+        return exchange_call(send)
     return lax.all_to_all(send, "ep", split_axis=0, concat_axis=0, tiled=True)
 
 
@@ -42,12 +346,17 @@
 
 
 def dispatch(rows, group):
+    if small(group * MIXTURE_EXPERTS):
+        return dispatch_call(rows.reshape(MIXTURE_EXPERTS, ROWS, -1), lax.axis_size("ws"))
     got = exchange(spread(rows, group))
     return lax.all_gather(got, "ws", axis=1, tiled=False)
 
 
 def combine(partial, group, n_ep, n_ws):
     width = partial.shape[-1]
+    if small(n_ep):
+        back = combine_call(partial.reshape(n_ep, n_ws, ROWS, width))
+        return back.reshape(MIXTURE_EXPERTS * ROWS, width)
     part = partial.reshape(n_ep, n_ws, ROWS, width).transpose(1, 0, 2, 3)
     part = part.reshape(n_ws * n_ep * ROWS, width)
     own = lax.psum_scatter(part, "ws", scatter_dimension=0, tiled=True)
@@ -103,8 +412,14 @@
     place = lax.axis_index("ws")
     scale = HEAD_SIZE ** (-0.5)
 
-    gain_one = lax.all_gather(gain_attn, ("ep", "ws"), axis=0, tiled=True).astype(f32)
-    gain_two = lax.all_gather(gain_ffn, ("ep", "ws"), axis=0, tiled=True).astype(f32)
+    short = small(n_ep) and gain_attn.shape[0] == 64
+    if short:
+        gains = jnp.concatenate([gain_attn, gain_ffn], 0).astype(f32)[None]
+        gains = gather_call(gains, n_ep, n_ws).reshape(n_ep * n_ws, 2, -1)
+        gain_one, gain_two = gains[:, 0].reshape(-1), gains[:, 1].reshape(-1)
+    else:
+        gain_one = lax.all_gather(gain_attn, ("ep", "ws"), axis=0, tiled=True).astype(f32)
+        gain_two = lax.all_gather(gain_ffn, ("ep", "ws"), axis=0, tiled=True).astype(f32)
     plain = group == 1 and key_value_weight.shape[1] == HEAD_SIZE
     if plain:
         half = n_ep // 2
@@ -257,9 +572,14 @@
     grad_normed = t_dot(attn_tokens, normed_back) + from_kv.astype(f32)
     grad_input_norm, grad_gain_one = norm_back(grad_normed, unit_one, inverse_one, gain_one)
     grad_input = grad_hidden + grad_input_norm
-    gain_shards = lax.psum_scatter(
-        jnp.stack([grad_gain_one, grad_gain_two], 0), ("ep", "ws"), scatter_dimension=1, tiled=True
-    )
+    gain_grads = jnp.stack([grad_gain_one, grad_gain_two], 0)
+    if short:
+        parts = gain_grads.reshape(2, n_ep, n_ws, -1).transpose(1, 2, 0, 3)
+        gain_shards = reduce_call(parts.reshape(n_ep, n_ws, 1, -1)).reshape(2, -1)
+    else:
+        gain_shards = lax.psum_scatter(
+            gain_grads, ("ep", "ws"), scatter_dimension=1, tiled=True
+        )
     return (
         result.astype(bf16),
         grad_input,

time: 1250 us -> 961 us (0.77)
  Pallas kernels: 0 us -> 537 us
  waiting for transfers between devices: 482 us -> 22.4 us
  blocking collectives: 320 us -> 0 us
  starting transfers between devices: 30.5 us -> 7.87 us
  local copies, waits for them, and re-layouts: 115 us -> 101 us
    pallas_call x0 -> x14, Pallas kernels: none -> 537 us  [the longest x4 199 us: combine_call(): pl.pallas_call(functools.partial(combine_kernel, n), out_shape=jax.ShapeD...]
    all_to_all x8 -> x0, blocking collectives: 279 us -> none  [exchange(): return lax.all_to_all(send, 'ep', split_axis=0, concat_axis=0, tiled=True)]
    unnamed x14 -> x4, waiting for transfers between devices: 131 us -> 0.07 us
    reduce_scatter x4 -> x0, waiting for transfers between devices: 102 us -> none  [combine(): own = lax.psum_scatter(part, 'ws', scatter_dimension=0, tiled=True)]
    all_gather x1, waiting for transfers between devices: 84.5 us -> 0.02 us  [local(): kv_own = lax.all_gather(mine, 'ep', axis=1, tiled=True)]
    all_to_all x4 -> x0, waiting for transfers between devices: 70.9 us -> none  [exchange(): return lax.all_to_all(send, 'ep', split_axis=0, concat_axis=0, tiled=True)]
    all_gather x4 -> x0, waiting for transfers between devices: 53.6 us -> none  [dispatch(): return lax.all_gather(got, 'ws', axis=1, tiled=False)]
    unnamed x1 -> x0, blocking collectives: 40.9 us -> none
  transfers between devices with their start and end apart: 19 -> 6, of which waited for: 12 -> 2; matrix products, arithmetic and copies ran while one was open for 21% -> 18% of each run, Pallas kernels for 0% -> 27%
where the time goes in v2:
time: 961 us; the launch traced here: 953 us
  Pallas kernels  537 us (56%)
  matrix products  241 us (25%)
  local copies, waits for them, and re-layouts  101 us (11%)
  other arithmetic  29.2 us (3%)
  waiting for transfers between devices  22.4 us (2%)
  between operations  15.3 us (2%)
    pallas_call x4, Pallas kernels, combine_call(): pl.pallas_call(functools.partial(combine_kernel, n), out_shape=jax.ShapeD...  199 us
    pallas_call x4, Pallas kernels, dispatch_call(): pl.pallas_call(functools.partial(dispatch_kernel, n), out_shape=jax.Shape...  191 us
    pallas_call x4, Pallas kernels, exchange_call(): pl.pallas_call(functools.partial(exchange_kernel, n), out_shape=jax.Shape...  125 us
    dot_general x12, matrix products, dot(): return jnp.dot(a, b, preferred_element_type=f32)  68 us
    dot_general x6, matrix products, dot_t(): lax.dot_general(a, b, (((1,), (1,)), ((), ())), preferred_element_type=f32)  63.9 us
    dot_general x12, matrix products, t_dot(): lax.dot_general(a, b, (((0,), (0,)), ((), ())), preferred_element_type=f32)  60.8 us
    unnamed x173, local copies, waits for them, and re-layouts  48.9 us
    slice x1, local copies, waits for them, and re-layouts, local(): gate_weight, up_weight = (w_in[0, :, 0], w_in[0, :, 1])  23.4 us
  transfers between devices with their start and end apart: 6, of which 2 were waited for; matrix products, arithmetic and copies ran while one was open for 18% of the time, Pallas kernels for 27%

profile of v2, /device:TPU:1, one launch (start us, length us, event | category | flops | bytes accessed | tf_op | source)
XLA Modules:
  0.0 953.4 jit_solution(12910342975493749056)
XLA Ops:
  9.9 11.4 %gather_gains.1 = f32[8,4,1,128]{3,2,1,0:T(1,128)} custom-call(f32[1,128]{1,0:T(1,128)} %maximum_convert_fusion.own), custom_call_target="tpu_custom_call" | custom-call | tf_op jit(solution)/shard_map/gather_gains/pallas_call | solution.py:272
  30.8 12.4 %collective-permute-done = bf16[2048,128]{1,0:T(8,128)(2,1)S(1)} collective-permute-done((bf16[2048,128]{1,0:T(8,128)(2,1)}, bf16[2048,128]{1,0:T(8,128)(2,1)S(1)}, u32[]{:S(2)}, u32[]{:S(2)}) %collective-permute-start) | collective-permute-done | bytes 524320 | tf_op jit(solution)/shard_map/ppermute | solution.py:431
  46.4 42.2 %dispatch.6 = bf16[8,4,40,2048]{3,2,1,0:T(8,128)(2,1)} custom-call(bf16[8,40,2048]{2,1,0:T(8,128)(2,1)} %bitcast.314), custom_call_target="tpu_custom_call" | custom-call | tf_op jit(solution)/shard_map/dispatch/pallas_call | solution.py:111
  90.2 68.5 %dispatch.4 = bf16[8,4,40,2048]{3,2,1,0:T(8,128)(2,1)} custom-call(bf16[8,40,2048]{2,1,0:T(8,128)(2,1)} %bitcast.319), custom_call_target="tpu_custom_call" | custom-call | tf_op jit(solution)/shard_map/dispatch/pallas_call | solution.py:111
  165.9 37.7 %exchange.4 = bf16[8,160,512]{2,1,0:T(8,128)(2,1)} custom-call(bf16[8,160,512]{2,1,0:T(8,128)(2,1)} %bitcast.325), custom_call_target="tpu_custom_call" | custom-call | tf_op jit(solution)/shard_map/exchange/pallas_call | solution.py:233
  209.0 23.4 %fusion.209 = (bf16[1,2048,1,1408]{3,2,1,0:T(2,128)(2,1)}, bf16[1,2048,1,1408]{3,2,1,0:T(2,128)(2,1)}) fusion(bf16[1,2048,2,1408]{3,2,1,0:T(2,128)(2,1)} %param.21), kind=kLoop, calls=%fused_computation.281 | loop fusion | bytes 23068672 | tf_op jit(solution)/shard_map/slice | solution.py:506
  278.7 31.2 %exchange.5 = bf16[8,160,512]{2,1,0:T(8,128)(2,1)} custom-call(bf16[8,160,512]{2,1,0:T(8,128)(2,1)} %bitcast.315), custom_call_target="tpu_custom_call" | custom-call | tf_op jit(solution)/shard_map/exchange/pallas_call | solution.py:233
  316.4 52.7 %combine.4 = bf16[8,40,2048]{2,1,0:T(8,128)(2,1)} custom-call(bf16[8,4,40,2048]{3,2,1,0:T(8,128)(2,1)} %bitcast.309), custom_call_target="tpu_custom_call" | custom-call | tf_op jit(solution)/shard_map/combine/pallas_call | solution.py:188
  373.4 39.8 %dispatch.5 = bf16[8,4,40,2048]{3,2,1,0:T(8,128)(2,1)} custom-call(bf16[8,40,2048]{2,1,0:T(8,128)(2,1)} %bitcast.320), custom_call_target="tpu_custom_call" | custom-call | tf_op jit(solution)/shard_map/dispatch/pallas_call | solution.py:111
  413.2 15.0 %fusion.22 = f32[1280,1408]{1,0:T(8,128)} fusion(bf16[1280,2048]{1,0:T(8,128)(2,1)} %bitcast.304, bf16[1,2048,1,1408]{3,2,1,0:T(2,128)(2,1)} %get-tuple-element.36), kind=kOutput, calls=%fused_computation.54 | convolution fusion | flops 7381975040 | bytes 18219008 | tf_op jit(solution)/shard_map/dot_general | solution.py:29
  428.2 13.5 %fusion.23 = f32[1280,1408]{1,0:T(8,128)} fusion(bf16[1280,2048]{1,0:T(8,128)(2,1)S(1)} %bitcast.307, bf16[1,2048,1,1408]{3,2,1,0:T(2,128)(2,1)} %get-tuple-element.37), kind=kOutput, calls=%fused_computation.55 | convolution fusion | flops 7381975040 | bytes 18219008 | tf_op jit(solution)/shard_map/dot_general | solution.py:29
  441.7 19.9 %multiply_convert_fusion = (bf16[1280,1408]{1,0:T(8,128)(2,1)}, bf16[1280,1408]{1,0:T(8,128)(2,1)}, bf16[1280,1408]{1,0:T(8,128)(2,1)}) fusion(f32[1280,1408]{1,0:T(8,128)} %fusion.22, f32[1280,1408]{1,0:T(8,128)} %fusion.23, bf16[1280,2048]{1,0:T(8,128)(2,1)} %bitcast.296, bf16[1,1408,2048]{2,1,0:T(8,128)(2,1)} %param.22), kind=kOutput, calls=%fused_computation.12 | convolution fusion | flops 7409008640 | bytes 36241408 | tf_op jit(solution)/shard_map/dot_general | solution.py:33
  461.5 12.7 %fusion.21 = f32[1280,2048]{1,0:T(8,128)S(1)} fusion(bf16[1280,1408]{1,0:T(8,128)(2,1)} %get-tuple-element.34, bf16[1,2048,1,1408]{3,2,1,0:T(2,128)(2,1)} %get-tuple-element.36), kind=kOutput, calls=%fused_computation.53 | convolution fusion | flops 7381975040 | bytes 19857408 | tf_op jit(solution)/shard_map/dot_general | solution.py:33
  474.2 14.4 %add_convert_fusion = bf16[1280,2048]{1,0:T(8,128)(2,1)} fusion(f32[1280,2048]{1,0:T(8,128)S(1)} %fusion.21, bf16[1280,1408]{1,0:T(8,128)(2,1)} %get-tuple-element.33, bf16[1,2048,1,1408]{3,2,1,0:T(2,128)(2,1)} %get-tuple-element.37), kind=kOutput, calls=%fused_computation.5 | convolution fusion | flops 7387217920 | bytes 25100288 | tf_op jit(solution)/shard_map/dot_general | solution.py:33
  488.6 44.0 %combine.6 = bf16[8,40,2048]{2,1,0:T(8,128)(2,1)} custom-call(bf16[8,4,40,2048]{3,2,1,0:T(8,128)(2,1)} %bitcast.308), custom_call_target="tpu_custom_call" | custom-call | tf_op jit(solution)/shard_map/combine/pallas_call | solution.py:188
  537.3 40.4 %dispatch.7 = bf16[8,4,40,2048]{3,2,1,0:T(8,128)(2,1)} custom-call(bf16[8,40,2048]{2,1,0:T(8,128)(2,1)} %bitcast.321), custom_call_target="tpu_custom_call" | custom-call | tf_op jit(solution)/shard_map/dispatch/pallas_call | solution.py:111
  584.2 25.4 %exchange.6 = bf16[8,160,512]{2,1,0:T(8,128)(2,1)} custom-call(bf16[8,160,512]{2,1,0:T(8,128)(2,1)} %bitcast.326), custom_call_target="tpu_custom_call" | custom-call | tf_op jit(solution)/shard_map/exchange/pallas_call | solution.py:233
  648.1 31.2 %exchange.7 = bf16[8,160,512]{2,1,0:T(8,128)(2,1)} custom-call(bf16[8,160,512]{2,1,0:T(8,128)(2,1)} %bitcast.316), custom_call_target="tpu_custom_call" | custom-call | tf_op jit(solution)/shard_map/exchange/pallas_call | solution.py:233
  702.6 58.2 %combine.7 = bf16[8,40,2048]{2,1,0:T(8,128)(2,1)} custom-call(bf16[8,4,40,2048]{3,2,1,0:T(8,128)(2,1)} %bitcast.310), custom_call_target="tpu_custom_call" | custom-call | tf_op jit(solution)/shard_map/combine/pallas_call | solution.py:188
  760.8 13.2 %convolution_convert_fusion.2 = bf16[1280,2048]{1,0:T(8,128)(2,1)} fusion(bf16[1280,1408]{1,0:T(8,128)(2,1)} %get-tuple-element.35, bf16[1,1408,2048]{2,1,0:T(8,128)(2,1)} %param.22), kind=kOutput, calls=%fused_computation.11 | convolution fusion | flops 7384596480 | bytes 14614528 | tf_op jit(solution)/shard_map/dot_general | solution.py:29
  774.0 44.2 %combine.5 = bf16[8,40,2048]{2,1,0:T(8,128)(2,1)} custom-call(bf16[8,4,40,2048]{3,2,1,0:T(8,128)(2,1)} %bitcast.311), custom_call_target="tpu_custom_call" | custom-call | tf_op jit(solution)/shard_map/combine/pallas_call | solution.py:188
  818.1 14.0 %convolution_bitcast_fusion.1 = f32[2048,1,1408]{2,0,1:T(8,128)} fusion(bf16[1280,2048]{1,0:T(8,128)(2,1)} %bitcast.305, bf16[1280,1408]{1,0:T(8,128)(2,1)} %get-tuple-element.33), kind=kOutput, calls=%fused_computation.7 | convolution fusion | flops 7381975040 | bytes 20381696 | tf_op jit(solution)/shard_map/dot_general | solution.py:37
  832.1 12.2 %convolution_bitcast_fusion.2 = f32[2048,1,1408]{2,0,1:T(8,128)S(1)} fusion(bf16[1280,2048]{1,0:T(8,128)(2,1)} %bitcast.306, bf16[1280,1408]{1,0:T(8,128)(2,1)} %get-tuple-element.34), kind=kOutput, calls=%fused_computation.8 | convolution fusion | flops 7381975040 | bytes 20381696 | tf_op jit(solution)/shard_map/dot_general | solution.py:37
  853.2 38.8 %copy.95 = f32[1,2048,2,1408]{3,2,1,0:T(2,128)} copy(f32[1,2048,2,1408]{3,1,2,0:T(8,128)} %maximum_bitcast_fusion) | data formatting | bytes 46137344
  (300 shorter events, 222.0 us)
Async XLA Ops:
  7.2 302.7 %copy-start = (bf16[1,512,2048]{2,1,0:T(8,128)(2,1)S(1)}, bf16[1,512,2048]{2,1,0:T(8,128)(2,1)}, u32[]{:S(2)}) copy-start(bf16[1,512,2048]{2,1,0:T(8,128)(2,1)} %param.20) | copy-start | bytes 6291460
  7.2 225.3 %all-gather.3.cloned.1.call-start = ((), (), s32[]{:S(2)}) async-start(), calls=%async_computation.2 | async-start | bytes 2621440 | tf_op jit(solution)/shard_map/all_gather | solution.py:447
  25.6 206.9 %all-gather.5.cloned.1.call-start = ((), (), s32[]{:S(2)}) async-start(), calls=%async_computation.3 | async-start | bytes 4718592 | tf_op jit(solution)/shard_map/all_gather | solution.py:432
  25.7 17.5 %collective-permute-start = (bf16[2048,128]{1,0:T(8,128)(2,1)}, bf16[2048,128]{1,0:T(8,128)(2,1)S(1)}, u32[]{:S(2)}, u32[]{:S(2)}) collective-permute-start(bf16[2048,128]{1,0:T(8,128)(2,1)} %param.18), channel_id=1, source_target_pairs={{0,0},{1,4},{2,8},{3,12},{4,1},{5,5},{6,9},{7,13},{8,2},{9,6},{10,... | collective-permute-start | bytes 1572872 | tf_op jit(solution)/shard_map/ppermute | solution.py:431
  30.7 501.9 %copy-start.51 = (s32[128]{0:T(128)}, s32[128]{0:T(128)S(1)}, u32[]{:S(2)}) copy-start(s32[128]{0:T(128)S(1)} %get-tuple-element.53) | copy-start | bytes 1540
  30.7 501.9 %copy-start.53 = (s32[128]{0:T(128)}, s32[128]{0:T(128)S(1)}, u32[]{:S(2)}) copy-start(s32[128]{0:T(128)S(1)} %get-tuple-element.52) | copy-start | bytes 1540
  43.9 870.5 %reduce-scatter.3.cloned.1.call-start = ((), (), s32[]{:S(2)}) async-start(), calls=%async_computation.4 | async-start | bytes 2621440 | tf_op jit(solution)/shard_map/reduce_scatter | solution.py:569
  46.3 42.2 %copy-start.71 = (s32[128,2]{0,1:T(2,128)S(1)}, s32[128,2]{0,1:T(2,128)}, u32[]{:S(2)}) copy-start(s32[128,2]{0,1:T(2,128)} %param.26) | copy-start | bytes 3076
  46.3 42.2 %copy-start.72 = (s32[128,2]{0,1:T(2,128)S(1)}, s32[128,2]{0,1:T(2,128)}, u32[]{:S(2)}) copy-start(s32[128,2]{0,1:T(2,128)} %param.25) | copy-start | bytes 3076
  46.4 42.3 %copy-start.17 = (bf16[128,2048]{1,0:T(8,128)(2,1)S(1)}, bf16[128,2048]{1,0:T(8,128)(2,1)}, u32[]{:S(2)}) copy-start(bf16[128,2048]{1,0:T(8,128)(2,1)} %fusion.60) | copy-start | bytes 1572868
  88.6 70.1 %copy-start.55 = (s32[128]{0:T(128)}, s32[128]{0:T(128)S(1)}, u32[]{:S(2)}) copy-start(s32[128]{0:T(128)S(1)} %get-tuple-element.56) | copy-start | bytes 1540
  88.6 70.1 %copy-start.58 = (s32[128]{0:T(128)}, s32[128]{0:T(128)S(1)}, u32[]{:S(2)}) copy-start(s32[128]{0:T(128)S(1)} %get-tuple-element.57) | copy-start | bytes 1540
  207.5 49.6 %copy-start.22 = (bf16[320,4,128]{2,1,0:T(4,128)(2,1)}, bf16[320,4,128]{2,1,0:T(4,128)(2,1)S(1)}, u32[]{:S(2)}) copy-start(bf16[320,4,128]{2,1,0:T(4,128)(2,1)S(1)} %reshape_transpose_squeeze.26) | copy-start | bytes 983044
  208.5 46.7 %copy-start.24 = (bf16[320,4,128]{2,1,0:T(4,128)(2,1)}, bf16[320,4,128]{2,1,0:T(4,128)(2,1)S(1)}, u32[]{:S(2)}) copy-start(bf16[320,4,128]{2,1,0:T(4,128)(2,1)S(1)} %reshape_transpose_squeeze.27) | copy-start | bytes 983044
  316.3 52.7 %copy-start.56 = (s32[128]{0:T(128)S(1)}, s32[128]{0:T(128)}, u32[]{:S(2)}) copy-start(s32[128]{0:T(128)} %copy-done.55) | copy-start | bytes 1540
  316.3 52.7 %copy-start.69 = (f32[128]{0:T(128)S(1)}, f32[128]{0:T(128)}, u32[]{:S(2)}) copy-start(f32[128]{0:T(128)} %get-tuple-element.55) | copy-start | bytes 1540
  316.3 54.7 %copy-start.59 = (s32[128]{0:T(128)S(1)}, s32[128]{0:T(128)}, u32[]{:S(2)}) copy-start(s32[128]{0:T(128)} %copy-done.58) | copy-start | bytes 1540
  316.3 54.7 %copy-start.70 = (f32[128]{0:T(128)S(1)}, f32[128]{0:T(128)}, u32[]{:S(2)}) copy-start(f32[128]{0:T(128)} %get-tuple-element.54) | copy-start | bytes 1540
  371.7 163.0 %copy-start.2 = (f32[128,2048]{1,0:T(8,128)}, f32[128,2048]{1,0:T(8,128)S(1)}, u32[]{:S(2)}) copy-start(f32[128,2048]{1,0:T(8,128)S(1)} %get-tuple-element.69) | copy-start | bytes 3145732
  685.1 244.1 %reduce-scatter.5.cloned.1.call-start = ((), (), s32[]{:S(2)}) async-start(), calls=%async_computation.5 | async-start | bytes 4718592 | tf_op jit(solution)/shard_map/reduce_scatter | solution.py:560
  844.3 50.2 %slice-start = ((s8[5242880]{0:T(1024)(128)(4,1)}), s8[4194304]{0:T(1024)(128)(4,1)S(1)}, s32[]{:S(2)}) async-start(s8[5242880]{0:T(1024)(128)(4,1)} %bitcast.286), calls=%async_computation.6 | async-start | bytes 8388608
  853.2 39.4 %copy-start.66 = (f32[128]{0:T(128)S(1)}, f32[128]{0:T(128)}, u32[]{:S(2)}) copy-start(f32[128]{0:T(128)} %copy-done.65) | copy-start | bytes 1540
  853.2 41.3 %slice-start.1 = ((s8[5242880]{0:T(1024)(128)(4,1)}), s8[1048576]{0:T(1024)(128)(4,1)S(1)}, s32[]{:S(2)}) async-start(s8[5242880]{0:T(1024)(128)(4,1)} %bitcast.286), calls=%async_computation.7 | async-start | bytes 2097152
  929.3 16.3 %collective-permute-start.1 = (bf16[2048,128]{1,0:T(8,128)(2,1)}, bf16[2048,128]{1,0:T(8,128)(2,1)S(1)}, u32[]{:S(2)}, u32[]{:S(2)}) collective-permute-start(bf16[2048,128]{1,0:T(8,128)(2,1)} %bitcast.329), channel_id=1, source_target_pairs={{0,0},{4,1},{8,2},{12,3},{1,4},{5,5},{9,6},{13,7},{2,8},{6,9},{10,... | collective-permute-start | bytes 1572872 | tf_op jit(solution)/shard_map/ppermute | solution.py:561
  (66 other events, 642.8 us)
Sparse Core Ops, SparseCore 0:
  25.7 31.3 all-gather.2
  59.7 107.5 all-gather.4
  685.2 40.6 reduce-scatter.2
  832.2 86.0 reduce-scatter.4

commit v3 on v1

--- a/solution.py
+++ b/solution.py
@@ -1,6 +1,10 @@
+import functools
+
 import jax
 import jax.numpy as jnp
 from jax import lax
+from jax.experimental import pallas as pl
+from jax.experimental.pallas import tpu as pltpu
 from jax.sharding import PartitionSpec as P
 
 KEY_VALUE_HEADS = 16
@@ -15,6 +19,12 @@
 very_negative = -1e30
 f32 = jnp.float32
 bf16 = jnp.bfloat16
+MESH = pl.DeviceIdType.MESH
+ANY = pl.BlockSpec(memory_space=pl.ANY)
+VM = pl.BlockSpec(memory_space=pltpu.VMEM)
+DMA = pltpu.SemaphoreType.DMA
+STEP = 256
+VMEM_LIMIT = 60 << 20
 
 
 def dot(a, b):
@@ -29,8 +39,609 @@
     return lax.dot_general(a, b, (((0,), (0,)), ((), ())), preferred_element_type=f32)
 
 
-def exchange(send):
+def flip(index, bits):
+    out, bit = index, 1
+    while bit <= bits:
+        if bits & bit:
+            out = out + bit - 2 * bit * ((index // bit) % 2)
+        bit *= 2
+    return out
+
+
+def far_first(n):
+    return sorted(range(1, n), key=lambda k: (-((k // 2).bit_length()), k))
+
+
+def greet(partners):
+    barrier = pltpu.get_barrier_semaphore()
+    for partner in partners:
+        pl.semaphore_signal(barrier, inc=1, device_id=partner, device_id_type=MESH)
+    pl.semaphore_wait(barrier, len(partners))
+
+
+def remote(src, dst, send, recv, device):
+    return pltpu.make_async_remote_copy(
+        src_ref=src, dst_ref=dst, send_sem=send, recv_sem=recv, device_id=device, device_id_type=MESH
+    )
+
+
+class Job:
+    def __init__(self, args, outs, scratch, steps, body):
+        self.args, self.outs, self.scratch, self.steps, self.body = args, outs, scratch, steps, body
+
+
+def run_jobs(exchange_job, fills, collective_id, name):
+    jobs = [exchange_job] + fills
+    args = [a for job in jobs for a in job.args]
+    outs = [o for job in jobs for o in job.outs]
+    scratch = [x for job in jobs for x in job.scratch]
+
+    def kernel(*refs):
+        bodies, at = [], [0, len(args), len(args) + len(outs)]
+        for job in jobs:
+            own = []
+            for k, part in enumerate((job.args, job.outs, job.scratch)):
+                own.append(refs[at[k] : at[k] + len(part)])
+                at[k] += len(part)
+            bodies.append(job.body(*own[0], *own[1], *own[2]))
+        work = [bodies[k + 1] for k in range(len(fills))]
+        queue = [g for g, job in zip(work, fills) for _ in range(job.steps)]
+        for g in work:
+            next(g)
+        done = 0
+        for k, _ in enumerate(bodies[0]):
+            target = (k + 1) * len(queue) // exchange_job.steps
+            while done < target:
+                next(queue[done])
+                done += 1
+        for g in work:
+            for _ in g:
+                pass
+
+    return pl.pallas_call(
+        kernel,
+        out_shape=outs,
+        in_specs=[ANY] * len(args),
+        out_specs=[ANY] * len(outs),
+        scratch_shapes=scratch,
+        compiler_params=pltpu.CompilerParams(
+            collective_id=collective_id, has_side_effects=True, vmem_limit_bytes=VMEM_LIMIT
+        ),
+        name=name,
+    )(*args)
+
+
+def fetch(pairs, sem):
+    copies = [
+        pltpu.make_async_copy(src, dst, sem.at[i]) for i, (src, dst) in enumerate(pairs)
+    ]
+    for copy in copies:
+        copy.start()
+    return copies
+
+
+def blocks_of(size):
+    return [(start, min(STEP, size - start)) for start in range(0, size, STEP)]
+
+
+def column_tiles(width, tile):
+    def body(c, carry):
+        tile(pl.multiple_of(c * STEP, STEP), STEP)
+        return carry
+
+    lax.fori_loop(0, width // STEP, body, 0)
+    if width % STEP:
+        tile(width // STEP * STEP, width % STEP)
+
+
+def grad_job(a, b):
+    depth, rows = a.shape
+    width = b.shape[1]
+
+    def body(a_hbm, b_hbm, out, a_ref, b_ref, turned, held, load_sem, sem):
+        loads = fetch(((a_hbm, a_ref), (b_hbm, b_ref)), load_sem)
+        yield
+        for load in loads:
+            load.wait()
+        copies = []
+        for i, (start, size) in enumerate(blocks_of(rows)):
+            if i >= 2:
+                copies[i - 2].wait()
+            turned[:size] = a_ref[:, start : start + size].T
+
+            def tile(at, columns, slot=i % 2, size=size):
+                held[slot, :size, pl.ds(at, columns)] = jnp.dot(
+                    turned[:size], b_ref[:, pl.ds(at, columns)], preferred_element_type=f32
+                )
+
+            column_tiles(width, tile)
+            copies.append(
+                pltpu.make_async_copy(
+                    held.at[i % 2, pl.ds(0, size)], out.at[pl.ds(start, size)], sem.at[i % 2]
+                )
+            )
+            copies[i].start()
+            yield
+        for copy in copies[-2:]:
+            copy.wait()
+
+    return Job(
+        [a, b],
+        [jax.ShapeDtypeStruct((rows, width), f32)],
+        [
+            pltpu.VMEM(a.shape, bf16),
+            pltpu.VMEM(b.shape, bf16),
+            pltpu.VMEM((STEP, depth), bf16),
+            pltpu.VMEM((2, STEP, width), f32),
+            DMA((2,)),
+            DMA((2,)),
+        ],
+        len(blocks_of(rows)),
+        body,
+    )
+
+
+def pair_grad_job(a, first, second):
+    depth, rows = a.shape
+    tiles = first.shape[1] // 128
+
+    def body(a_hbm, f_hbm, s_hbm, out, a_ref, f_ref, s_ref, turned, held, load_sem, sem):
+        loads = fetch(((a_hbm, a_ref), (f_hbm, f_ref), (s_hbm, s_ref)), load_sem)
+        flat = held.reshape(2 * tiles * STEP * 2, 128)
+        yield
+        for load in loads:
+            load.wait()
+        copies = []
+        for i, (start, size) in enumerate(blocks_of(rows)):
+            if i >= 2:
+                for copy in copies[i - 2]:
+                    copy.wait()
+            turned[:size] = a_ref[:, start : start + size].T
+
+            def tile(at, columns, slot=i % 2, size=size):
+                for j, b_ref in enumerate((f_ref, s_ref)):
+                    r = jnp.dot(
+                        turned[:size], b_ref[:, pl.ds(at, columns)], preferred_element_type=f32
+                    )
+                    for half in range(columns // 128):
+                        base = (slot * tiles + at // 128 + half) * (2 * STEP) + j
+                        flat[pl.ds(base, size, stride=2), :] = r[:, half * 128 : half * 128 + 128]
+
+            column_tiles(tiles * 128, tile)
+            copies.append(
+                [
+                    pltpu.make_async_copy(
+                        held.at[i % 2, c, pl.ds(0, size)],
+                        out.at[pl.ds(start, size), :, pl.ds(c * 128, 128)],
+                        sem.at[i % 2, c],
+                    )
+                    for c in range(tiles)
+                ]
+            )
+            for copy in copies[i]:
+                copy.start()
+            yield
+        for copy in copies[-2] + copies[-1]:
+            copy.wait()
+
+    return Job(
+        [a, first, second],
+        [jax.ShapeDtypeStruct((rows, 2, tiles * 128), f32)],
+        [
+            pltpu.VMEM(a.shape, bf16),
+            pltpu.VMEM(first.shape, bf16),
+            pltpu.VMEM(second.shape, bf16),
+            pltpu.VMEM((STEP, depth), bf16),
+            pltpu.VMEM((2, tiles, STEP, 2, 128), f32),
+            DMA((3,)),
+            DMA((2, tiles)),
+        ],
+        len(blocks_of(rows)),
+        body,
+    )
+
+
+def product_job(a, b, dtype):
+    rows, width = a.shape[0], b.shape[1]
+
+    def body(a_hbm, b_hbm, out, a_ref, b_ref, held, load_sem, sem):
+        loads = fetch(((a_hbm, a_ref), (b_hbm, b_ref)), load_sem)
+        yield
+        for load in loads:
+            load.wait()
+        copies = []
+        for i, (start, size) in enumerate(blocks_of(rows)):
+            if i >= 2:
+                copies[i - 2].wait()
+
+            def tile(at, columns, slot=i % 2, start=start, size=size):
+                held[slot, :size, pl.ds(at, columns)] = jnp.dot(
+                    a_ref[start : start + size],
+                    b_ref[:, pl.ds(at, columns)],
+                    preferred_element_type=f32,
+                ).astype(dtype)
+
+            column_tiles(width, tile)
+            copies.append(
+                pltpu.make_async_copy(
+                    held.at[i % 2, pl.ds(0, size)], out.at[pl.ds(start, size)], sem.at[i % 2]
+                )
+            )
+            copies[i].start()
+            yield
+        for copy in copies[-2:]:
+            copy.wait()
+
+    return Job(
+        [a, b],
+        [jax.ShapeDtypeStruct((rows, width), dtype)],
+        [
+            pltpu.VMEM(a.shape, bf16),
+            pltpu.VMEM(b.shape, bf16),
+            pltpu.VMEM((2, STEP, width), dtype),
+            DMA((2,)),
+            DMA((2,)),
+        ],
+        len(blocks_of(rows)),
+        body,
+    )
+
+
+def dispatch_job(rows, n_ws):
+    n, count, width = rows.shape
+
+    def body(rows, out, own, load_sem, ep_s, ep_r, y_s, y_r, c_s, c_r, x_s, x_r):
+        e, w = lax.axis_index("ep"), lax.axis_index("ws")
+        twin, other = flip(w, 1), flip(w, 2)
+        sources = [e] + [flip(e, k) for k in range(1, n)]
+        greet([(s, w) for s in sources[1:]] + [(e, twin), (e, other)])
+        first = []
+        for i, s in enumerate(sources[1:]):
+            first.append(remote(rows.at[s], out.at[e, w], ep_s.at[i], ep_r.at[i], (s, w)))
+            first[-1].start()
+        load = pltpu.make_async_copy(rows.at[e], own, load_sem.at[0])
+        load.start()
+        over_y, to_twin, relayed = [], [], []
+
+        def relay(j):
+            over_y[j].wait_recv()
+            block = out.at[sources[j], other]
+            relayed.append(remote(block, block, x_s.at[j], x_r.at[j], (e, twin)))
+            relayed[-1].start()
+
+        for j, s in enumerate(sources):
+            place = out.at[s, w]
+            block = rows.at[e] if j == 0 else place
+            if j:
+                first[j - 1].wait_recv()
+            over_y.append(remote(block, place, y_s.at[j], y_r.at[j], (e, other)))
+            over_y[-1].start()
+            to_twin.append(remote(block, place, c_s.at[j], c_r.at[j], (e, twin)))
+            to_twin[-1].start()
+            if j == 0:
+                load.wait()
+                store = pltpu.make_async_copy(own, out.at[e, w], load_sem.at[1])
+                store.start()
+            else:
+                relay(j - 1)
+            yield
+        relay(n - 1)
+        store.wait()
+        for copy in first + over_y:
+            copy.wait_send()
+        for copy in to_twin + relayed:
+            copy.wait()
+
+    return Job(
+        [rows],
+        [jax.ShapeDtypeStruct((n, n_ws, count, width), rows.dtype)],
+        [pltpu.VMEM((count, width), rows.dtype), DMA((2,)), DMA((n - 1,)), DMA((n - 1,))]
+        + [DMA((n,)) for _ in range(6)],
+        n,
+        body,
+    )
+
+
+def combine_job(part):
+    n, _, count, width = part.shape
+    block = (n, count, width)
+
+    def body(
+        part, out, mine, core, sum_y, from_y, total, load_sem, c_s, c_r, y_s, y_r, ep_s, ep_r, own_sem
+    ):
+        e, w = lax.axis_index("ep"), lax.axis_index("ws")
+        twin, other, last = flip(w, 1), flip(w, 2), flip(w, 3)
+        targets = [flip(e, k) for k in far_first(n)] + [e]
+        greet([(s, w) for s in targets[:-1]] + [(e, twin), (e, other)])
+        loads, cores = {}, {}
+        for half, near, far in ((1, other, last), (0, w, twin)):
+            for j, s in enumerate(targets):
+                cores[half, j] = remote(
+                    part.at[s, far], core.at[half, j], c_s.at[half, j], c_r.at[half, j], (e, twin)
+                )
+                cores[half, j].start()
+                loads[half, j] = pltpu.make_async_copy(
+                    part.at[s, near], mine.at[half, j], load_sem.at[half, j]
+                )
+                loads[half, j].start()
+        over_y, back = [], []
+
+        def send_y(j):
+            over_y.append(remote(sum_y.at[j], from_y.at[j], y_s.at[j], y_r.at[j], (e, other)))
+            over_y[-1].start()
+
+        def send_back(j):
+            back.append(remote(total.at[j], out.at[e], ep_s.at[j], ep_r.at[j], (targets[j], w)))
+            back[-1].start()
+
+        for j in range(n):
+            loads[1, j].wait()
+            cores[1, j].wait_recv()
+            sum_y[j] = (mine[1, j].astype(f32) + core[1, j].astype(f32)).astype(bf16)
+            if j:
+                send_y(j - 1)
+        loads[0, 0].wait()
+        cores[0, 0].wait_recv()
+        send_y(n - 1)
+        for j in range(n):
+            if j:
+                loads[0, j].wait()
+                cores[0, j].wait_recv()
+            over_y[j].wait_recv()
+            total[j] = (
+                mine[0, j].astype(f32) + core[0, j].astype(f32) + from_y[j].astype(f32)
+            ).astype(bf16)
+            if j:
+                send_back(j - 1)
+            yield
+        for copy in over_y + list(cores.values()):
+            copy.wait_send()
+        keep = pltpu.make_async_copy(total.at[n - 1], out.at[e], own_sem)
+        keep.start()
+        for copy in back:
+            copy.wait()
+        keep.wait()
+
+    return Job(
+        [part],
+        [jax.ShapeDtypeStruct(block, part.dtype)],
+        [
+            pltpu.VMEM((2,) + block, part.dtype),
+            pltpu.VMEM((2,) + block, part.dtype),
+            pltpu.VMEM(block, part.dtype),
+            pltpu.VMEM(block, part.dtype),
+            pltpu.VMEM(block, part.dtype),
+            DMA((2, n)),
+            DMA((2, n)),
+            DMA((2, n)),
+            DMA((n,)),
+            DMA((n,)),
+            DMA((n - 1,)),
+            DMA((n - 1,)),
+            DMA,
+        ],
+        n,
+        body,
+    )
+
+
+def exchange_job(rows):
+    n = rows.shape[0]
+
+    def body(rows, out, own, load_sem, ep_s, ep_r):
+        e, w = lax.axis_index("ep"), lax.axis_index("ws")
+        targets = [flip(e, k) for k in far_first(n)]
+        greet([(s, w) for s in targets])
+        copies = []
+        for i, s in enumerate(targets):
+            copies.append(remote(rows.at[s], out.at[e], ep_s.at[i], ep_r.at[i], (s, w)))
+            copies[-1].start()
+        load = pltpu.make_async_copy(rows.at[e], own, load_sem.at[0])
+        load.start()
+        load.wait()
+        store = pltpu.make_async_copy(own, out.at[e], load_sem.at[1])
+        store.start()
+        yield
+        store.wait()
+        for copy in copies:
+            copy.wait()
+
+    return Job(
+        [rows],
+        [jax.ShapeDtypeStruct(rows.shape, rows.dtype)],
+        [pltpu.VMEM(rows.shape[1:], rows.dtype), DMA((2,)), DMA((n - 1,)), DMA((n - 1,))],
+        1,
+        body,
+    )
+
+
+def attend_kernel(spans, q_ref, kv_ref, out):
+    count, _, slots, part = q_ref.shape
+    for w, span in enumerate(spans):
+
+        def head(h, carry, w=w, span=span):
+            at = pl.multiple_of(h * HEAD_SIZE, HEAD_SIZE)
+            columns = pl.ds(at, HEAD_SIZE)
+            q, probs, _, values = head_probs(q_ref, kv_ref, w, span, at)
+            mixed = dot(probs.astype(bf16), values)
+            out[:, w, :, columns] = mixed.reshape(count, slots, HEAD_SIZE).astype(bf16)
+            return carry
+
+        lax.fori_loop(0, part // HEAD_SIZE, head, 0)
+
+
+def slot_rows(ref, w, at):
+    count, _, slots, _ = ref.shape
+    rows = ref[:, w, :, pl.ds(at, HEAD_SIZE)].astype(f32)
+    return rows.reshape(count * slots, HEAD_SIZE).astype(bf16)
+
+
+def head_probs(q_ref, kv_ref, w, span, at):
+    half = kv_ref.shape[1] // 2
+    q = slot_rows(q_ref, w, at)
+    keys = kv_ref[:span, pl.ds(at, HEAD_SIZE)]
+    values = kv_ref[:span, pl.ds(pl.multiple_of(half + at, HEAD_SIZE), HEAD_SIZE)]
+    scores = dot_t(q, keys) * HEAD_SIZE ** (-0.5)
+    weight = jnp.exp(scores - jnp.max(scores, -1, keepdims=True))
+    probs = weight / jnp.sum(weight, -1, keepdims=True)
+    return q, probs, keys, values
+
+
+def attend_call(queries, kv, spans):
+    return pl.pallas_call(
+        functools.partial(attend_kernel, spans),
+        out_shape=jax.ShapeDtypeStruct(queries.shape, bf16),
+        in_specs=[VM, VM],
+        out_specs=VM,
+        compiler_params=pltpu.CompilerParams(vmem_limit_bytes=VMEM_LIMIT),
+        name="attend",
+    )(queries, kv)
+
+
+def attend_back_kernel(spans, q_ref, g_ref, kv_ref, grad_q, grad_kv, total):
+    count, _, slots, part = q_ref.shape
+    total[...] = jnp.zeros_like(total)
+    for w, span in enumerate(spans):
+
+        def head(h, carry, w=w, span=span):
+            at = pl.multiple_of(h * HEAD_SIZE, HEAD_SIZE)
+            columns = pl.ds(at, HEAD_SIZE)
+            q, probs, keys, values = head_probs(q_ref, kv_ref, w, span, at)
+            grad = slot_rows(g_ref, w, at)
+            grad_probs = dot_t(grad, values)
+            centred = jnp.sum(probs * grad_probs, -1, keepdims=True)
+            grad_scores = (probs * (grad_probs - centred)).astype(bf16)
+            grad_rows = dot(grad_scores, keys) * HEAD_SIZE ** (-0.5)
+            grad_q[:, w, :, columns] = grad_rows.reshape(count, slots, HEAD_SIZE).astype(bf16)
+            total[:span, columns] += t_dot(grad_scores, q) * HEAD_SIZE ** (-0.5)
+            at_value = pl.ds(pl.multiple_of(part + at, HEAD_SIZE), HEAD_SIZE)
+            total[:span, at_value] += t_dot(probs.astype(bf16), grad)
+            return carry
+
+        lax.fori_loop(0, part // HEAD_SIZE, head, 0)
+    grad_kv[...] = total[...].astype(bf16)
+
+
+def attend_back_call(queries, grads, kv, spans):
+    return pl.pallas_call(
+        functools.partial(attend_back_kernel, spans),
+        out_shape=[
+            jax.ShapeDtypeStruct(queries.shape, bf16),
+            jax.ShapeDtypeStruct(kv.shape, bf16),
+        ],
+        in_specs=[VM, VM, VM],
+        out_specs=[VM, VM],
+        scratch_shapes=[pltpu.VMEM(kv.shape, f32)],
+        compiler_params=pltpu.CompilerParams(vmem_limit_bytes=VMEM_LIMIT),
+        name="attend_back",
+    )(queries, grads, kv)
+
+
+def gather_kernel(n, n_ws, own, out, load_sem, w_s, w_r, ep_s, ep_r):
+    e, w = lax.axis_index("ep"), lax.axis_index("ws")
+    beside = [flip(w, k) for k in range(1, n_ws)]
+    across = [flip(e, k) for k in far_first(n)]
+    greet([(e, p) for p in beside] + [(s, w) for s in across])
+    keep = pltpu.make_async_copy(own, out.at[e, w], load_sem)
+    keep.start()
+    first = []
+    for i, p in enumerate(beside):
+        first.append(remote(own, out.at[e, w], w_s.at[i], w_r.at[i], (e, p)))
+        first[-1].start()
+    keep.wait()
+    for copy in first:
+        copy.wait()
+    second = []
+    for i, s in enumerate(across):
+        second.append(remote(out.at[e], out.at[e], ep_s.at[i], ep_r.at[i], (s, w)))
+        second[-1].start()
+    for copy in second:
+        copy.wait()
+
+
+def gather_call(own, n, n_ws):
+    return pl.pallas_call(
+        functools.partial(gather_kernel, n, n_ws),
+        out_shape=jax.ShapeDtypeStruct((n, n_ws) + own.shape, own.dtype),
+        in_specs=[VM],
+        out_specs=VM,
+        scratch_shapes=[DMA, DMA((n_ws - 1,)), DMA((n_ws - 1,)), DMA((n - 1,)), DMA((n - 1,))],
+        compiler_params=pltpu.CompilerParams(collective_id=3, has_side_effects=True),
+        name="gather_gains",
+    )(own)
+
+
+def reduce_kernel(n, n_ws, parts, out, held, all_parts, load_sem, w_s, w_r, ep_s, ep_r):
+    e, w = lax.axis_index("ep"), lax.axis_index("ws")
+    beside = [flip(w, k) for k in range(1, n_ws)]
+    across = [flip(e, k) for k in far_first(n)]
+    greet([(e, p) for p in beside] + [(s, w) for s in across])
+    keep = pltpu.make_async_copy(parts.at[:, w], held.at[:, w], load_sem.at[0])
+    keep.start()
+    first = []
+    for i, p in enumerate(beside):
+        first.append(remote(parts.at[:, p], held.at[:, w], w_s.at[i], w_r.at[i], (e, p)))
+        first[-1].start()
+    keep.wait()
+    for copy in first:
+        copy.wait()
+    keep = pltpu.make_async_copy(held.at[e], all_parts.at[e], load_sem.at[1])
+    keep.start()
+    second = []
+    for i, s in enumerate(across):
+        second.append(remote(held.at[s], all_parts.at[e], ep_s.at[i], ep_r.at[i], (s, w)))
+        second[-1].start()
+    keep.wait()
+    for copy in second:
+        copy.wait()
+    out[...] = jnp.sum(jnp.sum(all_parts[...], 0), 0)
+
+
+def reduce_call(parts):
+    n, n_ws = parts.shape[:2]
+    return pl.pallas_call(
+        functools.partial(reduce_kernel, n, n_ws),
+        out_shape=jax.ShapeDtypeStruct(parts.shape[2:], parts.dtype),
+        in_specs=[VM],
+        out_specs=VM,
+        scratch_shapes=[
+            pltpu.VMEM(parts.shape, parts.dtype),
+            pltpu.VMEM(parts.shape, parts.dtype),
+            DMA((2,)),
+            DMA((n_ws - 1,)),
+            DMA((n_ws - 1,)),
+            DMA((n - 1,)),
+            DMA((n - 1,)),
+        ],
+        compiler_params=pltpu.CompilerParams(collective_id=4, has_side_effects=True),
+        name="reduce_gains",
+    )(parts)
+
+
+def small(n_ep):
+    return n_ep == MIXTURE_EXPERTS and lax.axis_size("ws") == 4
+
+
+PLAIN = {
+    grad_job: t_dot,
+    pair_grad_job: lambda a, b, c: jnp.stack([t_dot(a, b), t_dot(a, c)], 1),
+    product_job: lambda a, b, dtype: dot(a, b).astype(dtype),
+}
+
+
+def beside(job, plain, arg, fills, collective_id, name):
+    if job is None:
+        return [plain(arg)] + [PLAIN[make](*rest) for make, *rest in fills]
+    return run_jobs(job(arg), [make(*rest) for make, *rest in fills], collective_id, name)
+
+
+def exchange_plain(send):
     return lax.all_to_all(send, "ep", split_axis=0, concat_axis=0, tiled=True)
+
+
+def exchange(send, *fills, collective_id=2, name="exchange"):
+    job = exchange_job if small(send.shape[0]) else None
+    return beside(job, exchange_plain, send, fills, collective_id, name)
 
 
 def spread(rows, group):
@@ -41,22 +652,31 @@
     )
 
 
-def dispatch(rows, group):
-    got = exchange(spread(rows, group))
-    return lax.all_gather(got, "ws", axis=1, tiled=False)
-
-
-def combine(partial, group, n_ep, n_ws):
+def dispatch(rows, group, *fills, collective_id=0, name="dispatch"):
+    width = rows.shape[-1]
+
+    def plain(blocks):
+        return lax.all_gather(exchange_plain(blocks), "ws", axis=1, tiled=False)
+
+    job = functools.partial(dispatch_job, n_ws=4) if small(MIXTURE_EXPERTS * group) else None
+    out = beside(job, plain, spread(rows, group), fills, collective_id, name)
+    return [out[0].reshape(-1, width)] + list(out[1:])
+
+
+def combine(partial, group, n_ep, n_ws, *fills, collective_id=1, name="combine"):
     width = partial.shape[-1]
-    part = partial.reshape(n_ep, n_ws, ROWS, width).transpose(1, 0, 2, 3)
-    part = part.reshape(n_ws * n_ep * ROWS, width)
-    own = lax.psum_scatter(part, "ws", scatter_dimension=0, tiled=True)
-    own = own.reshape(n_ep, ROWS, width)
-    back = exchange(own)
-    if group == 1:
-        return back.reshape(MIXTURE_EXPERTS * ROWS, width)
-    total = jnp.sum(back.reshape(MIXTURE_EXPERTS, group, ROWS, width).astype(f32), 1)
-    return total.astype(bf16).reshape(MIXTURE_EXPERTS * ROWS, width)
+
+    def plain(part):
+        part = part.transpose(1, 0, 2, 3).reshape(n_ws * n_ep * ROWS, width)
+        own = lax.psum_scatter(part, "ws", scatter_dimension=0, tiled=True)
+        return exchange_plain(own.reshape(n_ep, ROWS, width))
+
+    part = partial.reshape(n_ep, n_ws, ROWS, width)
+    job = combine_job if small(n_ep) else None
+    back, *rest = beside(job, plain, part, fills, collective_id, name)
+    if group > 1:
+        back = jnp.sum(back.reshape(MIXTURE_EXPERTS, group, ROWS, width).astype(f32), 1).astype(bf16)
+    return [back.reshape(MIXTURE_EXPERTS * ROWS, width)] + rest
 
 
 def slot_tables(routes, slots):
@@ -103,8 +723,14 @@
     place = lax.axis_index("ws")
     scale = HEAD_SIZE ** (-0.5)
 
-    gain_one = lax.all_gather(gain_attn, ("ep", "ws"), axis=0, tiled=True).astype(f32)
-    gain_two = lax.all_gather(gain_ffn, ("ep", "ws"), axis=0, tiled=True).astype(f32)
+    short = small(n_ep) and gain_attn.shape[0] == 64
+    if short:
+        gains = jnp.concatenate([gain_attn, gain_ffn], 0).astype(f32)[None]
+        gains = gather_call(gains, n_ep, n_ws).reshape(n_ep * n_ws, 2, -1)
+        gain_one, gain_two = gains[:, 0].reshape(-1), gains[:, 1].reshape(-1)
+    else:
+        gain_one = lax.all_gather(gain_attn, ("ep", "ws"), axis=0, tiled=True).astype(f32)
+        gain_two = lax.all_gather(gain_ffn, ("ep", "ws"), axis=0, tiled=True).astype(f32)
     plain = group == 1 and key_value_weight.shape[1] == HEAD_SIZE
     if plain:
         half = n_ep // 2
@@ -130,13 +756,15 @@
     ffn_tokens = ffn_pairs[0] + ffn_pairs[1]
 
     normed_sequence = lax.all_gather(normed, "ws", axis=0, tiled=True)
-    rows_one = dispatch(dot(attn_tokens, normed).astype(bf16), group).reshape(-1, width)
+    rows_one = dispatch(dot(attn_tokens, normed).astype(bf16), group)[0]
     kv = dot(normed_sequence, kv_own).astype(bf16)
     keys = kv[:, :own_width].reshape(sequence, -1, HEAD_SIZE)
     values = kv[:, own_width:].reshape(sequence, -1, HEAD_SIZE)
 
     owner_query = dot(rows_one, w_query[0]).astype(bf16)
-    queries = exchange(owner_query.reshape(n_ep, n_ws * ROWS, part))
+    queries = exchange(owner_query.reshape(n_ep, n_ws * ROWS, part))[0]
+    spans = [(w * local_tokens // BLOCK + 1) * BLOCK for w in range(n_ws)]
+    fused = small(n_ep)
     queries = queries.reshape(MIXTURE_EXPERTS, group, n_ws, ROWS, part)
 
     def by_block(rows):
@@ -156,21 +784,25 @@
         )
         return rows.reshape(n_ep, n_ws * ROWS, part)
 
-    spans = [(w * local_tokens // BLOCK + 1) * BLOCK for w in range(n_ws)]
-    kept = []
-    mixed_pieces = []
-    for q, span in zip(by_block(queries), spans):
-        scores = (
-            jnp.einsum("rhd,shd->hrs", q, keys[:span], preferred_element_type=f32) * scale
-        )
-        probs = jax.nn.softmax(scores, axis=-1)
-        mixed = jnp.einsum(
-            "hrs,shd->rhd", probs.astype(bf16), values[:span], preferred_element_type=f32
-        )
-        kept.append((q, probs))
-        mixed_pieces.append(mixed.astype(bf16))
-    owner_mixed = exchange(to_experts(mixed_pieces)).reshape(-1, part)
-    attn_slots = combine(dot(owner_mixed, w_output[0]).astype(bf16), group, n_ep, n_ws)
+    if fused:
+        queries = queries.reshape(n_ep, n_ws, ROWS, part)
+        mixed = attend_call(queries, kv, spans).reshape(n_ep, n_ws * ROWS, part)
+    else:
+        kept = []
+        mixed_pieces = []
+        for q, span in zip(by_block(queries), spans):
+            scores = (
+                jnp.einsum("rhd,shd->hrs", q, keys[:span], preferred_element_type=f32) * scale
+            )
+            probs = jax.nn.softmax(scores, axis=-1)
+            mixed = jnp.einsum(
+                "hrs,shd->rhd", probs.astype(bf16), values[:span], preferred_element_type=f32
+            )
+            kept.append((q, probs))
+            mixed_pieces.append(mixed.astype(bf16))
+        mixed = to_experts(mixed_pieces)
+    owner_mixed = exchange(mixed)[0].reshape(-1, part)
+    attn_slots = combine(dot(owner_mixed, w_output[0]).astype(bf16), group, n_ep, n_ws)[0]
 
     def weighted(pairs, gates, slot_values):
         return sum(gates[:, k : k + 1] * t_dot(pairs[k], slot_values) for k in range(2))
@@ -186,11 +818,17 @@
     normed_two = (unit_two * gain_two).astype(bf16)
 
     grad_out = cotangent.astype(f32)
-    expert_grad = dispatch(to_slots(ffn_pairs, gate_ffn, grad_out), group).reshape(-1, width)
-    expert_rows = dispatch(dot(ffn_tokens, normed_two).astype(bf16), group).reshape(-1, width)
+    grad_slots = to_slots(ffn_pairs, gate_ffn, grad_out)
     gate_weight, up_weight = w_in[0, :, 0], w_in[0, :, 1]
-    gate_pre = dot(expert_rows, gate_weight)
-    up_pre = dot(expert_rows, up_weight)
+    expert_rows = dispatch(dot(ffn_tokens, normed_two).astype(bf16), group)[0]
+    expert_grad, gate_pre, up_pre = dispatch(
+        grad_slots,
+        group,
+        (product_job, expert_rows, gate_weight, f32),
+        (product_job, expert_rows, up_weight, f32),
+        collective_id=5,
+        name="dispatch_ffn_in",
+    )
     sigmoid_gate = jax.nn.sigmoid(gate_pre)
     silu_gate = gate_pre * sigmoid_gate
     activated = (silu_gate * up_pre).astype(bf16)
@@ -200,44 +838,74 @@
         grad_act * up_pre * sigmoid_gate * (1.0 + gate_pre * (1.0 - sigmoid_gate))
     ).astype(bf16)
     back_two = (dot_t(grad_gate, gate_weight) + dot_t(grad_up, up_weight)).astype(bf16)
-    back_slots = combine(back_two, group, n_ep, n_ws)
-    ffn_slots = combine(dot(activated, w_out[0]).astype(bf16), group, n_ep, n_ws)
-    result = hidden_state + weighted(ffn_pairs, gate_ffn, ffn_slots)
-    grad_second = t_dot(activated, expert_grad)
-    grad_first = jnp.stack([t_dot(expert_rows, grad_gate), t_dot(expert_rows, grad_up)], 1)
+    back_slots, forward_part, grad_second = combine(
+        back_two,
+        group,
+        n_ep,
+        n_ws,
+        (product_job, activated, w_out[0], bf16),
+        (grad_job, activated, expert_grad),
+        collective_id=6,
+        name="combine_ffn_out",
+    )
 
     grad_normed_two = t_dot(ffn_tokens, back_slots)
     grad_hidden_norm, grad_gain_two = norm_back(grad_normed_two, unit_two, inverse_two, gain_two)
     grad_hidden = grad_out + grad_hidden_norm
-    owner_grad = dispatch(to_slots(attn_pairs, gate_attn, grad_hidden), group).reshape(-1, width)
-    grad_output = t_dot(owner_mixed, owner_grad)
+    owner_grad, grad_first = dispatch(
+        to_slots(attn_pairs, gate_attn, grad_hidden),
+        group,
+        (pair_grad_job, expert_rows, grad_gate, grad_up),
+        collective_id=7,
+        name="dispatch_grad_in",
+    )
     back_mixed = dot_t(owner_grad, w_output[0]).astype(bf16)
-    mixed_grads = exchange(back_mixed.reshape(n_ep, n_ws * ROWS, part))
-
-    grad_keys, grad_values, query_pieces = 0.0, 0.0, []
-    for (q, probs), grad, span in zip(kept, by_block(mixed_grads), spans):
-        grad_probs = jnp.einsum("rhd,shd->hrs", grad, values[:span], preferred_element_type=f32)
-        centred = jnp.sum(probs * grad_probs, -1, keepdims=True)
-        grad_scores = (probs * (grad_probs - centred)).astype(bf16)
-        grad_q = (
-            jnp.einsum("hrs,shd->rhd", grad_scores, keys[:span], preferred_element_type=f32)
-            * scale
-        )
-        query_pieces.append(grad_q.astype(bf16))
-        pad = ((0, sequence - span), (0, 0), (0, 0))
-        piece = jnp.einsum("hrs,rhd->shd", grad_scores, q, preferred_element_type=f32) * scale
-        grad_keys = grad_keys + jnp.pad(piece, pad)
-        piece = jnp.einsum(
-            "hrs,rhd->shd", probs.astype(bf16), grad, preferred_element_type=f32
-        )
-        grad_values = grad_values + jnp.pad(piece, pad)
-    grad_kv_rows = jnp.concatenate(
-        [grad_keys.reshape(sequence, -1), grad_values.reshape(sequence, -1)], 1
-    ).astype(bf16)
-    owner_grad_query = exchange(to_experts(query_pieces)).reshape(-1, part)
-    grad_query = t_dot(rows_one, owner_grad_query)
+    mixed_grads, grad_output = exchange(
+        back_mixed.reshape(n_ep, n_ws * ROWS, part),
+        (grad_job, owner_mixed, owner_grad),
+        collective_id=8,
+        name="exchange_grad_output",
+    )
+
+    if fused:
+        mixed_grads = mixed_grads.reshape(n_ep, n_ws, ROWS, part)
+        query_grads, grad_kv_rows = attend_back_call(queries, mixed_grads, kv, spans)
+        query_grads = query_grads.reshape(n_ep, n_ws * ROWS, part)
+    else:
+        grad_keys, grad_values, query_pieces = 0.0, 0.0, []
+        for (q, probs), grad, span in zip(kept, by_block(mixed_grads), spans):
+            grad_probs = jnp.einsum("rhd,shd->hrs", grad, values[:span], preferred_element_type=f32)
+            centred = jnp.sum(probs * grad_probs, -1, keepdims=True)
+            grad_scores = (probs * (grad_probs - centred)).astype(bf16)
+            grad_q = (
+                jnp.einsum("hrs,shd->rhd", grad_scores, keys[:span], preferred_element_type=f32)
+                * scale
+            )
+            query_pieces.append(grad_q.astype(bf16))
+            pad = ((0, sequence - span), (0, 0), (0, 0))
+            piece = jnp.einsum("hrs,rhd->shd", grad_scores, q, preferred_element_type=f32) * scale
+            grad_keys = grad_keys + jnp.pad(piece, pad)
+            piece = jnp.einsum(
+                "hrs,rhd->shd", probs.astype(bf16), grad, preferred_element_type=f32
+            )
+            grad_values = grad_values + jnp.pad(piece, pad)
+        grad_kv_rows = jnp.concatenate(
+            [grad_keys.reshape(sequence, -1), grad_values.reshape(sequence, -1)], 1
+        ).astype(bf16)
+        query_grads = to_experts(query_pieces)
+    owner_grad_query = exchange(query_grads)[0].reshape(-1, part)
     back_normed = dot_t(owner_grad_query, w_query[0]).astype(bf16)
-    normed_back = combine(back_normed, group, n_ep, n_ws)
+    normed_back, grad_query = combine(
+        back_normed,
+        group,
+        n_ep,
+        n_ws,
+        (grad_job, rows_one, owner_grad_query),
+        collective_id=9,
+        name="combine_grad_query",
+    )
+    ffn_slots = combine(forward_part, group, n_ep, n_ws)[0]
+    result = hidden_state + weighted(ffn_pairs, gate_ffn, ffn_slots)
 
     grad_kv = t_dot(normed_sequence, grad_kv_rows)
     if plain:
@@ -257,9 +925,14 @@
     grad_normed = t_dot(attn_tokens, normed_back) + from_kv.astype(f32)
     grad_input_norm, grad_gain_one = norm_back(grad_normed, unit_one, inverse_one, gain_one)
     grad_input = grad_hidden + grad_input_norm
-    gain_shards = lax.psum_scatter(
-        jnp.stack([grad_gain_one, grad_gain_two], 0), ("ep", "ws"), scatter_dimension=1, tiled=True
-    )
+    gain_grads = jnp.stack([grad_gain_one, grad_gain_two], 0)
+    if short:
+        parts = gain_grads.reshape(2, n_ep, n_ws, -1).transpose(1, 2, 0, 3)
+        gain_shards = reduce_call(parts.reshape(n_ep, n_ws, 1, -1)).reshape(2, -1)
+    else:
+        gain_shards = lax.psum_scatter(
+            gain_grads, ("ep", "ws"), scatter_dimension=1, tiled=True
+        )
     return (
         result.astype(bf16),
         grad_input,

time: 1250 us -> 865 us (0.69)
  Pallas kernels: 0 us -> 607 us
  waiting for transfers between devices: 482 us -> 23.2 us
  blocking collectives: 320 us -> 0 us
  matrix products: 236 us -> 116 us
  local copies, waits for them, and re-layouts: 115 us -> 78.5 us
  other arithmetic: 34.5 us -> 11.1 us
  starting transfers between devices: 30.5 us -> 8.69 us
    pallas_call x0 -> x16, Pallas kernels: none -> 607 us  [the longest x12 552 us: run_jobs(): pl.pallas_call(kernel, out_shape=outs, in_specs=[ANY] * len(args), out_sp...]
    all_to_all x8 -> x0, blocking collectives: 279 us -> none  [exchange(): return lax.all_to_all(send, 'ep', split_axis=0, concat_axis=0, tiled=True)]
    unnamed x14 -> x4, waiting for transfers between devices: 131 us -> 0.07 us
    reduce_scatter x4 -> x0, waiting for transfers between devices: 102 us -> none  [combine(): own = lax.psum_scatter(part, 'ws', scatter_dimension=0, tiled=True)]
    all_to_all x4 -> x0, waiting for transfers between devices: 70.9 us -> none  [exchange(): return lax.all_to_all(send, 'ep', split_axis=0, concat_axis=0, tiled=True)]
    all_gather x1, waiting for transfers between devices: 84.5 us -> 14.5 us  [local(): kv_own = lax.all_gather(mine, 'ep', axis=1, tiled=True)]
    all_gather x4 -> x0, waiting for transfers between devices: 53.6 us -> none  [dispatch(): return lax.all_gather(got, 'ws', axis=1, tiled=False)]
    dot_general x22 -> x0, matrix products: 47.9 us -> none  [the longest x4 17.2 us: local(): jnp.einsum('hrs,rhd->shd', probs.astype(bf16), grad, preferred_element_ty...]
  transfers between devices with their start and end apart: 19 -> 6, of which waited for: 12 -> 2; matrix products, arithmetic and copies ran while one was open for 21% -> 9% of each run, Pallas kernels for 0% -> 33%
where the time goes in v3:
time: 865 us; the launch traced here: 858 us
  Pallas kernels  607 us (70%)
  matrix products  116 us (13%)
  local copies, waits for them, and re-layouts  78.5 us (9%)
  waiting for transfers between devices  23.2 us (3%)
  between operations  14.6 us (2%)
  other arithmetic  11.1 us (1%)
  starting transfers between devices  8.69 us (1%)
    pallas_call x12, Pallas kernels, run_jobs(): pl.pallas_call(kernel, out_shape=outs, in_specs=[ANY] * len(args), out_sp...  552 us
    dot_general x6, matrix products, dot_t(): lax.dot_general(a, b, (((1,), (1,)), ((), ())), preferred_element_type=f32)  68 us
    unnamed x48, local copies, waits for them, and re-layouts  33.6 us
    dot_general x9, matrix products, dot(): return jnp.dot(a, b, preferred_element_type=f32)  27.8 us
    slice x1, local copies, waits for them, and re-layouts, local(): gate_weight, up_weight = (w_in[0, :, 0], w_in[0, :, 1])  22.7 us
    dot_general x7, matrix products, t_dot(): lax.dot_general(a, b, (((0,), (0,)), ((), ())), preferred_element_type=f32)  19.7 us
    pallas_call x1, Pallas kernels, attend_back_call(): pl.pallas_call(functools.partial(attend_back_kernel, spans), out_shape=[j...  18.4 us
  transfers between devices with their start and end apart: 6, of which 2 were waited for; matrix products, arithmetic and copies ran while one was open for 9% of the time, Pallas kernels for 33%

profile of v3, /device:TPU:1, one launch (start us, length us, event | category | flops | bytes accessed | tf_op | source)
XLA Modules:
  0.0 858.3 jit_solution(4066753670155927687)
XLA Ops:
  8.6 11.4 %gather_gains.1 = f32[8,4,1,128]{3,2,1,0:T(1,128)} custom-call(f32[1,128]{1,0:T(1,128)} %maximum_convert_fusion.own), custom_call_target="tpu_custom_call" | custom-call | tf_op jit(solution)/shard_map/gather_gains/pallas_call | solution.py:563
  33.3 51.6 %dispatch.2 = bf16[8,4,40,2048]{3,2,1,0:T(8,128)(2,1)} custom-call(bf16[8,40,2048]{2,1,0:T(8,128)(2,1)} %bitcast.118), custom_call_target="tpu_custom_call" | custom-call | tf_op jit(solution)/shard_map/dispatch/pallas_call | solution.py:101
  93.0 39.1 %exchange.3 = bf16[8,160,512]{2,1,0:T(8,128)(2,1)} custom-call(bf16[8,160,512]{2,1,0:T(8,128)(2,1)} %bitcast.134), custom_call_target="tpu_custom_call" | custom-call | tf_op jit(solution)/shard_map/exchange/pallas_call | solution.py:101
  134.4 22.7 %fusion.65 = (bf16[1,2048,1,1408]{3,2,1,0:T(2,128)(2,1)S(1)}, bf16[1,2048,1,1408]{3,2,1,0:T(2,128)(2,1)}) fusion(bf16[1,2048,2,1408]{3,2,1,0:T(2,128)(2,1)} %param.21), kind=kLoop, calls=%fused_computation.117 | loop fusion | bytes 23068672 | tf_op jit(solution)/shard_map/slice | solution.py:822
  157.1 12.5 %copy_bitcast_fusion = (bf16[2048,1408]{1,0:T(8,128)(2,1)}, bf16[2048,1408]{1,0:T(8,128)(2,1)}) fusion(bf16[1,2048,1,1408]{3,2,1,0:T(2,128)(2,1)S(1)} %get-tuple-element.46, bf16[1,2048,1,1408]{3,2,1,0:T(2,128)(2,1)} %get-tuple-element.47), kind=kLoop, calls=%fused_computation.8 | loop fusion | bytes 23068672 | tf_op jit(solution)/shard_map/squeeze | solution.py:822
  169.6 14.5 %all-gather.5.cloned.1.call-done = bf16[2048,1024]{1,0:T(8,128)(2,1)} async-done(((bf16[2048,128]{1,0:T(8,128)(2,1)}), bf16[2048,1024]{1,0:T(8,128)(2,1)}) %all-gather.5.cloned.1.call-update) | async-done | bytes 4194320 | tf_op jit(solution)/shard_map/all_gather | solution.py:743
  190.2 13.2 %attend.1 = bf16[8,4,40,512]{3,2,1,0:T(8,128)(2,1)} custom-call(bf16[8,4,40,512]{3,2,1,0:T(8,128)(2,1)} %bitcast.103, bf16[512,1024]{1,0:T(8,128)(2,1)} %convolution_convert_fusion.8.kv_ref), custom_call_target="tpu_custom_call" | custom-call | tf_op jit(solution)/shard_map/attend/pallas_call | solution.py:491
  203.4 25.9 %exchange.4 = bf16[8,160,512]{2,1,0:T(8,128)(2,1)} custom-call(bf16[8,160,512]{2,1,0:T(8,128)(2,1)} %bitcast.112), custom_call_target="tpu_custom_call" | custom-call | tf_op jit(solution)/shard_map/exchange/pallas_call | solution.py:101
  235.2 52.1 %combine.2 = bf16[8,40,2048]{2,1,0:T(8,128)(2,1)} custom-call(bf16[8,4,40,2048]{3,2,1,0:T(8,128)(2,1)} %bitcast.115), custom_call_target="tpu_custom_call" | custom-call | tf_op jit(solution)/shard_map/combine/pallas_call | solution.py:101
  292.7 40.3 %dispatch.3 = bf16[8,4,40,2048]{3,2,1,0:T(8,128)(2,1)} custom-call(bf16[8,40,2048]{2,1,0:T(8,128)(2,1)} %bitcast.119), custom_call_target="tpu_custom_call" | custom-call | tf_op jit(solution)/shard_map/dispatch/pallas_call | solution.py:101
  333.0 47.3 %dispatch_ffn_in.1 = (bf16[8,4,40,2048]{3,2,1,0:T(8,128)(2,1)}, f32[1280,1408]{1,0:T(8,128)}, f32[1280,1408]{1,0:T(8,128)}) custom-call(bf16[8,40,2048]{2,1,0:T(8,128)(2,1)} %bitcast.111, bf16[1280,2048]{1,0:T(8,128)(2,1)} %bitcast.96, bf16[2048,1408]{1,0:T(8,128)(2,1)} %get-tuple-element.63.refs_2_, bf16[1280,2048]{1,0:T(8,128)(2,1)} %bitcast.97, ...), custom_call_target="tpu_custom_call" | custom-call | tf_op jit(solution)/shard_map/dispatch_ffn_in/pallas_call | solution.py:101
  380.3 19.8 %multiply_convert_fusion = (bf16[1280,1408]{1,0:T(8,128)(2,1)}, bf16[1280,1408]{1,0:T(8,128)(2,1)}, bf16[1280,1408]{1,0:T(8,128)(2,1)}) fusion(f32[1280,1408]{1,0:T(8,128)} %get-tuple-element.24, f32[1280,1408]{1,0:T(8,128)} %get-tuple-element.25, bf16[1280,2048]{1,0:T(8,128)(2,1)} %bitcast.120, bf16[1,1408,2048]{2,1,0:T(8,128)(2,1)} %param.22), kind=kOutput, calls=%fused_computation.3 | convolution fusion | flops 7409008640 | bytes 36241408 | tf_op jit(solution)/shard_map/dot_general | solution.py:35
  400.1 14.4 %fusion.66 = f32[1280,2048]{1,0:T(8,128)} fusion(bf16[1280,1408]{1,0:T(8,128)(2,1)} %get-tuple-element.44.refs_2_, bf16[2048,1408]{1,0:T(8,128)(2,1)} %get-tuple-element.63.refs_2_), kind=kOutput, calls=%fused_computation.118 | convolution fusion | flops 7381975040 | bytes 19857408 | tf_op jit(solution)/shard_map/dot_general | solution.py:35
  414.5 13.9 %add_convert_fusion = bf16[1280,2048]{1,0:T(8,128)(2,1)} fusion(f32[1280,2048]{1,0:T(8,128)} %fusion.66, bf16[1280,1408]{1,0:T(8,128)(2,1)S(1)} %copy-done.8, bf16[2048,1408]{1,0:T(8,128)(2,1)} %get-tuple-element.62.refs_4_), kind=kOutput, calls=%fused_computation | convolution fusion | flops 7387217920 | bytes 25100288 | tf_op jit(solution)/shard_map/dot_general | solution.py:35
  428.4 49.3 %combine_ffn_out.1 = (bf16[8,40,2048]{2,1,0:T(8,128)(2,1)}, bf16[1280,2048]{1,0:T(8,128)(2,1)}, f32[1408,2048]{1,0:T(8,128)}) custom-call(bf16[8,4,40,2048]{3,2,1,0:T(8,128)(2,1)} %bitcast.122, bf16[1280,1408]{1,0:T(8,128)(2,1)} %get-tuple-element.43.refs_1_.refs_3_, bf16[1408,2048]{1,0:T(8,128)(2,1)} %bitcast.110, ...), custom_call_target="tpu_custom_call" | custom-call | tf_op jit(solution)/shard_map/combine_ffn_out/pallas_call | solution.py:101
  482.3 44.5 %dispatch_grad_in.1 = (bf16[8,4,40,2048]{3,2,1,0:T(8,128)(2,1)}, f32[2048,2,1408]{2,1,0:T(2,128)}) custom-call(bf16[8,40,2048]{2,1,0:T(8,128)(2,1)} %bitcast.127, bf16[1280,2048]{1,0:T(8,128)(2,1)} %bitcast.98, bf16[1280,1408]{1,0:T(8,128)(2,1)} %get-tuple-element.44.refs_2_, bf16[1280,1408]{1,0:T(8,128)(2,1)} %get-tuple-element.45.refs_3_), custom_call_target="tpu_custom_call" | custom-call | tf_op jit(solution)/shard_map/dispatch_grad_in/pallas_call | solution.py:101
  533.2 25.2 %exchange_grad_output.1 = (bf16[8,160,512]{2,1,0:T(8,128)(2,1)}, f32[512,2048]{1,0:T(8,128)}) custom-call(bf16[8,160,512]{2,1,0:T(8,128)(2,1)} %bitcast.136, bf16[1280,512]{1,0:T(8,128)(2,1)} %bitcast.124, bf16[1280,2048]{1,0:T(8,128)(2,1)} %bitcast.117), custom_call_target="tpu_custom_call" | custom-call | tf_op jit(solution)/shard_map/exchange_grad_output/pallas_call | solution.py:101
  558.5 18.4 %attend_back.1 = (bf16[8,4,40,512]{3,2,1,0:T(8,128)(2,1)}, bf16[512,1024]{1,0:T(8,128)(2,1)}) custom-call(bf16[8,4,40,512]{3,2,1,0:T(8,128)(2,1)} %bitcast.104, bf16[8,4,40,512]{3,2,1,0:T(8,128)(2,1)} %bitcast.131, bf16[512,1024]{1,0:T(8,128)(2,1)} %convolution_convert_fusion.8.kv_ref), custom_call_target="tpu_custom_call" | custom-call | tf_op jit(solution)/shard_map/attend_back/pallas_call | solution.py:526
  596.2 71.1 %combine.3 = bf16[8,40,2048]{2,1,0:T(8,128)(2,1)} custom-call(bf16[8,4,40,2048]{3,2,1,0:T(8,128)(2,1)} %bitcast.113), custom_call_target="tpu_custom_call" | custom-call | tf_op jit(solution)/shard_map/combine/pallas_call | solution.py:101
  667.4 41.1 %exchange.5 = bf16[8,160,512]{2,1,0:T(8,128)(2,1)} custom-call(bf16[8,160,512]{2,1,0:T(8,128)(2,1)} %bitcast.132), custom_call_target="tpu_custom_call" | custom-call | tf_op jit(solution)/shard_map/exchange/pallas_call | solution.py:101
  715.8 64.5 %combine_grad_query.1 = (bf16[8,40,2048]{2,1,0:T(8,128)(2,1)}, f32[2048,512]{1,0:T(8,128)}) custom-call(bf16[8,4,40,2048]{3,2,1,0:T(8,128)(2,1)} %bitcast.114, bf16[1280,2048]{1,0:T(8,128)(2,1)} %bitcast.101, bf16[1280,512]{1,0:T(8,128)(2,1)} %bitcast.126), custom_call_target="tpu_custom_call" | custom-call | tf_op jit(solution)/shard_map/combine_grad_query/pallas_call | solution.py:101
  788.8 11.8 %reduce_gains.1 = f32[1,128]{1,0:T(1,128)} custom-call(f32[8,4,1,128]{3,2,1,0:T(1,128)} %reshape.172.parts), custom_call_target="tpu_custom_call" | custom-call | tf_op jit(solution)/shard_map/reduce_gains/pallas_call | solution.py:602
  824.4 16.3 %copy.37 = f32[1,2048,2,1408]{3,2,1,0:T(2,128)} copy(f32[1,2048,2,1408]{3,2,1,0:T(2,128)} %bitcast.99) | data formatting | bytes 46137344
  840.7 10.6 %copy.38 = f32[1,1408,2048]{2,1,0:T(8,128)} copy(f32[1,1408,2048]{2,1,0:T(8,128)} %bitcast.109) | data formatting | bytes 23068672
  (108 shorter events, 112.4 us)
Async XLA Ops:
  7.2 222.1 %copy-start = (bf16[1,512,2048]{2,1,0:T(8,128)(2,1)S(1)}, bf16[1,512,2048]{2,1,0:T(8,128)(2,1)}, u32[]{:S(2)}) copy-start(bf16[1,512,2048]{2,1,0:T(8,128)(2,1)} %param.20) | copy-start | bytes 6291460
  7.2 162.4 %all-gather.3.cloned.1.call-start = ((), (), s32[]{:S(2)}) async-start(), calls=%async_computation.2 | async-start | bytes 2621440 | tf_op jit(solution)/shard_map/all_gather | solution.py:758
  22.3 62.6 %copy-start.10 = (f32[2048]{0:T(1024)}, f32[2048]{0:T(1024)S(1)}, u32[]{:S(2)}) copy-start(f32[2048]{0:T(1024)S(1)} %mul.191) | copy-start | bytes 24580
  23.5 61.4 %copy-start.12 = (f32[128]{0:T(128)}, f32[128]{0:T(128)S(1)}, u32[]{:S(2)}) copy-start(f32[128]{0:T(128)S(1)} %add_rsqrt_fusion.1) | copy-start | bytes 1540
  25.6 158.5 %all-gather.5.cloned.1.call-start = ((), (), s32[]{:S(2)}) async-start(), calls=%async_computation.3 | async-start | bytes 4718592 | tf_op jit(solution)/shard_map/all_gather | solution.py:743
  25.6 66.5 %collective-permute-start = (bf16[2048,128]{1,0:T(8,128)(2,1)}, bf16[2048,128]{1,0:T(8,128)(2,1)S(1)}, u32[]{:S(2)}, u32[]{:S(2)}) collective-permute-start(bf16[2048,128]{1,0:T(8,128)(2,1)} %param.18), channel_id=1, source_target_pairs={{0,0},{1,4},{2,8},{3,12},{4,1},{5,5},{6,9},{7,13},{8,2},{9,6},{10,... | collective-permute-start | bytes 1572872 | tf_op jit(solution)/shard_map/ppermute | solution.py:742
  33.3 51.6 %copy-start.20 = (f32[128,2]{0,1:T(2,128)S(1)}, f32[128,2]{0,1:T(2,128)}, u32[]{:S(2)}) copy-start(f32[128,2]{0,1:T(2,128)} %param.23) | copy-start | bytes 3076
  33.3 51.6 %copy-start.18 = (s32[128,2]{0,1:T(2,128)S(1)}, s32[128,2]{0,1:T(2,128)}, u32[]{:S(2)}) copy-start(s32[128,2]{0,1:T(2,128)} %param.28) | copy-start | bytes 3076
  33.3 51.6 %copy-start.19 = (s32[128,2]{0,1:T(2,128)S(1)}, s32[128,2]{0,1:T(2,128)}, u32[]{:S(2)}) copy-start(s32[128,2]{0,1:T(2,128)} %param.27) | copy-start | bytes 3076
  84.9 8.1 copy-start.21
  85.0 47.2 %copy-start.4 = (bf16[128,2048]{1,0:T(8,128)(2,1)S(1)}, bf16[128,2048]{1,0:T(8,128)(2,1)}, u32[]{:S(2)}) copy-start(bf16[128,2048]{1,0:T(8,128)(2,1)} %param.29) | copy-start | bytes 1572868
  92.9 691.8 %reduce-scatter.3.cloned.1.call-start = ((), (), s32[]{:S(2)}) async-start(), calls=%async_computation.4 | async-start | bytes 2621440 | tf_op jit(solution)/shard_map/reduce_scatter | solution.py:922
  93.0 41.4 %copy-start.14 = (f32[128]{0:T(128)}, f32[128]{0:T(128)S(1)}, u32[]{:S(2)}) copy-start(f32[128]{0:T(128)S(1)} %get-tuple-element.50) | copy-start | bytes 1540
  93.0 41.4 %copy-start.16 = (f32[128]{0:T(128)}, f32[128]{0:T(128)S(1)}, u32[]{:S(2)}) copy-start(f32[128]{0:T(128)S(1)} %get-tuple-element.51) | copy-start | bytes 1540
  235.2 53.9 %copy-start.3 = (bf16[128,2048]{1,0:T(8,128)(2,1)S(1)}, bf16[128,2048]{1,0:T(8,128)(2,1)}, u32[]{:S(2)}) copy-start(bf16[128,2048]{1,0:T(8,128)(2,1)} %param.15) | copy-start | bytes 1572868
  400.1 14.4 %copy-start.8 = (bf16[1280,1408]{1,0:T(8,128)(2,1)S(1)}, bf16[1280,1408]{1,0:T(8,128)(2,1)}, u32[]{:S(2)}) copy-start(bf16[1280,1408]{1,0:T(8,128)(2,1)} %get-tuple-element.45.refs_3_) | copy-start | bytes 10813444
  583.1 218.9 %reduce-scatter.5.cloned.1.call-start = ((), (), s32[]{:S(2)}) async-start(), calls=%async_computation.5 | async-start | bytes 4718592 | tf_op jit(solution)/shard_map/reduce_scatter | solution.py:913
  715.8 64.6 %copy-start.17 = (f32[128]{0:T(128)S(1)}, f32[128]{0:T(128)}, u32[]{:S(2)}) copy-start(f32[128]{0:T(128)} %copy-done.16) | copy-start | bytes 1540
  715.8 66.4 %copy-start.15 = (f32[128]{0:T(128)S(1)}, f32[128]{0:T(128)}, u32[]{:S(2)}) copy-start(f32[128]{0:T(128)} %copy-done.14) | copy-start | bytes 1540
  780.2 4.5 copy-start.11
  780.2 4.5 copy-start.13
  784.8 21.3 %copy-start.2 = (f32[128,2048]{1,0:T(8,128)S(1)}, f32[128,2048]{1,0:T(8,128)}, u32[]{:S(2)}) copy-start(f32[128,2048]{1,0:T(8,128)} %copy-done.1) | copy-start | bytes 3145732
  801.9 16.8 %copy-start.7 = (f32[2048,512]{1,0:T(8,128)S(1)}, f32[2048,512]{1,0:T(8,128)}, u32[]{:S(2)}) copy-start(f32[2048,512]{1,0:T(8,128)} %get-tuple-element.33) | copy-start | bytes 12582916
  801.9 15.7 %collective-permute-start.1 = (bf16[2048,128]{1,0:T(8,128)(2,1)}, bf16[2048,128]{1,0:T(8,128)(2,1)S(1)}, u32[]{:S(2)}, u32[]{:S(2)}) collective-permute-start(bf16[2048,128]{1,0:T(8,128)(2,1)} %bitcast.137), channel_id=1, source_target_pairs={{0,0},{4,1},{8,2},{12,3},{1,4},{5,5},{9,6},{13,7},{2,8},{6,9},{10,... | collective-permute-start | bytes 1572872 | tf_op jit(solution)/shard_map/ppermute | solution.py:914
  (4 other events, 8.8 us)
Sparse Core Ops, SparseCore 0:
  25.7 39.5 all-gather.2
  93.1 90.9 all-gather.4
  583.2 45.5 reduce-scatter.2
  632.9 145.8 reduce-scatter.4

commit v4 on v3

--- a/solution.py
+++ b/solution.py
@@ -241,50 +241,243 @@
     )
 
 
-def product_job(a, b, dtype):
-    rows, width = a.shape[0], b.shape[1]
-
-    def body(a_hbm, b_hbm, out, a_ref, b_ref, held, load_sem, sem):
-        loads = fetch(((a_hbm, a_ref), (b_hbm, b_ref)), load_sem)
+def split_job(weight):
+    rows, _, width = weight.shape
+
+    def body(w_hbm, first, second, block, wide, held, load_sem, sem):
+        flat = wide.reshape(2 * STEP, 128)
+        steps = rows // STEP
+
+        def load(i):
+            return pltpu.make_async_copy(
+                w_hbm.at[pl.ds(i * STEP, STEP)], block.at[i % 2], load_sem.at[i % 2]
+            )
+
+        load(0).start()
+        yield
+        copies = []
+        for i in range(steps):
+            slot = i % 2
+            if i + 1 < steps:
+                load(i + 1).start()
+            load(i).wait()
+            if i >= 2:
+                for copy in copies[i - 2]:
+                    copy.wait()
+
+            def tile(c, carry, slot=slot):
+                at = pl.ds(pl.multiple_of(c * 128, 128), 128)
+                wide[...] = block[slot, :, :, at].astype(f32)
+                for j in range(2):
+                    held[slot, j, :, at] = flat[pl.ds(j, STEP, stride=2), :].astype(bf16)
+                return carry
+
+            lax.fori_loop(0, width // 128, tile, 0)
+            copies.append(
+                [
+                    pltpu.make_async_copy(
+                        held.at[slot, j], out.at[pl.ds(i * STEP, STEP)], sem.at[slot, j]
+                    )
+                    for j, out in enumerate((first, second))
+                ]
+            )
+            for copy in copies[i]:
+                copy.start()
+            yield
+        for copy in copies[-2] + copies[-1]:
+            copy.wait()
+
+    return Job(
+        [weight],
+        [jax.ShapeDtypeStruct((rows, width), bf16)] * 2,
+        [
+            pltpu.VMEM((2, STEP, 2, width), bf16),
+            pltpu.VMEM((STEP, 2, 128), f32),
+            pltpu.VMEM((2, 2, STEP, width), bf16),
+            DMA((2,)),
+            DMA((2, 2)),
+        ],
+        rows // STEP,
+        body,
+    )
+
+
+def ffn_job(x, gate_weight, up_weight, down_weight):
+    rows, width = x.shape
+    hidden = gate_weight.shape[1]
+
+    def body(
+        x_hbm, g_hbm, u_hbm, d_hbm, gate_out, up_out, act_out, out, x_ref, g_ref, u_ref, d_ref, pre, act, res,
+        load_sem, sem
+    ):
+        loads = fetch(((x_hbm, x_ref), (g_hbm, g_ref), (u_hbm, u_ref), (d_hbm, d_ref)), load_sem)
         yield
         for load in loads:
             load.wait()
         copies = []
         for i, (start, size) in enumerate(blocks_of(rows)):
+            slot = i % 2
+            here = pl.ds(start, size)
             if i >= 2:
-                copies[i - 2].wait()
-
-            def tile(at, columns, slot=i % 2, start=start, size=size):
-                held[slot, :size, pl.ds(at, columns)] = jnp.dot(
-                    a_ref[start : start + size],
-                    b_ref[:, pl.ds(at, columns)],
-                    preferred_element_type=f32,
-                ).astype(dtype)
-
-            column_tiles(width, tile)
+                for copy in copies[i - 2]:
+                    copy.wait()
+
+            def tile(at, columns, slot=slot, start=start, size=size):
+                part = pl.ds(at, columns)
+                left = x_ref[start : start + size]
+                gate = dot(left, g_ref[:, part])
+                up = dot(left, u_ref[:, part])
+                pre[slot, 0, :, part] = gate
+                pre[slot, 1, :, part] = up
+                act[slot, :, part] = (gate * jax.nn.sigmoid(gate) * up).astype(bf16)
+
+            column_tiles(hidden, tile)
+            yield
+
+            def last(at, columns, slot=slot):
+                part = pl.ds(at, columns)
+                res[slot, :, part] = dot(act[slot], d_ref[:, part]).astype(bf16)
+
+            column_tiles(width, last)
             copies.append(
-                pltpu.make_async_copy(
-                    held.at[i % 2, pl.ds(0, size)], out.at[pl.ds(start, size)], sem.at[i % 2]
-                )
+                [
+                    pltpu.make_async_copy(src.at[slot], dst.at[here], sem.at[slot, k])
+                    for k, (src, dst) in enumerate(((act, act_out), (res, out)))
+                ]
+                + [
+                    pltpu.make_async_copy(pre.at[slot, k], dst.at[here], sem.at[slot, 2 + k])
+                    for k, dst in enumerate((gate_out, up_out))
+                ]
             )
-            copies[i].start()
+            for copy in copies[i]:
+                copy.start()
             yield
-        for copy in copies[-2:]:
+        for copy in copies[-2] + copies[-1]:
             copy.wait()
 
     return Job(
-        [a, b],
-        [jax.ShapeDtypeStruct((rows, width), dtype)],
+        [x, gate_weight, up_weight, down_weight],
+        [jax.ShapeDtypeStruct((rows, hidden), f32)] * 2
+        + [jax.ShapeDtypeStruct((rows, hidden), bf16), jax.ShapeDtypeStruct((rows, width), bf16)],
         [
-            pltpu.VMEM(a.shape, bf16),
-            pltpu.VMEM(b.shape, bf16),
-            pltpu.VMEM((2, STEP, width), dtype),
-            DMA((2,)),
-            DMA((2,)),
+            pltpu.VMEM(x.shape, bf16),
+            pltpu.VMEM(gate_weight.shape, bf16),
+            pltpu.VMEM(up_weight.shape, bf16),
+            pltpu.VMEM(down_weight.shape, bf16),
+            pltpu.VMEM((2, 2, STEP, hidden), f32),
+            pltpu.VMEM((2, STEP, hidden), bf16),
+            pltpu.VMEM((2, STEP, width), bf16),
+            DMA((4,)),
+            DMA((2, 4)),
         ],
-        len(blocks_of(rows)),
+        2 * (rows // STEP),
         body,
     )
+
+
+def ffn_plain(x, gate_weight, up_weight, down_weight):
+    gate_pre, up_pre = dot(x, gate_weight), dot(x, up_weight)
+    activated = (gate_pre * jax.nn.sigmoid(gate_pre) * up_pre).astype(bf16)
+    return gate_pre, up_pre, activated, dot(activated, down_weight).astype(bf16)
+
+
+def before_activation(grad_act, gate_pre, up_pre):
+    sigmoid_gate = jax.nn.sigmoid(gate_pre)
+    grad_up = (grad_act * gate_pre * sigmoid_gate).astype(bf16)
+    grad_gate = (
+        grad_act * up_pre * sigmoid_gate * (1.0 + gate_pre * (1.0 - sigmoid_gate))
+    ).astype(bf16)
+    return grad_gate, grad_up
+
+
+def ffn_back_job(grad, gate_pre, up_pre, gate_weight, up_weight, down_weight):
+    rows, width = grad.shape
+    hidden = gate_weight.shape[1]
+
+    def body(
+        x_hbm, gp_hbm, up_hbm, g_hbm, u_hbm, d_hbm, gate_out, up_out, out, x_ref, g_ref, u_ref, d_ref, pre, hid,
+        res, load_sem, pre_sem, sem
+    ):
+        loads = fetch(((x_hbm, x_ref), (g_hbm, g_ref), (u_hbm, u_ref), (d_hbm, d_ref)), load_sem)
+
+        def load_pre(i):
+            here = pl.ds(i * STEP, STEP)
+            return [
+                pltpu.make_async_copy(src.at[here], pre.at[i % 2, k], pre_sem.at[i % 2, k])
+                for k, src in enumerate((gp_hbm, up_hbm))
+            ]
+
+        for copy in load_pre(0):
+            copy.start()
+        yield
+        for load in loads:
+            load.wait()
+        copies = []
+        steps = rows // STEP
+        for i in range(steps):
+            slot, start = i % 2, i * STEP
+            here = pl.ds(start, STEP)
+            if i + 1 < steps:
+                for copy in load_pre(i + 1):
+                    copy.start()
+            for copy in load_pre(i):
+                copy.wait()
+            if i >= 2:
+                for copy in copies[i - 2]:
+                    copy.wait()
+
+            def tile(at, columns, slot=slot, start=start):
+                part = pl.ds(at, columns)
+                grad_act = dot_t(x_ref[start : start + STEP], d_ref[part, :])
+                pair = before_activation(grad_act, pre[slot, 0, :, part], pre[slot, 1, :, part])
+                hid[slot, 0, :, part], hid[slot, 1, :, part] = pair
+
+            column_tiles(hidden, tile)
+            yield
+
+            def last(at, columns, slot=slot):
+                part = pl.ds(at, columns)
+                total = dot_t(hid[slot, 0], g_ref[part, :]) + dot_t(hid[slot, 1], u_ref[part, :])
+                res[slot, :, part] = total.astype(bf16)
+
+            column_tiles(width, last)
+            copies.append(
+                [pltpu.make_async_copy(res.at[slot], out.at[here], sem.at[slot, 2])]
+                + [
+                    pltpu.make_async_copy(hid.at[slot, k], dst.at[here], sem.at[slot, k])
+                    for k, dst in enumerate((gate_out, up_out))
+                ]
+            )
+            for copy in copies[i]:
+                copy.start()
+            yield
+        for copy in copies[-2] + copies[-1]:
+            copy.wait()
+
+    return Job(
+        [grad, gate_pre, up_pre, gate_weight, up_weight, down_weight],
+        [jax.ShapeDtypeStruct((rows, hidden), bf16)] * 2 + [jax.ShapeDtypeStruct((rows, width), bf16)],
+        [
+            pltpu.VMEM(grad.shape, bf16),
+            pltpu.VMEM(gate_weight.shape, bf16),
+            pltpu.VMEM(up_weight.shape, bf16),
+            pltpu.VMEM(down_weight.shape, bf16),
+            pltpu.VMEM((2, 2, STEP, hidden), f32),
+            pltpu.VMEM((2, 2, STEP, hidden), bf16),
+            pltpu.VMEM((2, STEP, width), bf16),
+            DMA((4,)),
+            DMA((2, 2)),
+            DMA((2, 3)),
+        ],
+        2 * (rows // STEP),
+        body,
+    )
+
+
+def ffn_back_plain(grad, gate_pre, up_pre, gate_weight, up_weight, down_weight):
+    grad_gate, grad_up = before_activation(dot_t(grad, down_weight), gate_pre, up_pre)
+    back = dot_t(grad_gate, gate_weight) + dot_t(grad_up, up_weight)
+    return grad_gate, grad_up, back.astype(bf16)
 
 
 def dispatch_job(rows, n_ws):
@@ -623,15 +816,17 @@
 
 
 PLAIN = {
-    grad_job: t_dot,
-    pair_grad_job: lambda a, b, c: jnp.stack([t_dot(a, b), t_dot(a, c)], 1),
-    product_job: lambda a, b, dtype: dot(a, b).astype(dtype),
+    grad_job: lambda a, b: [t_dot(a, b)],
+    pair_grad_job: lambda a, b, c: [jnp.stack([t_dot(a, b), t_dot(a, c)], 1)],
+    split_job: lambda weight: [weight[:, 0], weight[:, 1]],
+    ffn_job: ffn_plain,
+    ffn_back_job: ffn_back_plain,
 }
 
 
 def beside(job, plain, arg, fills, collective_id, name):
     if job is None:
-        return [plain(arg)] + [PLAIN[make](*rest) for make, *rest in fills]
+        return [plain(arg)] + [out for make, *rest in fills for out in PLAIN[make](*rest)]
     return run_jobs(job(arg), [make(*rest) for make, *rest in fills], collective_id, name)
 
 
@@ -756,7 +951,13 @@
     ffn_tokens = ffn_pairs[0] + ffn_pairs[1]
 
     normed_sequence = lax.all_gather(normed, "ws", axis=0, tiled=True)
-    rows_one = dispatch(dot(attn_tokens, normed).astype(bf16), group)[0]
+    rows_one, gate_weight, up_weight = dispatch(
+        dot(attn_tokens, normed).astype(bf16),
+        group,
+        (split_job, w_in[0]),
+        collective_id=10,
+        name="dispatch_split",
+    )
     kv = dot(normed_sequence, kv_own).astype(bf16)
     keys = kv[:, :own_width].reshape(sequence, -1, HEAD_SIZE)
     values = kv[:, own_width:].reshape(sequence, -1, HEAD_SIZE)
@@ -802,7 +1003,7 @@
             mixed_pieces.append(mixed.astype(bf16))
         mixed = to_experts(mixed_pieces)
     owner_mixed = exchange(mixed)[0].reshape(-1, part)
-    attn_slots = combine(dot(owner_mixed, w_output[0]).astype(bf16), group, n_ep, n_ws)[0]
+    attn_slots = combine(dot(owner_mixed, w_output[0]).astype(bf16), group, n_ep, n_ws, collective_id=11)[0]
 
     def weighted(pairs, gates, slot_values):
         return sum(gates[:, k : k + 1] * t_dot(pairs[k], slot_values) for k in range(2))
@@ -819,34 +1020,32 @@
 
     grad_out = cotangent.astype(f32)
     grad_slots = to_slots(ffn_pairs, gate_ffn, grad_out)
-    gate_weight, up_weight = w_in[0, :, 0], w_in[0, :, 1]
     expert_rows = dispatch(dot(ffn_tokens, normed_two).astype(bf16), group)[0]
-    expert_grad, gate_pre, up_pre = dispatch(
+    expert_grad, gate_pre, up_pre, activated, forward_part = dispatch(
         grad_slots,
         group,
-        (product_job, expert_rows, gate_weight, f32),
-        (product_job, expert_rows, up_weight, f32),
+        (ffn_job, expert_rows, gate_weight, up_weight, w_out[0]),
         collective_id=5,
-        name="dispatch_ffn_in",
-    )
-    sigmoid_gate = jax.nn.sigmoid(gate_pre)
-    silu_gate = gate_pre * sigmoid_gate
-    activated = (silu_gate * up_pre).astype(bf16)
-    grad_act = dot_t(expert_grad, w_out[0])
-    grad_up = (grad_act * silu_gate).astype(bf16)
-    grad_gate = (
-        grad_act * up_pre * sigmoid_gate * (1.0 + gate_pre * (1.0 - sigmoid_gate))
-    ).astype(bf16)
-    back_two = (dot_t(grad_gate, gate_weight) + dot_t(grad_up, up_weight)).astype(bf16)
-    back_slots, forward_part, grad_second = combine(
+        name="dispatch_ffn",
+    )
+    ffn_slots, grad_gate, grad_up, back_two = combine(
+        forward_part,
+        group,
+        n_ep,
+        n_ws,
+        (ffn_back_job, expert_grad, gate_pre, up_pre, gate_weight, up_weight, w_out[0]),
+        collective_id=1,
+        name="combine_ffn_back",
+    )
+    result = hidden_state + weighted(ffn_pairs, gate_ffn, ffn_slots)
+    back_slots, grad_second = combine(
         back_two,
         group,
         n_ep,
         n_ws,
-        (product_job, activated, w_out[0], bf16),
         (grad_job, activated, expert_grad),
         collective_id=6,
-        name="combine_ffn_out",
+        name="combine_grad_out",
     )
 
     grad_normed_two = t_dot(ffn_tokens, back_slots)
@@ -904,8 +1103,6 @@
         collective_id=9,
         name="combine_grad_query",
     )
-    ffn_slots = combine(forward_part, group, n_ep, n_ws)[0]
-    result = hidden_state + weighted(ffn_pairs, gate_ffn, ffn_slots)
 
     grad_kv = t_dot(normed_sequence, grad_kv_rows)
     if plain:

time: 865 us -> 799 us (0.924)
  matrix products: 116 us -> 60.9 us
  waiting for transfers between devices: 23.2 us -> 64.8 us
  local copies, waits for them, and re-layouts: 78.5 us -> 44.9 us
  Pallas kernels: 607 us -> 585 us
    dot_general x6 -> x3, matrix products: 68 us -> 18.6 us  [dot_t(): lax.dot_general(a, b, (((1,), (1,)), ((), ())), preferred_element_type=f32)]
    reduce_scatter x1, waiting for transfers between devices: 0.01 us -> 24.4 us  [local(): piece = lax.psum_scatter(pieces, 'ep', scatter_dimension=0, tiled=False)]
    slice x1 -> x0, local copies, waits for them, and re-layouts: 22.7 us -> none  [local(): gate_weight, up_weight = (w_in[0, :, 0], w_in[0, :, 1])]
    pallas_call x12, Pallas kernels: 552 us -> 533 us  [run_jobs(): pl.pallas_call(kernel, out_shape=outs, in_specs=[ANY] * len(args), out_sp...]
    ppermute x1, waiting for transfers between devices: 0.01 us -> 12.9 us  [local(): mine = lax.ppermute(key_value_weight, ('ep', 'ws'), there)]
    squeeze x1 -> x0, local copies, waits for them, and re-layouts: 12.5 us -> none  [local(): gate_weight, up_weight = (w_in[0, :, 0], w_in[0, :, 1])]
    unnamed x48 -> x50, local copies, waits for them, and re-layouts: 33.6 us -> 35.2 us
  transfers between devices with their start and end apart: 6 -> 6, of which waited for: 2 -> 4; matrix products, arithmetic and copies ran while one was open for 9% -> 5% of each run, Pallas kernels for 33% -> 25%
where the time goes in v4:
time: 799 us; the launch traced here: 788 us
  Pallas kernels  585 us (73%)
  waiting for transfers between devices  64.8 us (8%)
  matrix products  60.9 us (8%)
  local copies, waits for them, and re-layouts  44.9 us (6%)
  between operations  14.7 us (2%)
  other arithmetic  8.95 us (1%)
  starting transfers between devices  8.54 us (1%)
    pallas_call x12, Pallas kernels, run_jobs(): pl.pallas_call(kernel, out_shape=outs, in_specs=[ANY] * len(args), out_sp...  533 us
    unnamed x50, local copies, waits for them, and re-layouts  35.2 us
    dot_general x9, matrix products, dot(): return jnp.dot(a, b, preferred_element_type=f32)  28 us
    reduce_scatter x1, waiting for transfers between devices, local(): piece = lax.psum_scatter(pieces, 'ep', scatter_dimension=0, tiled=False)  24.4 us
    dot_general x3, matrix products, dot_t(): lax.dot_general(a, b, (((1,), (1,)), ((), ())), preferred_element_type=f32)  18.6 us
    pallas_call x1, Pallas kernels, attend_back_call(): pl.pallas_call(functools.partial(attend_back_kernel, spans), out_shape=[j...  18.4 us
    all_gather x1, waiting for transfers between devices, local(): kv_own = lax.all_gather(mine, 'ep', axis=1, tiled=True)  17.6 us
  transfers between devices with their start and end apart: 6, of which 4 were waited for; matrix products, arithmetic and copies ran while one was open for 5% of the time, Pallas kernels for 25%

profile of v4, /device:TPU:1, one launch (start us, length us, event | category | flops | bytes accessed | tf_op | source)
XLA Modules:
  0.0 787.5 jit_solution(7522314911739533304)
XLA Ops:
  8.7 11.4 %gather_gains.1 = f32[8,4,1,128]{3,2,1,0:T(1,128)} custom-call(f32[1,128]{1,0:T(1,128)} %maximum_convert_fusion.own), custom_call_target="tpu_custom_call" | custom-call | tf_op jit(solution)/shard_map/gather_gains/pallas_call | solution.py:756
  30.1 12.9 %collective-permute-done = bf16[2048,128]{1,0:T(8,128)(2,1)S(1)} collective-permute-done((bf16[2048,128]{1,0:T(8,128)(2,1)S(1)}, bf16[2048,128]{1,0:T(8,128)(2,1)S(1)}, u32[]{:S(2)}, u32[]{:S(2)}) %collective-permute-start) | collective-permute-done | bytes 524320 | tf_op jit(solution)/shard_map/ppermute | solution.py:937
  46.4 43.2 %dispatch_split.1 = (bf16[8,4,40,2048]{3,2,1,0:T(8,128)(2,1)}, bf16[2048,1408]{1,0:T(8,128)(2,1)}, bf16[2048,1408]{1,0:T(8,128)(2,1)}) custom-call(bf16[8,40,2048]{2,1,0:T(8,128)(2,1)} %bitcast.101, bf16[2048,2,1408]{2,1,0:T(2,128)(2,1)} %bitcast.96), custom_call_target="tpu_custom_call" | custom-call | tf_op jit(solution)/shard_map/dispatch_split/pallas_call | solution.py:101
  89.6 7.1 convolution_convert_fusion.5
  96.7 50.5 %exchange.3 = bf16[8,160,512]{2,1,0:T(8,128)(2,1)} custom-call(bf16[8,160,512]{2,1,0:T(8,128)(2,1)} %bitcast.124), custom_call_target="tpu_custom_call" | custom-call | tf_op jit(solution)/shard_map/exchange/pallas_call | solution.py:101
  149.6 17.6 %all-gather.5.cloned.1.call-done = bf16[2048,1024]{1,0:T(8,128)(2,1)} async-done(((bf16[2048,128]{1,0:T(8,128)(2,1)}), bf16[2048,1024]{1,0:T(8,128)(2,1)}) %all-gather.5.cloned.1.call-update) | async-done | bytes 4194320 | tf_op jit(solution)/shard_map/all_gather | solution.py:938
  173.4 13.2 %attend.1 = bf16[8,4,40,512]{3,2,1,0:T(8,128)(2,1)} custom-call(bf16[8,4,40,512]{3,2,1,0:T(8,128)(2,1)} %bitcast.92, bf16[512,1024]{1,0:T(8,128)(2,1)} %convolution_convert_fusion.8.kv_ref), custom_call_target="tpu_custom_call" | custom-call | tf_op jit(solution)/shard_map/attend/pallas_call | solution.py:684
  186.6 26.3 %exchange.4 = bf16[8,160,512]{2,1,0:T(8,128)(2,1)} custom-call(bf16[8,160,512]{2,1,0:T(8,128)(2,1)} %bitcast.102), custom_call_target="tpu_custom_call" | custom-call | tf_op jit(solution)/shard_map/exchange/pallas_call | solution.py:101
  219.0 52.5 %combine.1 = bf16[8,40,2048]{2,1,0:T(8,128)(2,1)} custom-call(bf16[8,4,40,2048]{3,2,1,0:T(8,128)(2,1)} %bitcast.106), custom_call_target="tpu_custom_call" | custom-call | tf_op jit(solution)/shard_map/combine/pallas_call | solution.py:101
  275.8 39.2 %dispatch.1 = bf16[8,4,40,2048]{3,2,1,0:T(8,128)(2,1)} custom-call(bf16[8,40,2048]{2,1,0:T(8,128)(2,1)} %bitcast.111), custom_call_target="tpu_custom_call" | custom-call | tf_op jit(solution)/shard_map/dispatch/pallas_call | solution.py:101
  315.0 56.4 %dispatch_ffn.1 = (bf16[8,4,40,2048]{3,2,1,0:T(8,128)(2,1)}, f32[1280,1408]{1,0:T(8,128)}, f32[1280,1408]{1,0:T(8,128)}, bf16[1280,1408]{1,0:T(8,128)(2,1)}, bf16[1280,2048]{1,0:T(8,128)(2,1)}) custom-call(bf16[8,40,2048]{2,1,0:T(8,128)(2,1)} %bitcast.98, bf16[1280,2048]{1,0:T(8,128)(2,1)} %bitcast.84, bf16[2048,1408]{1,0:T(8,128)(2,1)} %get-tuple-element.32.refs_2_.refs_4_, ...), custom_call_target="tpu_custom_call" | custom-call | tf_op jit(solution)/shard_map/dispatch_ffn/pallas_call | solution.py:101
  371.4 52.7 %combine_ffn_back.1 = (bf16[8,40,2048]{2,1,0:T(8,128)(2,1)}, bf16[1280,1408]{1,0:T(8,128)(2,1)}, bf16[1280,1408]{1,0:T(8,128)(2,1)}, bf16[1280,2048]{1,0:T(8,128)(2,1)}) custom-call(bf16[8,4,40,2048]{3,2,1,0:T(8,128)(2,1)} %bitcast.100, bf16[1280,2048]{1,0:T(8,128)(2,1)} %bitcast.89, f32[1280,1408]{1,0:T(8,128)} %get-tuple-element.36.refs_2_, ...), custom_call_target="tpu_custom_call" | custom-call | tf_op jit(solution)/shard_map/combine_ffn_back/pallas_call | solution.py:101
  424.1 48.0 %combine_grad_out.1 = (bf16[8,40,2048]{2,1,0:T(8,128)(2,1)}, f32[1408,2048]{1,0:T(8,128)}) custom-call(bf16[8,4,40,2048]{3,2,1,0:T(8,128)(2,1)} %bitcast.99, bf16[1280,1408]{1,0:T(8,128)(2,1)} %get-tuple-element.40.refs_1_, bf16[1280,2048]{1,0:T(8,128)(2,1)} %bitcast.90), custom_call_target="tpu_custom_call" | custom-call | tf_op jit(solution)/shard_map/combine_grad_out/pallas_call | solution.py:101
  476.7 42.5 %dispatch_grad_in.1 = (bf16[8,4,40,2048]{3,2,1,0:T(8,128)(2,1)}, f32[2048,2,1408]{2,1,0:T(2,128)}) custom-call(bf16[8,40,2048]{2,1,0:T(8,128)(2,1)} %bitcast.116, bf16[1280,2048]{1,0:T(8,128)(2,1)} %bitcast.85, bf16[1280,1408]{1,0:T(8,128)(2,1)} %get-tuple-element.42.refs_2_, bf16[1280,1408]{1,0:T(8,128)(2,1)} %get-tuple-element.43.refs_3_), custom_call_target="tpu_custom_call" | custom-call | tf_op jit(solution)/shard_map/dispatch_grad_in/pallas_call | solution.py:101
  525.7 25.5 %exchange_grad_output.1 = (bf16[8,160,512]{2,1,0:T(8,128)(2,1)}, f32[512,2048]{1,0:T(8,128)}) custom-call(bf16[8,160,512]{2,1,0:T(8,128)(2,1)} %bitcast.125, bf16[1280,512]{1,0:T(8,128)(2,1)} %bitcast.113, bf16[1280,2048]{1,0:T(8,128)(2,1)} %bitcast.110), custom_call_target="tpu_custom_call" | custom-call | tf_op jit(solution)/shard_map/exchange_grad_output/pallas_call | solution.py:101
  551.2 18.4 %attend_back.1 = (bf16[8,4,40,512]{3,2,1,0:T(8,128)(2,1)}, bf16[512,1024]{1,0:T(8,128)(2,1)}) custom-call(bf16[8,4,40,512]{3,2,1,0:T(8,128)(2,1)} %bitcast.93, bf16[8,4,40,512]{3,2,1,0:T(8,128)(2,1)} %bitcast.120, bf16[512,1024]{1,0:T(8,128)(2,1)} %convolution_convert_fusion.8.kv_ref), custom_call_target="tpu_custom_call" | custom-call | tf_op jit(solution)/shard_map/attend_back/pallas_call | solution.py:719
  583.0 6.7 copy.24
  589.7 31.3 %exchange.5 = bf16[8,160,512]{2,1,0:T(8,128)(2,1)} custom-call(bf16[8,160,512]{2,1,0:T(8,128)(2,1)} %bitcast.122), custom_call_target="tpu_custom_call" | custom-call | tf_op jit(solution)/shard_map/exchange/pallas_call | solution.py:101
  627.0 64.5 %combine_grad_query.1 = (bf16[8,40,2048]{2,1,0:T(8,128)(2,1)}, f32[2048,512]{1,0:T(8,128)}) custom-call(bf16[8,4,40,2048]{3,2,1,0:T(8,128)(2,1)} %bitcast.105, bf16[1280,2048]{1,0:T(8,128)(2,1)} %bitcast.104, bf16[1280,512]{1,0:T(8,128)(2,1)} %bitcast.115), custom_call_target="tpu_custom_call" | custom-call | tf_op jit(solution)/shard_map/combine_grad_query/pallas_call | solution.py:101
  696.5 9.2 %reduce_gains.1 = f32[1,128]{1,0:T(1,128)} custom-call(f32[8,4,1,128]{3,2,1,0:T(1,128)} %reshape.172.parts), custom_call_target="tpu_custom_call" | custom-call | tf_op jit(solution)/shard_map/reduce_gains/pallas_call | solution.py:795
  707.0 24.4 %reduce-scatter.5.cloned.1.call-done = bf16[1,2048,128]{2,1,0:T(8,128)(2,1)} async-done(((bf16[8,2048,128]{2,1,0:T(8,128)(2,1)}), bf16[1,2048,128]{2,1,0:T(8,128)(2,1)}) %reduce-scatter.5.cloned.1.call-update) | async-done | bytes 524304 | tf_op jit(solution)/shard_map/reduce_scatter | solution.py:1110
  736.9 9.8 %collective-permute-done.1 = bf16[2048,128]{1,0:T(8,128)(2,1)S(1)} collective-permute-done((bf16[2048,128]{1,0:T(8,128)(2,1)}, bf16[2048,128]{1,0:T(8,128)(2,1)S(1)}, u32[]{:S(2)}, u32[]{:S(2)}) %collective-permute-start.1) | collective-permute-done | bytes 524320 | tf_op jit(solution)/shard_map/ppermute | solution.py:1111
  753.4 16.3 %copy.31 = f32[1,2048,2,1408]{3,2,1,0:T(2,128)} copy(f32[1,2048,2,1408]{3,2,1,0:T(2,128)} %bitcast.88) | data formatting | bytes 46137344
  769.8 10.8 %copy.32 = f32[1,1408,2048]{2,1,0:T(8,128)} copy(f32[1,1408,2048]{2,1,0:T(8,128)} %bitcast.97) | data formatting | bytes 23068672
  (105 shorter events, 82.5 us)
Async XLA Ops:
  7.2 205.7 %copy-start = (bf16[1,512,2048]{2,1,0:T(8,128)(2,1)S(1)}, bf16[1,512,2048]{2,1,0:T(8,128)(2,1)}, u32[]{:S(2)}) copy-start(bf16[1,512,2048]{2,1,0:T(8,128)(2,1)} %param.20) | copy-start | bytes 6291460
  7.2 36.6 %copy-start.15 = (s32[128,2]{0,1:T(2,128)S(1)}, s32[128,2]{0,1:T(2,128)}, u32[]{:S(2)}) copy-start(s32[128,2]{0,1:T(2,128)} %param.25) | copy-start | bytes 3076
  7.2 36.6 %copy-start.14 = (s32[128,2]{0,1:T(2,128)S(1)}, s32[128,2]{0,1:T(2,128)}, u32[]{:S(2)}) copy-start(s32[128,2]{0,1:T(2,128)} %param.26) | copy-start | bytes 3076
  7.2 142.4 %all-gather.3.cloned.1.call-start = ((), (), s32[]{:S(2)}) async-start(), calls=%async_computation.2 | async-start | bytes 2621440 | tf_op jit(solution)/shard_map/all_gather | solution.py:953
  22.3 3.4 copy-start.22
  25.6 141.6 %all-gather.5.cloned.1.call-start = ((), (), s32[]{:S(2)}) async-start(), calls=%async_computation.3 | async-start | bytes 4718592 | tf_op jit(solution)/shard_map/all_gather | solution.py:938
  25.7 17.2 %collective-permute-start = (bf16[2048,128]{1,0:T(8,128)(2,1)S(1)}, bf16[2048,128]{1,0:T(8,128)(2,1)S(1)}, u32[]{:S(2)}, u32[]{:S(2)}) collective-permute-start(bf16[2048,128]{1,0:T(8,128)(2,1)S(1)} %copy-done.22), channel_id=1, source_target_pairs={{0,0},{1,4},{2,8},{3,12},{4,1},{5,5},{6,9},{7,13},{8,2},{9,6},{10,... | collective-permute-start | bytes 1572872 | tf_op jit(solution)/shard_map/ppermute | solution.py:937
  43.8 649.6 %reduce-scatter.3.cloned.1.call-start = ((), (), s32[]{:S(2)}) async-start(), calls=%async_computation.4 | async-start | bytes 2621440 | tf_op jit(solution)/shard_map/reduce_scatter | solution.py:1119
  96.7 50.6 %copy-start.18 = (f32[128,2]{0,1:T(2,128)S(1)}, f32[128,2]{0,1:T(2,128)}, u32[]{:S(2)}) copy-start(f32[128,2]{0,1:T(2,128)} %param.23) | copy-start | bytes 3076
  96.7 50.6 %copy-start.16 = (s32[128,2]{0,1:T(2,128)S(1)}, s32[128,2]{0,1:T(2,128)}, u32[]{:S(2)}) copy-start(s32[128,2]{0,1:T(2,128)} %param.28) | copy-start | bytes 3076
  96.7 50.6 %copy-start.17 = (s32[128,2]{0,1:T(2,128)S(1)}, s32[128,2]{0,1:T(2,128)}, u32[]{:S(2)}) copy-start(s32[128,2]{0,1:T(2,128)} %param.27) | copy-start | bytes 3076
  96.7 50.6 %copy-start.19 = (f32[128,2]{0,1:T(2,128)S(1)}, f32[128,2]{0,1:T(2,128)}, u32[]{:S(2)}) copy-start(f32[128,2]{0,1:T(2,128)} %param.24) | copy-start | bytes 3076
  96.7 50.7 %copy-start.8 = (bf16[128,2048]{1,0:T(8,128)(2,1)S(1)}, bf16[128,2048]{1,0:T(8,128)(2,1)}, u32[]{:S(2)}) copy-start(bf16[128,2048]{1,0:T(8,128)(2,1)} %param.29) | copy-start | bytes 1572868
  472.1 2.0 copy-start.9
  474.5 2.2 copy-start.2
  575.8 155.7 %reduce-scatter.5.cloned.1.call-start = ((), (), s32[]{:S(2)}) async-start(), calls=%async_computation.5 | async-start | bytes 4718592 | tf_op jit(solution)/shard_map/reduce_scatter | solution.py:1110
  589.7 31.4 %copy-start.20 = (bf16[1,2048,512]{2,1,0:T(8,128)(2,1)S(1)}, bf16[1,2048,512]{2,1,0:T(8,128)(2,1)}, u32[]{:S(2)}) copy-start(bf16[1,2048,512]{2,1,0:T(8,128)(2,1)} %param.19) | copy-start | bytes 6291460
  627.0 64.5 %copy-start.7 = (bf16[8,40,2048]{2,1,0:T(8,128)(2,1)S(1)}, bf16[8,40,2048]{2,1,0:T(8,128)(2,1)}, u32[]{:S(2)}) copy-start(bf16[8,40,2048]{2,1,0:T(8,128)(2,1)} %get-tuple-element.38) | copy-start | bytes 3932164
  693.3 42.1 %copy-start.3 = (f32[128,2048]{1,0:T(8,128)S(1)}, f32[128,2048]{1,0:T(8,128)}, u32[]{:S(2)}) copy-start(f32[128,2048]{1,0:T(8,128)} %copy-done.2) | copy-start | bytes 3145732
  693.3 42.1 %copy-start.12 = (bf16[128,2048]{1,0:T(8,128)(2,1)S(1)}, bf16[128,2048]{1,0:T(8,128)(2,1)}, u32[]{:S(2)}) copy-start(bf16[128,2048]{1,0:T(8,128)(2,1)} %reduce-scatter.3.cloned.1.call-done) | copy-start | bytes 1572868
  731.4 15.3 %collective-permute-start.1 = (bf16[2048,128]{1,0:T(8,128)(2,1)}, bf16[2048,128]{1,0:T(8,128)(2,1)S(1)}, u32[]{:S(2)}, u32[]{:S(2)}) collective-permute-start(bf16[2048,128]{1,0:T(8,128)(2,1)} %bitcast.126), channel_id=1, source_target_pairs={{0,0},{4,1},{8,2},{12,3},{1,4},{5,5},{9,6},{13,7},{2,8},{6,9},{10,... | collective-permute-start | bytes 1572872 | tf_op jit(solution)/shard_map/ppermute | solution.py:1111
  735.5 12.3 %copy-start.11 = (f32[2048,512]{1,0:T(8,128)S(1)}, f32[2048,512]{1,0:T(8,128)}, u32[]{:S(2)}) copy-start(f32[2048,512]{1,0:T(8,128)} %get-tuple-element.49) | copy-start | bytes 12582916
  747.7 3.7 copy-start.10
  769.8 10.8 %copy-start.1 = (bf16[1,512,2048]{2,1,0:T(8,128)(2,1)S(1)}, bf16[1,512,2048]{2,1,0:T(8,128)(2,1)}, u32[]{:S(2)}) copy-start(bf16[1,512,2048]{2,1,0:T(8,128)(2,1)} %param.20) | copy-start | bytes 6291460
  (5 other events, 7.6 us)
Sparse Core Ops, SparseCore 0:
  25.8 30.9 all-gather.2
  59.4 107.8 all-gather.4
  575.9 36.2 reduce-scatter.2
  616.2 115.1 reduce-scatter.4

commit v5 on v4

--- a/solution.py
+++ b/solution.py
@@ -66,35 +66,41 @@
 
 
 class Job:
-    def __init__(self, args, outs, scratch, steps, body):
+    def __init__(self, args, outs, scratch, steps, body, partners=()):
         self.args, self.outs, self.scratch, self.steps, self.body = args, outs, scratch, steps, body
-
-
-def run_jobs(exchange_job, fills, collective_id, name):
-    jobs = [exchange_job] + fills
-    args = [a for job in jobs for a in job.args]
-    outs = [o for job in jobs for o in job.outs]
-    scratch = [x for job in jobs for x in job.scratch]
+        self.partners = partners
+
+
+def run_jobs(jobs, fills, collective_id, name):
+    whole = jobs + fills
+    args = [a for job in whole for a in job.args]
+    outs = [o for job in whole for o in job.outs]
+    scratch = [x for job in whole for x in job.scratch]
+    turns = sorted((k / job.steps, i) for i, job in enumerate(jobs) for k in range(job.steps))
+    partners = sorted({p for job in jobs for p in job.partners})
 
     def kernel(*refs):
         bodies, at = [], [0, len(args), len(args) + len(outs)]
-        for job in jobs:
+        for job in whole:
             own = []
             for k, part in enumerate((job.args, job.outs, job.scratch)):
                 own.append(refs[at[k] : at[k] + len(part)])
                 at[k] += len(part)
             bodies.append(job.body(*own[0], *own[1], *own[2]))
-        work = [bodies[k + 1] for k in range(len(fills))]
+        moves, work = bodies[: len(jobs)], bodies[len(jobs) :]
         queue = [g for g, job in zip(work, fills) for _ in range(job.steps)]
         for g in work:
             next(g)
+        e, w = lax.axis_index("ep"), lax.axis_index("ws")
+        greet([(flip(e, p), flip(w, q)) for p, q in partners])
         done = 0
-        for k, _ in enumerate(bodies[0]):
-            target = (k + 1) * len(queue) // exchange_job.steps
+        for k, (_, i) in enumerate(turns):
+            next(moves[i])
+            target = (k + 1) * len(queue) // len(turns)
             while done < target:
                 next(queue[done])
                 done += 1
-        for g in work:
+        for g in moves + work:
             for _ in g:
                 pass
 
@@ -487,7 +493,6 @@
         e, w = lax.axis_index("ep"), lax.axis_index("ws")
         twin, other = flip(w, 1), flip(w, 2)
         sources = [e] + [flip(e, k) for k in range(1, n)]
-        greet([(s, w) for s in sources[1:]] + [(e, twin), (e, other)])
         first = []
         for i, s in enumerate(sources[1:]):
             first.append(remote(rows.at[s], out.at[e, w], ep_s.at[i], ep_r.at[i], (s, w)))
@@ -532,6 +537,7 @@
         + [DMA((n,)) for _ in range(6)],
         n,
         body,
+        [(k, 0) for k in range(1, n)] + [(0, 1), (0, 2)],
     )
 
 
@@ -545,7 +551,6 @@
         e, w = lax.axis_index("ep"), lax.axis_index("ws")
         twin, other, last = flip(w, 1), flip(w, 2), flip(w, 3)
         targets = [flip(e, k) for k in far_first(n)] + [e]
-        greet([(s, w) for s in targets[:-1]] + [(e, twin), (e, other)])
         loads, cores = {}, {}
         for half, near, far in ((1, other, last), (0, w, twin)):
             for j, s in enumerate(targets):
@@ -615,6 +620,7 @@
         ],
         n,
         body,
+        [(k, 0) for k in range(1, n)] + [(0, 1), (0, 2)],
     )
 
 
@@ -624,7 +630,6 @@
     def body(rows, out, own, load_sem, ep_s, ep_r):
         e, w = lax.axis_index("ep"), lax.axis_index("ws")
         targets = [flip(e, k) for k in far_first(n)]
-        greet([(s, w) for s in targets])
         copies = []
         for i, s in enumerate(targets):
             copies.append(remote(rows.at[s], out.at[e], ep_s.at[i], ep_r.at[i], (s, w)))
@@ -645,6 +650,187 @@
         [pltpu.VMEM(rows.shape[1:], rows.dtype), DMA((2,)), DMA((n - 1,)), DMA((n - 1,))],
         1,
         body,
+        [(k, 0) for k in range(1, n)],
+    )
+
+
+def gather_weights_job(mine, normed, n, n_ws):
+    rows, block = mine.shape
+    routes = [(4, 0), (1, 0), (2, 0), (2, 4), (1, 4), (1, 2), (1, 6)]
+
+    def body(mine, normed, out, seq, held, held_rows, load_sem, s_sem, r_sem, w_s, w_r):
+        e, w = lax.axis_index("ep"), lax.axis_index("ws")
+        twin, other = flip(w, 1), flip(w, 2)
+        copies = {}
+
+        def send(hop, offset, half):
+            k = routes.index((hop, offset))
+            s = flip(e, offset)
+            part = pl.ds(half * (rows // 2), rows // 2)
+            place = out.at[part, pl.ds(pl.multiple_of(s * block, block), block)]
+            copies[hop, offset, half] = remote(
+                place if offset else mine.at[part],
+                place,
+                s_sem.at[k, half],
+                r_sem.at[k, half],
+                (flip(e, hop), w),
+            )
+            copies[hop, offset, half].start()
+
+        for half in range(2):
+            for route in routes[:3]:
+                send(*route, half)
+        over_y = remote(normed, seq.at[w], w_s.at[0], w_r.at[0], (e, other))
+        over_y.start()
+        to_twin = remote(normed, seq.at[w], w_s.at[1], w_r.at[1], (e, twin))
+        to_twin.start()
+        loads = fetch(((mine, held), (normed, held_rows)), load_sem)
+        for load in loads:
+            load.wait()
+        own = out.at[:, pl.ds(pl.multiple_of(e * block, block), block)]
+        stores = fetch(((held, own), (held_rows, seq.at[w])), load_sem)
+        yield
+        over_y.wait_recv()
+        relay = remote(seq.at[other], seq.at[other], w_s.at[2], w_r.at[2], (e, twin))
+        relay.start()
+        for arrival, onward in (
+            ((4, 0), ((2, 4), (1, 4))),
+            ((2, 0), ((1, 2),)),
+            ((2, 4), ((1, 6),)),
+        ):
+            for half in range(2):
+                copies[(*arrival, half)].wait_recv()
+                for route in onward:
+                    send(*route, half)
+                yield
+        for store in stores:
+            store.wait()
+        for (hop, offset, _), copy in copies.items():
+            copy.wait_send()
+            if hop == 1:
+                copy.wait_recv()
+        over_y.wait_send()
+        to_twin.wait()
+        relay.wait()
+
+    return Job(
+        [mine, normed],
+        [
+            jax.ShapeDtypeStruct((rows, n * block), bf16),
+            jax.ShapeDtypeStruct((n_ws,) + normed.shape, bf16),
+        ],
+        [
+            pltpu.VMEM(mine.shape, bf16),
+            pltpu.VMEM(normed.shape, bf16),
+            DMA((2,)),
+            DMA((7, 2)),
+            DMA((7, 2)),
+            DMA((3,)),
+            DMA((3,)),
+        ],
+        7,
+        body,
+        [(1, 0), (2, 0), (4, 0), (0, 1), (0, 2)],
+    )
+
+
+def add_blocks(out, *refs):
+    step = 64 if out.shape[1] > 1024 else 256
+
+    def body(i, carry):
+        at = pl.ds(pl.multiple_of(i * step, step), step)
+        total = refs[0][at].astype(f32)
+        for ref in refs[1:]:
+            total = total + ref[at].astype(f32)
+        out[at] = total.astype(bf16)
+        return carry
+
+    lax.fori_loop(0, out.shape[0] // step, body, 0)
+
+
+def reduce_weights_job(pieces, part, n):
+    rows = pieces.shape[0]
+    block = pieces.shape[1] // n
+    offsets = (6, 4, 2, 0)
+
+    def body(
+        pieces, part, out, out_rows, mine, from_x, sums, from_z, last_z, fourth, total, own, core, sum_y, from_y,
+        total_rows, load_sem, x_s, x_r, z_s, z_r, w_load, w_s, w_r, sem
+    ):
+        e, w = lax.axis_index("ep"), lax.axis_index("ws")
+        twin, other, last = flip(w, 1), flip(w, 2), flip(w, 3)
+
+        def columns(s):
+            return pieces.at[:, pl.ds(pl.multiple_of(s * block, block), block)]
+
+        across = []
+        for i, offset in enumerate(offsets):
+            across.append(
+                remote(columns(flip(e, offset + 1)), from_x.at[i], x_s.at[i], x_r.at[i], (flip(e, 1), w))
+            )
+            across[i].start()
+        cores = [
+            remote(part.at[to], core.at[k], w_s.at[k], w_r.at[k], (e, twin))
+            for k, to in enumerate((last, twin))
+        ]
+        for copy in cores:
+            copy.start()
+        loads = fetch([(columns(flip(e, o)), mine.at[i]) for i, o in enumerate(offsets)], load_sem)
+        own_loads = fetch(((part.at[other], own.at[0]), (part.at[w], own.at[1])), w_load)
+        yield
+
+        def add(i):
+            loads[i].wait()
+            across[i].wait_recv()
+            add_blocks(sums.at[i], mine.at[i], from_x.at[i])
+
+        own_loads[0].wait()
+        cores[0].wait_recv()
+        add_blocks(sum_y, own.at[0], core.at[0])
+        add(0)
+        over_y = remote(sum_y, from_y, w_s.at[2], w_r.at[2], (e, other))
+        over_y.start()
+        yield
+        add(1)
+        first = remote(sums.at[0], from_z.at[0], z_s.at[0], z_r.at[0], (flip(e, 2), w))
+        first.start()
+        yield
+        add(2)
+        first.wait_recv()
+        add_blocks(fourth, sums.at[1], from_z.at[0])
+        second = remote(sums.at[2], from_z.at[1], z_s.at[1], z_r.at[1], (flip(e, 2), w))
+        second.start()
+        yield
+        add(3)
+        third = remote(fourth, last_z, z_s.at[2], z_r.at[2], (flip(e, 4), w))
+        third.start()
+        yield
+        own_loads[1].wait()
+        cores[1].wait_recv()
+        over_y.wait_recv()
+        add_blocks(total_rows, own.at[1], core.at[1], from_y)
+        second.wait_recv()
+        third.wait_recv()
+        add_blocks(total, sums.at[3], from_z.at[1], last_z)
+        stores = fetch(((total_rows, out_rows), (total, out)), sem)
+        for copy in across + cores + [over_y, first, second, third]:
+            copy.wait_send()
+        for store in stores:
+            store.wait()
+
+    one, rows_one = (rows, block), part.shape[1:]
+    return Job(
+        [pieces, part],
+        [jax.ShapeDtypeStruct(one, bf16), jax.ShapeDtypeStruct(rows_one, bf16)],
+        [pltpu.VMEM((4,) + one, bf16) for _ in range(3)]
+        + [pltpu.VMEM((2,) + one, bf16)]
+        + [pltpu.VMEM(one, bf16) for _ in range(3)]
+        + [pltpu.VMEM((2,) + rows_one, bf16) for _ in range(2)]
+        + [pltpu.VMEM(rows_one, bf16) for _ in range(3)]
+        + [DMA((4,)), DMA((4,)), DMA((4,)), DMA((3,)), DMA((3,)), DMA((2,)), DMA((3,)), DMA((3,)), DMA((2,))],
+        5,
+        body,
+        [(1, 0), (2, 0), (4, 0), (0, 1), (0, 2)],
     )
 
 
@@ -827,7 +1013,7 @@
 def beside(job, plain, arg, fills, collective_id, name):
     if job is None:
         return [plain(arg)] + [out for make, *rest in fills for out in PLAIN[make](*rest)]
-    return run_jobs(job(arg), [make(*rest) for make, *rest in fills], collective_id, name)
+    return run_jobs([job(arg)], [make(*rest) for make, *rest in fills], collective_id, name)
 
 
 def exchange_plain(send):
@@ -918,7 +1104,8 @@
     place = lax.axis_index("ws")
     scale = HEAD_SIZE ** (-0.5)
 
-    short = small(n_ep) and gain_attn.shape[0] == 64
+    fused = small(n_ep) and key_value_weight.shape[1] == HEAD_SIZE
+    short = fused and gain_attn.shape[0] == 64
     if short:
         gains = jnp.concatenate([gain_attn, gain_ffn], 0).astype(f32)[None]
         gains = gather_call(gains, n_ep, n_ws).reshape(n_ep * n_ws, 2, -1)
@@ -935,7 +1122,6 @@
             for w in range(n_ws)
         ]
         mine = lax.ppermute(key_value_weight, ("ep", "ws"), there)
-        kv_own = lax.all_gather(mine, "ep", axis=1, tiled=True)
     else:
         whole = lax.all_gather(key_value_weight, ("ep", "ws"), axis=1, tiled=True)
         whole = whole.reshape(width, 2 * group, n_ws, part)
@@ -950,14 +1136,24 @@
     attn_tokens = attn_pairs[0] + attn_pairs[1]
     ffn_tokens = ffn_pairs[0] + ffn_pairs[1]
 
-    normed_sequence = lax.all_gather(normed, "ws", axis=0, tiled=True)
-    rows_one, gate_weight, up_weight = dispatch(
-        dot(attn_tokens, normed).astype(bf16),
-        group,
-        (split_job, w_in[0]),
-        collective_id=10,
-        name="dispatch_split",
-    )
+    slots_one = dot(attn_tokens, normed).astype(bf16)
+    if fused:
+        rows_one, kv_own, normed_sequence, gate_weight, up_weight = run_jobs(
+            [
+                dispatch_job(slots_one.reshape(n_ep, ROWS, width), n_ws),
+                gather_weights_job(mine, normed, n_ep, n_ws),
+            ],
+            [split_job(w_in[0])],
+            10,
+            "dispatch_weights",
+        )
+        rows_one = rows_one.reshape(-1, width)
+        normed_sequence = normed_sequence.reshape(sequence, width)
+    else:
+        if plain:
+            kv_own = lax.all_gather(mine, "ep", axis=1, tiled=True)
+        normed_sequence = lax.all_gather(normed, "ws", axis=0, tiled=True)
+        rows_one, gate_weight, up_weight = dispatch(slots_one, group, (split_job, w_in[0]))
     kv = dot(normed_sequence, kv_own).astype(bf16)
     keys = kv[:, :own_width].reshape(sequence, -1, HEAD_SIZE)
     values = kv[:, own_width:].reshape(sequence, -1, HEAD_SIZE)
@@ -965,7 +1161,6 @@
     owner_query = dot(rows_one, w_query[0]).astype(bf16)
     queries = exchange(owner_query.reshape(n_ep, n_ws * ROWS, part))[0]
     spans = [(w * local_tokens // BLOCK + 1) * BLOCK for w in range(n_ws)]
-    fused = small(n_ep)
     queries = queries.reshape(MIXTURE_EXPERTS, group, n_ws, ROWS, part)
 
     def by_block(rows):
@@ -1092,7 +1287,23 @@
             [grad_keys.reshape(sequence, -1), grad_values.reshape(sequence, -1)], 1
         ).astype(bf16)
         query_grads = to_experts(query_pieces)
-    owner_grad_query = exchange(query_grads)[0].reshape(-1, part)
+    grad_kv = t_dot(normed_sequence, grad_kv_rows)
+    from_kv = dot_t(grad_kv_rows, kv_own).astype(bf16)
+    if fused:
+        owner_grad_query, piece, from_kv = run_jobs(
+            [
+                exchange_job(query_grads),
+                reduce_weights_job(
+                    grad_kv.astype(bf16), from_kv.reshape(n_ws, local_tokens, width), n_ep
+                ),
+            ],
+            [],
+            12,
+            "exchange_weights",
+        )
+        owner_grad_query = owner_grad_query.reshape(-1, part)
+    else:
+        owner_grad_query = exchange(query_grads)[0].reshape(-1, part)
     back_normed = dot_t(owner_grad_query, w_query[0]).astype(bf16)
     normed_back, grad_query = combine(
         back_normed,
@@ -1104,8 +1315,10 @@
         name="combine_grad_query",
     )
 
-    grad_kv = t_dot(normed_sequence, grad_kv_rows)
-    if plain:
+    if fused:
+        back = [(b, a) for a, b in there]
+        grad_kv_shard = lax.ppermute(piece, ("ep", "ws"), back).astype(f32)
+    elif plain:
         pieces = grad_kv.reshape(width, n_ep, HEAD_SIZE).transpose(1, 0, 2).astype(bf16)
         piece = lax.psum_scatter(pieces, "ep", scatter_dimension=0, tiled=False)
         grad_kv_shard = lax.ppermute(piece, ("ep", "ws"), [(b, a) for a, b in there]).astype(f32)
@@ -1116,9 +1329,8 @@
         grad_kv_shard = lax.psum_scatter(
             pieces, ("ep", "ws"), scatter_dimension=1, tiled=True
         ).astype(f32)
-    from_kv = lax.psum_scatter(
-        dot_t(grad_kv_rows, kv_own).astype(bf16), "ws", scatter_dimension=0, tiled=True
-    )
+    if not fused:
+        from_kv = lax.psum_scatter(from_kv, "ws", scatter_dimension=0, tiled=True)
     grad_normed = t_dot(attn_tokens, normed_back) + from_kv.astype(f32)
     grad_input_norm, grad_gain_one = norm_back(grad_normed, unit_one, inverse_one, gain_one)
     grad_input = grad_hidden + grad_input_norm

time: 799 us -> 788 us (0.986)
  Pallas kernels: 585 us -> 653 us
  waiting for transfers between devices: 64.8 us -> 8.92 us
  between operations: 14.7 us -> 1.49 us
    pallas_call x12, Pallas kernels: 533 us -> 595 us  [run_jobs(): pl.pallas_call(kernel, out_shape=outs, in_specs=[ANY] * len(args), out_sp...]
    reduce_scatter x2 -> x0, waiting for transfers between devices: 24.4 us -> none  [the longest x1 24.4 us: local(): piece = lax.psum_scatter(pieces, 'ep', scatter_dimension=0, tiled=False)]
    all_gather x2 -> x0, waiting for transfers between devices: 17.6 us -> none  [the longest x1 17.6 us: local(): kv_own = lax.all_gather(mine, 'ep', axis=1, tiled=True)]
    ppermute x1, waiting for transfers between devices: 12.9 us -> 0.01 us  [local(): mine = lax.ppermute(key_value_weight, ('ep', 'ws'), there)]
    unnamed x50 -> x44, local copies, waits for them, and re-layouts: 35.2 us -> 33.5 us
  transfers between devices with their start and end apart: 6 -> 2, of which waited for: 4 -> 1; matrix products, arithmetic and copies ran while one was open for 5% -> 2% of each run, Pallas kernels for 25% -> 2%
where the time goes in v5:
time: 788 us; the launch traced here: 778 us
  Pallas kernels  653 us (83%)
  matrix products  59.5 us (8%)
  local copies, waits for them, and re-layouts  37.3 us (5%)
  other arithmetic  9.31 us (1%)
  waiting for transfers between devices  8.92 us (1%)
  starting transfers between devices  8.86 us (1%)
    pallas_call x12, Pallas kernels, run_jobs(): pl.pallas_call(kernel, out_shape=outs, in_specs=[ANY] * len(args), out_sp...  595 us
    unnamed x44, local copies, waits for them, and re-layouts  33.5 us
    dot_general x9, matrix products, dot(): return jnp.dot(a, b, preferred_element_type=f32)  26.9 us
    dot_general x3, matrix products, dot_t(): lax.dot_general(a, b, (((1,), (1,)), ((), ())), preferred_element_type=f32)  18.8 us
    pallas_call x1, Pallas kernels, attend_back_call(): pl.pallas_call(functools.partial(attend_back_kernel, spans), out_shape=[j...  18.4 us
    pallas_call x1, Pallas kernels, gather_call(): pl.pallas_call(functools.partial(gather_kernel, n, n_ws), out_shape=jax.S...  16 us
  transfers between devices with their start and end apart: 2, of which 1 were waited for; matrix products, arithmetic and copies ran while one was open for 2% of the time, Pallas kernels for 2%

profile of v5, /device:TPU:1, one launch (start us, length us, event | category | flops | bytes accessed | tf_op | source)
XLA Modules:
  0.0 778.4 jit_solution(14704668941851608249)
XLA Ops:
  6.6 16.0 %gather_gains.1 = f32[8,4,1,128]{3,2,1,0:T(1,128)} custom-call(f32[1,128]{1,0:T(1,128)} %maximum_convert_fusion.own), custom_call_target="tpu_custom_call" | custom-call | tf_op jit(solution)/shard_map/gather_gains/pallas_call | solution.py:942
  33.4 84.1 %dispatch_weights.1 = (bf16[8,4,40,2048]{3,2,1,0:T(8,128)(2,1)}, bf16[2048,1024]{1,0:T(8,128)(2,1)}, bf16[4,128,2048]{2,1,0:T(8,128)(2,1)}, bf16[2048,1408]{1,0:T(8,128)(2,1)}, bf16[2048,1408]{1,0:T(8,128)(2,1)}) custom-call(bf16[8,40,2048]{2,1,0:T(8,128)(2,1)} %bitcast.111, bf16[2048,128]{1,0:T(8,128)(2,1)} %collective-permute-done.refs_1_, ...), custom_call_target="tpu_custom_call" | custom-call | tf_op jit(solution)/shard_map/dispatch_weights/pallas_call | solution.py:107
  117.5 7.1 convolution_convert_fusion.5
  124.6 25.2 %exchange.2 = bf16[8,160,512]{2,1,0:T(8,128)(2,1)} custom-call(bf16[8,160,512]{2,1,0:T(8,128)(2,1)} %bitcast.119), custom_call_target="tpu_custom_call" | custom-call | tf_op jit(solution)/shard_map/exchange/pallas_call | solution.py:107
  149.8 6.1 convolution_convert_fusion.8.kv_ref
  155.9 13.2 %attend.1 = bf16[8,4,40,512]{3,2,1,0:T(8,128)(2,1)} custom-call(bf16[8,4,40,512]{3,2,1,0:T(8,128)(2,1)} %bitcast.90, bf16[512,1024]{1,0:T(8,128)(2,1)} %convolution_convert_fusion.8.kv_ref), custom_call_target="tpu_custom_call" | custom-call | tf_op jit(solution)/shard_map/attend/pallas_call | solution.py:870
  169.1 31.2 %exchange.3 = bf16[8,160,512]{2,1,0:T(8,128)(2,1)} custom-call(bf16[8,160,512]{2,1,0:T(8,128)(2,1)} %bitcast.99), custom_call_target="tpu_custom_call" | custom-call | tf_op jit(solution)/shard_map/exchange/pallas_call | solution.py:107
  200.3 6.1 convolution_convert_fusion.1
  206.4 51.3 %combine.1 = bf16[8,40,2048]{2,1,0:T(8,128)(2,1)} custom-call(bf16[8,4,40,2048]{3,2,1,0:T(8,128)(2,1)} %bitcast.103), custom_call_target="tpu_custom_call" | custom-call | tf_op jit(solution)/shard_map/combine/pallas_call | solution.py:107
  262.0 40.3 %dispatch.1 = bf16[8,4,40,2048]{3,2,1,0:T(8,128)(2,1)} custom-call(bf16[8,40,2048]{2,1,0:T(8,128)(2,1)} %bitcast.108), custom_call_target="tpu_custom_call" | custom-call | tf_op jit(solution)/shard_map/dispatch/pallas_call | solution.py:107
  302.3 55.2 %dispatch_ffn.1 = (bf16[8,4,40,2048]{3,2,1,0:T(8,128)(2,1)}, f32[1280,1408]{1,0:T(8,128)}, f32[1280,1408]{1,0:T(8,128)}, bf16[1280,1408]{1,0:T(8,128)(2,1)}, bf16[1280,2048]{1,0:T(8,128)(2,1)}) custom-call(bf16[8,40,2048]{2,1,0:T(8,128)(2,1)} %bitcast.96, bf16[1280,2048]{1,0:T(8,128)(2,1)} %bitcast.83, bf16[2048,1408]{1,0:T(8,128)(2,1)} %get-tuple-element.39.refs_2_.refs_4_, ...), custom_call_target="tpu_custom_call" | custom-call | tf_op jit(solution)/shard_map/dispatch_ffn/pallas_call | solution.py:107
  357.5 53.9 %combine_ffn_back.1 = (bf16[8,40,2048]{2,1,0:T(8,128)(2,1)}, bf16[1280,1408]{1,0:T(8,128)(2,1)}, bf16[1280,1408]{1,0:T(8,128)(2,1)}, bf16[1280,2048]{1,0:T(8,128)(2,1)}) custom-call(bf16[8,4,40,2048]{3,2,1,0:T(8,128)(2,1)} %bitcast.98, bf16[1280,2048]{1,0:T(8,128)(2,1)} %bitcast.88, f32[1280,1408]{1,0:T(8,128)} %get-tuple-element.43.refs_2_, ...), custom_call_target="tpu_custom_call" | custom-call | tf_op jit(solution)/shard_map/combine_ffn_back/pallas_call | solution.py:107
  411.4 47.0 %combine_grad_out.1 = (bf16[8,40,2048]{2,1,0:T(8,128)(2,1)}, f32[1408,2048]{1,0:T(8,128)}) custom-call(bf16[8,4,40,2048]{3,2,1,0:T(8,128)(2,1)} %bitcast.97, bf16[1280,1408]{1,0:T(8,128)(2,1)} %get-tuple-element.47.refs_1_, bf16[1280,2048]{1,0:T(8,128)(2,1)} %bitcast.89), custom_call_target="tpu_custom_call" | custom-call | tf_op jit(solution)/shard_map/combine_grad_out/pallas_call | solution.py:107
  463.0 42.8 %dispatch_grad_in.1 = (bf16[8,4,40,2048]{3,2,1,0:T(8,128)(2,1)}, f32[2048,2,1408]{2,1,0:T(2,128)}) custom-call(bf16[8,40,2048]{2,1,0:T(8,128)(2,1)} %bitcast.112, bf16[1280,2048]{1,0:T(8,128)(2,1)} %bitcast.84, bf16[1280,1408]{1,0:T(8,128)(2,1)} %get-tuple-element.49.refs_2_, bf16[1280,1408]{1,0:T(8,128)(2,1)} %get-tuple-element.50.refs_3_), custom_call_target="tpu_custom_call" | custom-call | tf_op jit(solution)/shard_map/dispatch_grad_in/pallas_call | solution.py:107
  505.8 6.5 convolution_convert_fusion.4
  512.3 26.0 %exchange_grad_output.1 = (bf16[8,160,512]{2,1,0:T(8,128)(2,1)}, f32[512,2048]{1,0:T(8,128)}) custom-call(bf16[8,160,512]{2,1,0:T(8,128)(2,1)} %bitcast.123, bf16[1280,512]{1,0:T(8,128)(2,1)} %bitcast.110, bf16[1280,2048]{1,0:T(8,128)(2,1)} %bitcast.107), custom_call_target="tpu_custom_call" | custom-call | tf_op jit(solution)/shard_map/exchange_grad_output/pallas_call | solution.py:107
  538.3 18.4 %attend_back.1 = (bf16[8,4,40,512]{3,2,1,0:T(8,128)(2,1)}, bf16[512,1024]{1,0:T(8,128)(2,1)}) custom-call(bf16[8,4,40,512]{3,2,1,0:T(8,128)(2,1)} %bitcast.91, bf16[8,4,40,512]{3,2,1,0:T(8,128)(2,1)} %bitcast.116, bf16[512,1024]{1,0:T(8,128)(2,1)} %convolution_convert_fusion.8.kv_ref), custom_call_target="tpu_custom_call" | custom-call | tf_op jit(solution)/shard_map/attend_back/pallas_call | solution.py:905
  556.7 6.3 convolution_convert_fusion.3
  567.4 93.0 %exchange_weights.1 = (bf16[8,160,512]{2,1,0:T(8,128)(2,1)}, bf16[2048,128]{1,0:T(8,128)(2,1)}, bf16[128,2048]{1,0:T(8,128)(2,1)}) custom-call(bf16[8,160,512]{2,1,0:T(8,128)(2,1)} %bitcast.120, bf16[2048,1024]{1,0:T(8,128)(2,1)} %convolution_convert_fusion.2.refs_1_, bf16[4,128,2048]{2,1,0:T(8,128)(2,1)} %bitcast.115), custom_call_target="tpu_custom_call" | custom-call | tf_op jit(solution)/shard_map/exchange_weights/pallas_call | solution.py:107
  666.4 44.9 %combine_grad_query.1 = (bf16[8,40,2048]{2,1,0:T(8,128)(2,1)}, f32[2048,512]{1,0:T(8,128)}) custom-call(bf16[8,4,40,2048]{3,2,1,0:T(8,128)(2,1)} %bitcast.102, bf16[1280,2048]{1,0:T(8,128)(2,1)} %bitcast.101, bf16[1280,512]{1,0:T(8,128)(2,1)} %bitcast.122), custom_call_target="tpu_custom_call" | custom-call | tf_op jit(solution)/shard_map/combine_grad_query/pallas_call | solution.py:107
  715.2 10.6 %reduce_gains.1 = f32[1,128]{1,0:T(1,128)} custom-call(f32[8,4,1,128]{3,2,1,0:T(1,128)} %reshape.182.parts), custom_call_target="tpu_custom_call" | custom-call | tf_op jit(solution)/shard_map/reduce_gains/pallas_call | solution.py:981
  735.2 8.9 %collective-permute-done.1 = bf16[2048,128]{1,0:T(8,128)(2,1)S(1)} collective-permute-done((bf16[2048,128]{1,0:T(8,128)(2,1)}, bf16[2048,128]{1,0:T(8,128)(2,1)S(1)}, u32[]{:S(2)}, u32[]{:S(2)}) %collective-permute-start.1) | collective-permute-done | bytes 524320 | tf_op jit(solution)/shard_map/ppermute | solution.py:1320
  750.9 16.3 %copy.30 = f32[1,2048,2,1408]{3,2,1,0:T(2,128)} copy(f32[1,2048,2,1408]{3,2,1,0:T(2,128)} %bitcast.87) | data formatting | bytes 46137344
  767.2 10.8 %copy.31 = f32[1,1408,2048]{2,1,0:T(8,128)} copy(f32[1,1408,2048]{2,1,0:T(8,128)} %bitcast.94) | data formatting | bytes 23068672
  (86 shorter events, 55.8 us)
Async XLA Ops:
  0.6 199.7 %copy-start = (bf16[1,512,2048]{2,1,0:T(8,128)(2,1)S(1)}, bf16[1,512,2048]{2,1,0:T(8,128)(2,1)}, u32[]{:S(2)}) copy-start(bf16[1,512,2048]{2,1,0:T(8,128)(2,1)} %param.20) | copy-start | bytes 6291460
  0.7 30.4 %copy-start.9 = (bf16[128,2048]{1,0:T(8,128)(2,1)S(1)}, bf16[128,2048]{1,0:T(8,128)(2,1)}, u32[]{:S(2)}) copy-start(bf16[128,2048]{1,0:T(8,128)(2,1)} %param.29) | copy-start | bytes 1572868
  0.7 32.7 %collective-permute-start = (bf16[2048,128]{1,0:T(8,128)(2,1)}, bf16[2048,128]{1,0:T(8,128)(2,1)}, u32[]{:S(2)}, u32[]{:S(2)}) collective-permute-start(bf16[2048,128]{1,0:T(8,128)(2,1)} %param.18), channel_id=1, source_target_pairs={{0,0},{1,4},{2,8},{3,12},{4,1},{5,5},{6,9},{7,13},{8,2},{9,6},{10,... | collective-permute-start | bytes 1572872 | tf_op jit(solution)/shard_map/ppermute | solution.py:1124
  29.5 2.2 copy-start.11
  29.5 2.2 copy-start.16
  257.7 2.0 copy-start.4
  257.7 2.0 copy-start.6
  458.4 2.0 copy-start.10
  460.8 2.2 copy-start.2
  556.7 6.3 copy-start.18
  556.7 6.4 copy-start.19
  567.4 93.0 %copy-start.17 = (bf16[1,2048,512]{2,1,0:T(8,128)(2,1)S(1)}, bf16[1,2048,512]{2,1,0:T(8,128)(2,1)}, u32[]{:S(2)}) copy-start(bf16[1,2048,512]{2,1,0:T(8,128)(2,1)} %param.19) | copy-start | bytes 6291460
  666.4 44.9 %copy-start.15 = (bf16[128,2048]{1,0:T(8,128)(2,1)S(1)}, bf16[128,2048]{1,0:T(8,128)(2,1)}, u32[]{:S(2)}) copy-start(bf16[128,2048]{1,0:T(8,128)(2,1)} %get-tuple-element.57) | copy-start | bytes 1572868
  711.3 20.2 %copy-start.7 = (bf16[8,40,2048]{2,1,0:T(8,128)(2,1)S(1)}, bf16[8,40,2048]{2,1,0:T(8,128)(2,1)}, u32[]{:S(2)}) copy-start(bf16[8,40,2048]{2,1,0:T(8,128)(2,1)} %get-tuple-element.45) | copy-start | bytes 3932164
  725.9 6.1 copy-start.8
  727.2 16.9 %collective-permute-start.1 = (bf16[2048,128]{1,0:T(8,128)(2,1)}, bf16[2048,128]{1,0:T(8,128)(2,1)S(1)}, u32[]{:S(2)}, u32[]{:S(2)}) collective-permute-start(bf16[2048,128]{1,0:T(8,128)(2,1)} %get-tuple-element.58), channel_id=1, source_target_pairs={{0,0},{4,1},{8,2},{12,3},{1,4},{5,5},{9,6},{13,7},{2,8},{6,9},{10,... | collective-permute-start | bytes 1572872 | tf_op jit(solution)/shard_map/ppermute | solution.py:1320
  732.0 1.3 copy-start.3
  732.0 1.3 copy-start.5
  732.0 1.9 copy-start.14
  733.9 11.3 %copy-start.13 = (f32[2048,512]{1,0:T(8,128)S(1)}, f32[2048,512]{1,0:T(8,128)}, u32[]{:S(2)}) copy-start(f32[2048,512]{1,0:T(8,128)} %get-tuple-element.59) | copy-start | bytes 12582916
  745.2 3.7 copy-start.12
  767.2 10.8 %copy-start.1 = (bf16[1,512,2048]{2,1,0:T(8,128)(2,1)S(1)}, bf16[1,512,2048]{2,1,0:T(8,128)(2,1)}, u32[]{:S(2)}) copy-start(bf16[1,512,2048]{2,1,0:T(8,128)(2,1)} %param.20) | copy-start | bytes 6291460

commit v6 on v5

--- a/solution.py
+++ b/solution.py
@@ -656,18 +656,20 @@
 
 def gather_weights_job(mine, normed, n, n_ws):
     rows, block = mine.shape
-    routes = [(4, 0), (1, 0), (2, 0), (2, 4), (1, 4), (1, 2), (1, 6)]
-
-    def body(mine, normed, out, seq, held, held_rows, load_sem, s_sem, r_sem, w_s, w_r):
+    routes = [(4, 0), (2, 0), (2, 4)]
+
+    def body(
+        mine, normed, out, seq, held, held_rows, load_sem, s_sem, r_sem, x_s, x_r, y_s, y_r, c_s, c_r, t_s, t_r
+    ):
         e, w = lax.axis_index("ep"), lax.axis_index("ws")
-        twin, other = flip(w, 1), flip(w, 2)
+        twin, other, near = flip(w, 1), flip(w, 2), flip(e, 1)
         copies = {}
 
         def send(hop, offset, half):
             k = routes.index((hop, offset))
-            s = flip(e, offset)
             part = pl.ds(half * (rows // 2), rows // 2)
-            place = out.at[part, pl.ds(pl.multiple_of(s * block, block), block)]
+            at = pl.multiple_of(flip(e, offset) // 2 * block, block)
+            place = out.at[part, pl.ds(at, block)]
             copies[hop, offset, half] = remote(
                 place if offset else mine.at[part],
                 place,
@@ -678,59 +680,98 @@
             copies[hop, offset, half].start()
 
         for half in range(2):
-            for route in routes[:3]:
+            for route in routes[:2]:
                 send(*route, half)
-        over_y = remote(normed, seq.at[w], w_s.at[0], w_r.at[0], (e, other))
-        over_y.start()
-        to_twin = remote(normed, seq.at[w], w_s.at[1], w_r.at[1], (e, twin))
-        to_twin.start()
+        to_near = remote(normed, seq.at[e % 2, w], x_s, x_r, (near, w))
+        to_near.start()
+        over_y, to_twin, relays = [], [], []
+
+        def spread_rows(k, half, src):
+            place = seq.at[half, w]
+            over_y.append(remote(src, place, y_s.at[k], y_r.at[k], (e, other)))
+            over_y[k].start()
+            to_twin.append(remote(src, place, c_s.at[k], c_r.at[k], (e, twin)))
+            to_twin[k].start()
+
+        def relay(k, half):
+            over_y[k].wait_recv()
+            place = seq.at[half, other]
+            relays.append(remote(place, place, t_s.at[k], t_r.at[k], (e, twin)))
+            relays[k].start()
+
+        spread_rows(0, e % 2, normed)
         loads = fetch(((mine, held), (normed, held_rows)), load_sem)
         for load in loads:
             load.wait()
-        own = out.at[:, pl.ds(pl.multiple_of(e * block, block), block)]
-        stores = fetch(((held, own), (held_rows, seq.at[w])), load_sem)
-        yield
-        over_y.wait_recv()
-        relay = remote(seq.at[other], seq.at[other], w_s.at[2], w_r.at[2], (e, twin))
-        relay.start()
-        for arrival, onward in (
-            ((4, 0), ((2, 4), (1, 4))),
-            ((2, 0), ((1, 2),)),
-            ((2, 4), ((1, 6),)),
-        ):
-            for half in range(2):
-                copies[(*arrival, half)].wait_recv()
-                for route in onward:
-                    send(*route, half)
-                yield
+        own = out.at[:, pl.ds(pl.multiple_of(e // 2 * block, block), block)]
+        stores = fetch(((held, own), (held_rows, seq.at[e % 2, w])), load_sem)
+        yield
+        to_near.wait_recv()
+        spread_rows(1, near % 2, seq.at[near % 2, w])
+        yield
+        copies[4, 0, 0].wait_recv()
+        send(2, 4, 0)
+        yield
+        relay(0, e % 2)
+        copies[4, 0, 1].wait_recv()
+        send(2, 4, 1)
+        yield
+        relay(1, near % 2)
+        yield
         for store in stores:
             store.wait()
-        for (hop, offset, _), copy in copies.items():
+        for (_, offset, half), copy in copies.items():
             copy.wait_send()
-            if hop == 1:
+            if (_, offset) != (4, 0):
                 copy.wait_recv()
-        over_y.wait_send()
-        to_twin.wait()
-        relay.wait()
+        to_near.wait_send()
+        for copy in over_y:
+            copy.wait_send()
+        for copy in to_twin + relays:
+            copy.wait()
 
     return Job(
         [mine, normed],
         [
-            jax.ShapeDtypeStruct((rows, n * block), bf16),
-            jax.ShapeDtypeStruct((n_ws,) + normed.shape, bf16),
+            jax.ShapeDtypeStruct((rows, n // 2 * block), bf16),
+            jax.ShapeDtypeStruct((2, n_ws) + normed.shape, bf16),
         ],
         [
             pltpu.VMEM(mine.shape, bf16),
             pltpu.VMEM(normed.shape, bf16),
             DMA((2,)),
-            DMA((7, 2)),
-            DMA((7, 2)),
-            DMA((3,)),
-            DMA((3,)),
-        ],
-        7,
+            DMA((3, 2)),
+            DMA((3, 2)),
+            DMA,
+            DMA,
+        ]
+        + [DMA((2,)) for _ in range(6)],
+        5,
         body,
         [(1, 0), (2, 0), (4, 0), (0, 1), (0, 2)],
+    )
+
+
+def swap_job(blocks):
+    def body(blocks, out, held, load_sem, s_sem, r_sem):
+        e, w = lax.axis_index("ep"), lax.axis_index("ws")
+        near = flip(e, 1)
+        copy = remote(blocks.at[near % 2], out.at[e % 2], s_sem, r_sem, (near, w))
+        copy.start()
+        load = fetch(((blocks.at[e % 2], held),), load_sem)[0]
+        load.wait()
+        store = fetch(((held, out.at[e % 2]),), load_sem)[0]
+        yield
+        store.wait()
+        copy.wait()
+
+    return Job(
+        [blocks],
+        [jax.ShapeDtypeStruct(blocks.shape, blocks.dtype)],
+        [pltpu.VMEM(blocks.shape[1:], blocks.dtype), DMA((1,)), DMA, DMA],
+        1,
+        body,
+        [(1, 0)],
     )
 
 
@@ -750,84 +791,96 @@
 
 def reduce_weights_job(pieces, part, n):
     rows = pieces.shape[0]
-    block = pieces.shape[1] // n
-    offsets = (6, 4, 2, 0)
+    block = pieces.shape[1] // (n // 2)
+    offsets = (4, 0)
 
     def body(
-        pieces, part, out, out_rows, mine, from_x, sums, from_z, last_z, fourth, total, own, core, sum_y, from_y,
-        total_rows, load_sem, x_s, x_r, z_s, z_r, w_load, w_s, w_r, sem
+        pieces, part, out, out_rows, mine, from_z, fourth, last_z, total, own, core, sum_y, from_y, total_near,
+        from_near, total_rows, load_sem, z_s, z_r, w_load, c_s, c_r, y_s, y_r, x_s, x_r, sem
     ):
         e, w = lax.axis_index("ep"), lax.axis_index("ws")
-        twin, other, last = flip(w, 1), flip(w, 2), flip(w, 3)
+        twin, other, last, near = flip(w, 1), flip(w, 2), flip(w, 3), flip(e, 1)
 
         def columns(s):
-            return pieces.at[:, pl.ds(pl.multiple_of(s * block, block), block)]
-
-        across = []
+            return pieces.at[:, pl.ds(pl.multiple_of(s // 2 * block, block), block)]
+
+        over_z = []
         for i, offset in enumerate(offsets):
-            across.append(
-                remote(columns(flip(e, offset + 1)), from_x.at[i], x_s.at[i], x_r.at[i], (flip(e, 1), w))
+            over_z.append(
+                remote(columns(flip(e, offset + 2)), from_z.at[i], z_s.at[i], z_r.at[i], (flip(e, 2), w))
             )
-            across[i].start()
-        cores = [
-            remote(part.at[to], core.at[k], w_s.at[k], w_r.at[k], (e, twin))
-            for k, to in enumerate((last, twin))
-        ]
-        for copy in cores:
-            copy.start()
+            over_z[i].start()
+        halves = (near % 2, e % 2)
+        cores = {}
+        for k, to in enumerate((last, twin)):
+            for h, half in enumerate(halves):
+                cores[h, k] = remote(
+                    part.at[half, to], core.at[h, k], c_s.at[h, k], c_r.at[h, k], (e, twin)
+                )
+                cores[h, k].start()
         loads = fetch([(columns(flip(e, o)), mine.at[i]) for i, o in enumerate(offsets)], load_sem)
-        own_loads = fetch(((part.at[other], own.at[0]), (part.at[w], own.at[1])), w_load)
-        yield
-
-        def add(i):
-            loads[i].wait()
-            across[i].wait_recv()
-            add_blocks(sums.at[i], mine.at[i], from_x.at[i])
-
-        own_loads[0].wait()
-        cores[0].wait_recv()
-        add_blocks(sum_y, own.at[0], core.at[0])
-        add(0)
-        over_y = remote(sum_y, from_y, w_s.at[2], w_r.at[2], (e, other))
-        over_y.start()
-        yield
-        add(1)
-        first = remote(sums.at[0], from_z.at[0], z_s.at[0], z_r.at[0], (flip(e, 2), w))
-        first.start()
-        yield
-        add(2)
-        first.wait_recv()
-        add_blocks(fourth, sums.at[1], from_z.at[0])
-        second = remote(sums.at[2], from_z.at[1], z_s.at[1], z_r.at[1], (flip(e, 2), w))
-        second.start()
-        yield
-        add(3)
-        third = remote(fourth, last_z, z_s.at[2], z_r.at[2], (flip(e, 4), w))
-        third.start()
-        yield
-        own_loads[1].wait()
-        cores[1].wait_recv()
-        over_y.wait_recv()
-        add_blocks(total_rows, own.at[1], core.at[1], from_y)
-        second.wait_recv()
-        third.wait_recv()
-        add_blocks(total, sums.at[3], from_z.at[1], last_z)
+        own_loads = {}
+        for h, half in enumerate(halves):
+            for k, to in enumerate((other, w)):
+                own_loads[h, k] = pltpu.make_async_copy(
+                    part.at[half, to], own.at[h, k], w_load.at[h, k]
+                )
+                own_loads[h, k].start()
+        yield
+        over_y = []
+
+        def send_y(h):
+            over_y.append(remote(sum_y.at[h], from_y.at[h], y_s.at[h], y_r.at[h], (e, other)))
+            over_y[h].start()
+
+        for h in range(2):
+            own_loads[h, 0].wait()
+            cores[h, 0].wait_recv()
+            add_blocks(sum_y.at[h], own.at[h, 0], core.at[h, 0])
+            if h:
+                send_y(0)
+        yield
+        loads[0].wait()
+        over_z[0].wait_recv()
+        send_y(1)
+        add_blocks(fourth, mine.at[0], from_z.at[0])
+        yield
+        own_loads[0, 1].wait()
+        cores[0, 1].wait_recv()
+        over_y[0].wait_recv()
+        far = remote(fourth, last_z, z_s.at[2], z_r.at[2], (flip(e, 4), w))
+        far.start()
+        add_blocks(total_near, own.at[0, 1], core.at[0, 1], from_y.at[0])
+        yield
+        own_loads[1, 1].wait()
+        cores[1, 1].wait_recv()
+        over_y[1].wait_recv()
+        to_near = remote(total_near, from_near, x_s, x_r, (near, w))
+        to_near.start()
+        yield
+        to_near.wait_recv()
+        add_blocks(total_rows, own.at[1, 1], core.at[1, 1], from_y.at[1], from_near)
+        loads[1].wait()
+        over_z[1].wait_recv()
+        far.wait_recv()
+        add_blocks(total, mine.at[1], from_z.at[1], last_z)
         stores = fetch(((total_rows, out_rows), (total, out)), sem)
-        for copy in across + cores + [over_y, first, second, third]:
+        for copy in over_z + list(cores.values()) + over_y + [far, to_near]:
             copy.wait_send()
         for store in stores:
             store.wait()
 
-    one, rows_one = (rows, block), part.shape[1:]
+    one, rows_one = (rows, block), part.shape[2:]
     return Job(
         [pieces, part],
         [jax.ShapeDtypeStruct(one, bf16), jax.ShapeDtypeStruct(rows_one, bf16)],
-        [pltpu.VMEM((4,) + one, bf16) for _ in range(3)]
-        + [pltpu.VMEM((2,) + one, bf16)]
+        [pltpu.VMEM((2,) + one, bf16) for _ in range(2)]
         + [pltpu.VMEM(one, bf16) for _ in range(3)]
+        + [pltpu.VMEM((2, 2) + rows_one, bf16) for _ in range(2)]
         + [pltpu.VMEM((2,) + rows_one, bf16) for _ in range(2)]
         + [pltpu.VMEM(rows_one, bf16) for _ in range(3)]
-        + [DMA((4,)), DMA((4,)), DMA((4,)), DMA((3,)), DMA((3,)), DMA((2,)), DMA((3,)), DMA((3,)), DMA((2,))],
+        + [DMA((2,)), DMA((3,)), DMA((3,)), DMA((2, 2)), DMA((2, 2)), DMA((2, 2))]
+        + [DMA((2,)), DMA((2,)), DMA, DMA, DMA((2,))],
         5,
         body,
         [(1, 0), (2, 0), (4, 0), (0, 1), (0, 2)],
@@ -855,11 +908,19 @@
     return rows.reshape(count * slots, HEAD_SIZE).astype(bf16)
 
 
+def kv_place(kv, at):
+    h = at // HEAD_SIZE
+    column = pl.multiple_of(h // 2 * HEAD_SIZE, HEAD_SIZE)
+    half = kv.shape[2] // 2
+    value_column = pl.multiple_of(half + column, HEAD_SIZE)
+    return h % 2, pl.ds(column, HEAD_SIZE), pl.ds(value_column, HEAD_SIZE)
+
+
 def head_probs(q_ref, kv_ref, w, span, at):
-    half = kv_ref.shape[1] // 2
     q = slot_rows(q_ref, w, at)
-    keys = kv_ref[:span, pl.ds(at, HEAD_SIZE)]
-    values = kv_ref[:span, pl.ds(pl.multiple_of(half + at, HEAD_SIZE), HEAD_SIZE)]
+    side, key_columns, value_columns = kv_place(kv_ref, at)
+    keys = kv_ref[side, :span, key_columns]
+    values = kv_ref[side, :span, value_columns]
     scores = dot_t(q, keys) * HEAD_SIZE ** (-0.5)
     weight = jnp.exp(scores - jnp.max(scores, -1, keepdims=True))
     probs = weight / jnp.sum(weight, -1, keepdims=True)
@@ -892,9 +953,9 @@
             grad_scores = (probs * (grad_probs - centred)).astype(bf16)
             grad_rows = dot(grad_scores, keys) * HEAD_SIZE ** (-0.5)
             grad_q[:, w, :, columns] = grad_rows.reshape(count, slots, HEAD_SIZE).astype(bf16)
-            total[:span, columns] += t_dot(grad_scores, q) * HEAD_SIZE ** (-0.5)
-            at_value = pl.ds(pl.multiple_of(part + at, HEAD_SIZE), HEAD_SIZE)
-            total[:span, at_value] += t_dot(probs.astype(bf16), grad)
+            side, key_columns, value_columns = kv_place(kv_ref, at)
+            total[side, :span, key_columns] += t_dot(grad_scores, q) * HEAD_SIZE ** (-0.5)
+            total[side, :span, value_columns] += t_dot(probs.astype(bf16), grad)
             return carry
 
         lax.fori_loop(0, part // HEAD_SIZE, head, 0)
@@ -1148,20 +1209,27 @@
             "dispatch_weights",
         )
         rows_one = rows_one.reshape(-1, width)
-        normed_sequence = normed_sequence.reshape(sequence, width)
+        normed_sequence = normed_sequence.reshape(2 * sequence, width)
     else:
         if plain:
             kv_own = lax.all_gather(mine, "ep", axis=1, tiled=True)
         normed_sequence = lax.all_gather(normed, "ws", axis=0, tiled=True)
         rows_one, gate_weight, up_weight = dispatch(slots_one, group, (split_job, w_in[0]))
     kv = dot(normed_sequence, kv_own).astype(bf16)
-    keys = kv[:, :own_width].reshape(sequence, -1, HEAD_SIZE)
-    values = kv[:, own_width:].reshape(sequence, -1, HEAD_SIZE)
+    if not fused:
+        keys = kv[:, :own_width].reshape(sequence, -1, HEAD_SIZE)
+        values = kv[:, own_width:].reshape(sequence, -1, HEAD_SIZE)
 
     owner_query = dot(rows_one, w_query[0]).astype(bf16)
-    queries = exchange(owner_query.reshape(n_ep, n_ws * ROWS, part))[0]
+    owner_query = owner_query.reshape(n_ep, n_ws * ROWS, part)
+    if fused:
+        queries, kv = run_jobs(
+            [exchange_job(owner_query), swap_job(kv.reshape(2, sequence, -1))], [], 13, "exchange_kv"
+        )
+    else:
+        queries = exchange(owner_query)[0]
+    queries = queries.reshape(MIXTURE_EXPERTS, group, n_ws, ROWS, part)
     spans = [(w * local_tokens // BLOCK + 1) * BLOCK for w in range(n_ws)]
-    queries = queries.reshape(MIXTURE_EXPERTS, group, n_ws, ROWS, part)
 
     def by_block(rows):
         rows = rows.reshape(MIXTURE_EXPERTS, group, n_ws, ROWS, part)
@@ -1287,34 +1355,34 @@
             [grad_keys.reshape(sequence, -1), grad_values.reshape(sequence, -1)], 1
         ).astype(bf16)
         query_grads = to_experts(query_pieces)
+    if fused:
+        owner_grad_query, grad_kv_rows = run_jobs(
+            [exchange_job(query_grads), swap_job(grad_kv_rows)], [], 14, "exchange_grad_kv"
+        )
+        owner_grad_query = owner_grad_query.reshape(-1, part)
+        grad_kv_rows = grad_kv_rows.reshape(2 * sequence, -1)
+    else:
+        owner_grad_query = exchange(query_grads)[0].reshape(-1, part)
     grad_kv = t_dot(normed_sequence, grad_kv_rows)
     from_kv = dot_t(grad_kv_rows, kv_own).astype(bf16)
+    back_normed = dot_t(owner_grad_query, w_query[0]).astype(bf16)
     if fused:
-        owner_grad_query, piece, from_kv = run_jobs(
+        normed_back, piece, from_kv, grad_query = run_jobs(
             [
-                exchange_job(query_grads),
+                combine_job(back_normed.reshape(n_ep, n_ws, ROWS, width)),
                 reduce_weights_job(
-                    grad_kv.astype(bf16), from_kv.reshape(n_ws, local_tokens, width), n_ep
+                    grad_kv.astype(bf16), from_kv.reshape(2, n_ws, local_tokens, width), n_ep
                 ),
             ],
-            [],
-            12,
-            "exchange_weights",
+            [grad_job(rows_one, owner_grad_query)],
+            9,
+            "combine_weights",
         )
-        owner_grad_query = owner_grad_query.reshape(-1, part)
+        normed_back = normed_back.reshape(-1, width)
     else:
-        owner_grad_query = exchange(query_grads)[0].reshape(-1, part)
-    back_normed = dot_t(owner_grad_query, w_query[0]).astype(bf16)
-    normed_back, grad_query = combine(
-        back_normed,
-        group,
-        n_ep,
-        n_ws,
-        (grad_job, rows_one, owner_grad_query),
-        collective_id=9,
-        name="combine_grad_query",
-    )
-
+        normed_back, grad_query = combine(
+            back_normed, group, n_ep, n_ws, (grad_job, rows_one, owner_grad_query)
+        )
     if fused:
         back = [(b, a) for a, b in there]
         grad_kv_shard = lax.ppermute(piece, ("ep", "ws"), back).astype(f32)

time: 788 us -> 743 us (0.943)
  Pallas kernels: 653 us -> 618 us
    pallas_call x12, Pallas kernels: 595 us -> 558 us  [run_jobs(): pl.pallas_call(kernel, out_shape=outs, in_specs=[ANY] * len(args), out_sp...]
    unnamed x44 -> x52, local copies, waits for them, and re-layouts: 33.5 us -> 34.3 us
where the time goes in v6:
time: 743 us; the launch traced here: 737 us
  Pallas kernels  618 us (83%)
  matrix products  54 us (7%)
  local copies, waits for them, and re-layouts  38.1 us (5%)
  other arithmetic  9.32 us (1%)
  starting transfers between devices  8.82 us (1%)
    pallas_call x12, Pallas kernels, run_jobs(): pl.pallas_call(kernel, out_shape=outs, in_specs=[ANY] * len(args), out_sp...  558 us
    unnamed x52, local copies, waits for them, and re-layouts  34.3 us
    dot_general x9, matrix products, dot(): return jnp.dot(a, b, preferred_element_type=f32)  23.8 us
    pallas_call x1, Pallas kernels, attend_back_call(): pl.pallas_call(functools.partial(attend_back_kernel, spans), out_shape=[j...  18.6 us
    dot_general x3, matrix products, dot_t(): lax.dot_general(a, b, (((1,), (1,)), ((), ())), preferred_element_type=f32)  16.9 us
    pallas_call x1, Pallas kernels, gather_call(): pl.pallas_call(functools.partial(gather_kernel, n, n_ws), out_shape=jax.S...  16 us
  transfers between devices with their start and end apart: 2, of which 1 were waited for; matrix products, arithmetic and copies ran while one was open for 2% of the time, Pallas kernels for 2%

profile of v6, /device:TPU:1, one launch (start us, length us, event | category | flops | bytes accessed | tf_op | source)
XLA Modules:
  0.0 736.9 jit_solution(15022722870957426358)
XLA Ops:
  6.6 16.0 %gather_gains.1 = f32[8,4,1,128]{3,2,1,0:T(1,128)} custom-call(f32[1,128]{1,0:T(1,128)} %maximum_convert_fusion.own), custom_call_target="tpu_custom_call" | custom-call | tf_op jit(solution)/shard_map/gather_gains/pallas_call | solution.py:1003
  34.2 71.6 %dispatch_weights.1 = (bf16[8,4,40,2048]{3,2,1,0:T(8,128)(2,1)}, bf16[2048,512]{1,0:T(8,128)(2,1)}, bf16[2,4,128,2048]{3,2,1,0:T(8,128)(2,1)}, bf16[2048,1408]{1,0:T(8,128)(2,1)}, bf16[2048,1408]{1,0:T(8,128)(2,1)}) custom-call(bf16[8,40,2048]{2,1,0:T(8,128)(2,1)} %bitcast.113, bf16[2048,128]{1,0:T(8,128)(2,1)} %copy-done.17, bf16[128,2048]{1,0:T(8,128)(2,1)} %copy-done.12, ...), custom_call_target="tpu_custom_call" | custom-call | tf_op jit(solution)/shard_map/dispatch_weights/pallas_call | solution.py:107
  105.8 6.3 convolution_convert_fusion.8
  116.1 28.8 %exchange_kv.1 = (bf16[8,160,512]{2,1,0:T(8,128)(2,1)}, bf16[2,512,512]{2,1,0:T(8,128)(2,1)}) custom-call(bf16[8,160,512]{2,1,0:T(8,128)(2,1)} %bitcast.124, bf16[2,512,512]{2,1,0:T(8,128)(2,1)} %bitcast.126), custom_call_target="tpu_custom_call" | custom-call | tf_op jit(solution)/shard_map/exchange_kv/pallas_call | solution.py:107
  144.9 13.4 %attend.1 = bf16[8,4,40,512]{3,2,1,0:T(8,128)(2,1)} custom-call(bf16[8,4,40,512]{3,2,1,0:T(8,128)(2,1)} %bitcast.99, bf16[2,512,512]{2,1,0:T(8,128)(2,1)} %get-tuple-element.43.kv_ref), custom_call_target="tpu_custom_call" | custom-call | tf_op jit(solution)/shard_map/attend/pallas_call | solution.py:931
  158.3 27.8 %exchange.1 = bf16[8,160,512]{2,1,0:T(8,128)(2,1)} custom-call(bf16[8,160,512]{2,1,0:T(8,128)(2,1)} %bitcast.101), custom_call_target="tpu_custom_call" | custom-call | tf_op jit(solution)/shard_map/exchange/pallas_call | solution.py:107
  186.1 5.9 convolution_convert_fusion.1
  192.0 51.4 %combine.1 = bf16[8,40,2048]{2,1,0:T(8,128)(2,1)} custom-call(bf16[8,4,40,2048]{3,2,1,0:T(8,128)(2,1)} %bitcast.102), custom_call_target="tpu_custom_call" | custom-call | tf_op jit(solution)/shard_map/combine/pallas_call | solution.py:107
  247.7 39.5 %dispatch.1 = bf16[8,4,40,2048]{3,2,1,0:T(8,128)(2,1)} custom-call(bf16[8,40,2048]{2,1,0:T(8,128)(2,1)} %bitcast.107), custom_call_target="tpu_custom_call" | custom-call | tf_op jit(solution)/shard_map/dispatch/pallas_call | solution.py:107
  287.2 55.3 %dispatch_ffn.1 = (bf16[8,4,40,2048]{3,2,1,0:T(8,128)(2,1)}, f32[1280,1408]{1,0:T(8,128)}, f32[1280,1408]{1,0:T(8,128)}, bf16[1280,1408]{1,0:T(8,128)(2,1)}, bf16[1280,2048]{1,0:T(8,128)(2,1)}) custom-call(bf16[8,40,2048]{2,1,0:T(8,128)(2,1)} %bitcast.96, bf16[1280,2048]{1,0:T(8,128)(2,1)} %bitcast.85, bf16[2048,1408]{1,0:T(8,128)(2,1)} %get-tuple-element.44.refs_2_.refs_4_, ...), custom_call_target="tpu_custom_call" | custom-call | tf_op jit(solution)/shard_map/dispatch_ffn/pallas_call | solution.py:107
  342.5 54.8 %combine_ffn_back.1 = (bf16[8,40,2048]{2,1,0:T(8,128)(2,1)}, bf16[1280,1408]{1,0:T(8,128)(2,1)}, bf16[1280,1408]{1,0:T(8,128)(2,1)}, bf16[1280,2048]{1,0:T(8,128)(2,1)}) custom-call(bf16[8,4,40,2048]{3,2,1,0:T(8,128)(2,1)} %bitcast.98, bf16[1280,2048]{1,0:T(8,128)(2,1)} %bitcast.90, f32[1280,1408]{1,0:T(8,128)} %get-tuple-element.48.refs_2_, ...), custom_call_target="tpu_custom_call" | custom-call | tf_op jit(solution)/shard_map/combine_ffn_back/pallas_call | solution.py:107
  397.3 46.3 %combine_grad_out.1 = (bf16[8,40,2048]{2,1,0:T(8,128)(2,1)}, f32[1408,2048]{1,0:T(8,128)}) custom-call(bf16[8,4,40,2048]{3,2,1,0:T(8,128)(2,1)} %bitcast.97, bf16[1280,1408]{1,0:T(8,128)(2,1)} %get-tuple-element.52.refs_1_, bf16[1280,2048]{1,0:T(8,128)(2,1)} %bitcast.91), custom_call_target="tpu_custom_call" | custom-call | tf_op jit(solution)/shard_map/combine_grad_out/pallas_call | solution.py:107
  448.2 43.6 %dispatch_grad_in.1 = (bf16[8,4,40,2048]{3,2,1,0:T(8,128)(2,1)}, f32[2048,2,1408]{2,1,0:T(2,128)}) custom-call(bf16[8,40,2048]{2,1,0:T(8,128)(2,1)} %bitcast.114, bf16[1280,2048]{1,0:T(8,128)(2,1)} %bitcast.86, bf16[1280,1408]{1,0:T(8,128)(2,1)} %get-tuple-element.54.refs_2_, bf16[1280,1408]{1,0:T(8,128)(2,1)} %get-tuple-element.55.refs_3_), custom_call_target="tpu_custom_call" | custom-call | tf_op jit(solution)/shard_map/dispatch_grad_in/pallas_call | solution.py:107
  491.8 6.5 convolution_convert_fusion.4
  498.3 25.5 %exchange_grad_output.1 = (bf16[8,160,512]{2,1,0:T(8,128)(2,1)}, f32[512,2048]{1,0:T(8,128)}) custom-call(bf16[8,160,512]{2,1,0:T(8,128)(2,1)} %bitcast.125, bf16[1280,512]{1,0:T(8,128)(2,1)} %bitcast.112, bf16[1280,2048]{1,0:T(8,128)(2,1)} %bitcast.106), custom_call_target="tpu_custom_call" | custom-call | tf_op jit(solution)/shard_map/exchange_grad_output/pallas_call | solution.py:107
  523.7 18.6 %attend_back.1 = (bf16[8,4,40,512]{3,2,1,0:T(8,128)(2,1)}, bf16[2,512,512]{2,1,0:T(8,128)(2,1)}) custom-call(bf16[8,4,40,512]{3,2,1,0:T(8,128)(2,1)} %bitcast.100, bf16[8,4,40,512]{3,2,1,0:T(8,128)(2,1)} %bitcast.120, bf16[2,512,512]{2,1,0:T(8,128)(2,1)} %get-tuple-element.43.kv_ref), custom_call_target="tpu_custom_call" | custom-call | tf_op jit(solution)/shard_map/attend_back/pallas_call | solution.py:966
  542.4 34.0 %exchange_grad_kv.1 = (bf16[8,160,512]{2,1,0:T(8,128)(2,1)}, bf16[2,512,512]{2,1,0:T(8,128)(2,1)}) custom-call(bf16[8,160,512]{2,1,0:T(8,128)(2,1)} %bitcast.123, bf16[2,512,512]{2,1,0:T(8,128)(2,1)} %get-tuple-element.59.refs_1_), custom_call_target="tpu_custom_call" | custom-call | tf_op jit(solution)/shard_map/exchange_grad_kv/pallas_call | solution.py:107
  576.4 5.8 convolution_convert_fusion.2
  585.9 4.6 convolution_convert_fusion
  590.6 79.7 %combine_weights.1 = (bf16[8,40,2048]{2,1,0:T(8,128)(2,1)}, bf16[2048,128]{1,0:T(8,128)(2,1)}, bf16[128,2048]{1,0:T(8,128)(2,1)}, f32[2048,512]{1,0:T(8,128)}) custom-call(bf16[8,4,40,2048]{3,2,1,0:T(8,128)(2,1)} %bitcast.110, bf16[2048,512]{1,0:T(8,128)(2,1)} %convolution_convert_fusion.3.refs_1_, bf16[2,4,128,2048]{3,2,1,0:T(8,128)(2,1)} %bitcast.115, ...), custom_call_target="tpu_custom_call" | custom-call | tf_op jit(solution)/shard_map/combine_weights/pallas_call | solution.py:107
  674.3 12.1 %reduce_gains.1 = f32[1,128]{1,0:T(1,128)} custom-call(f32[8,4,1,128]{3,2,1,0:T(1,128)} %reshape.190.parts), custom_call_target="tpu_custom_call" | custom-call | tf_op jit(solution)/shard_map/reduce_gains/pallas_call | solution.py:1042
  695.7 7.2 collective-permute-done.1
  709.6 16.3 %copy.30 = f32[1,2048,2,1408]{3,2,1,0:T(2,128)} copy(f32[1,2048,2,1408]{3,2,1,0:T(2,128)} %bitcast.89) | data formatting | bytes 46137344
  726.0 10.8 %copy.31 = f32[1,1408,2048]{2,1,0:T(8,128)} copy(f32[1,1408,2048]{2,1,0:T(8,128)} %bitcast.94) | data formatting | bytes 23068672
  (94 shorter events, 54.1 us)
Async XLA Ops:
  0.6 185.5 %copy-start = (bf16[1,512,2048]{2,1,0:T(8,128)(2,1)S(1)}, bf16[1,512,2048]{2,1,0:T(8,128)(2,1)}, u32[]{:S(2)}) copy-start(bf16[1,512,2048]{2,1,0:T(8,128)(2,1)} %param.20) | copy-start | bytes 6291460
  0.7 30.4 %copy-start.10 = (bf16[128,2048]{1,0:T(8,128)(2,1)S(1)}, bf16[128,2048]{1,0:T(8,128)(2,1)}, u32[]{:S(2)}) copy-start(bf16[128,2048]{1,0:T(8,128)(2,1)} %param.29) | copy-start | bytes 1572868
  0.7 32.7 %collective-permute-start = (bf16[2048,128]{1,0:T(8,128)(2,1)}, bf16[2048,128]{1,0:T(8,128)(2,1)S(1)}, u32[]{:S(2)}, u32[]{:S(2)}) collective-permute-start(bf16[2048,128]{1,0:T(8,128)(2,1)} %param.18), channel_id=1, source_target_pairs={{0,0},{1,4},{2,8},{3,12},{4,1},{5,5},{6,9},{7,13},{8,2},{9,6},{10,... | collective-permute-start | bytes 1572872 | tf_op jit(solution)/shard_map/ppermute | solution.py:1185
  29.5 2.2 copy-start.12
  29.5 2.2 copy-start.18
  105.8 6.3 copy-start.9
  105.8 6.3 copy-start.20
  243.4 2.0 copy-start.4
  243.4 2.0 copy-start.6
  443.6 2.0 copy-start.11
  446.0 2.2 copy-start.2
  542.4 34.0 %copy-start.22 = (bf16[2048,512]{1,0:T(8,128)(2,1)S(1)}, bf16[2048,512]{1,0:T(8,128)(2,1)}, u32[]{:S(2)}) copy-start(bf16[2048,512]{1,0:T(8,128)(2,1)} %get-tuple-element.41) | copy-start | bytes 6291460
  576.4 5.8 copy-start.19
  576.4 5.8 copy-start.23
  582.2 3.8 copy-start.16
  582.2 3.8 copy-start.21
  670.3 21.7 %copy-start.7 = (bf16[8,40,2048]{2,1,0:T(8,128)(2,1)S(1)}, bf16[8,40,2048]{2,1,0:T(8,128)(2,1)}, u32[]{:S(2)}) copy-start(bf16[8,40,2048]{2,1,0:T(8,128)(2,1)} %get-tuple-element.50) | copy-start | bytes 3932164
  686.4 6.1 copy-start.8
  687.8 15.1 %collective-permute-start.1 = (bf16[2048,128]{1,0:T(8,128)(2,1)}, bf16[2048,128]{1,0:T(8,128)(2,1)S(1)}, u32[]{:S(2)}, u32[]{:S(2)}) collective-permute-start(bf16[2048,128]{1,0:T(8,128)(2,1)} %get-tuple-element.64), channel_id=1, source_target_pairs={{0,0},{4,1},{8,2},{12,3},{1,4},{5,5},{9,6},{13,7},{2,8},{6,9},{10,... | collective-permute-start | bytes 1572872 | tf_op jit(solution)/shard_map/ppermute | solution.py:1388
  692.5 1.4 copy-start.3
  692.5 1.9 copy-start.15
  694.4 9.5 %copy-start.14 = (f32[2048,512]{1,0:T(8,128)S(1)}, f32[2048,512]{1,0:T(8,128)}, u32[]{:S(2)}) copy-start(f32[2048,512]{1,0:T(8,128)} %get-tuple-element.65) | copy-start | bytes 12582916
  703.9 3.7 copy-start.13
  726.0 10.8 %copy-start.1 = (bf16[1,512,2048]{2,1,0:T(8,128)(2,1)S(1)}, bf16[1,512,2048]{2,1,0:T(8,128)(2,1)}, u32[]{:S(2)}) copy-start(bf16[1,512,2048]{2,1,0:T(8,128)(2,1)} %param.20) | copy-start | bytes 6291460
  (2 other events, 2.1 us)

commit v7 on v6

--- a/solution.py
+++ b/solution.py
@@ -654,6 +654,115 @@
     )
 
 
+def exchange_combine_job(rows, weight, product, n_ws):
+    n, held, depth = rows.shape
+    count, width = held // n_ws, max(weight.shape)
+    block = (n, count, width)
+    turned = weight.shape[0] == width
+
+    def body(
+        rows, w_hbm, moved, out, w_ref, here, part, core, sum_y, from_y, total, load_sem, ep_s, ep_r, c_s, c_r,
+        y_s, y_r, b_s, b_r
+    ):
+        e, w = lax.axis_index("ep"), lax.axis_index("ws")
+        twin, other, last = flip(w, 1), flip(w, 2), flip(w, 3)
+        places = [e] + [flip(e, k) for k in range(1, n)]
+        weights = pltpu.make_async_copy(w_hbm, w_ref, load_sem.at[n])
+        weights.start()
+        arrivals = []
+        for i, s in enumerate(places[1:]):
+            arrivals.append(remote(rows.at[s], moved.at[e], ep_s.at[i], ep_r.at[i], (s, w)))
+            arrivals[i].start()
+        cores, over_y, back, stores = {}, [], [], []
+
+        def multiply(j):
+            if j:
+                arrivals[j - 1].wait_recv()
+            src = moved.at[places[j]] if j else rows.at[e]
+            load = pltpu.make_async_copy(src, here.at[j], load_sem.at[j])
+            load.start()
+            load.wait()
+            if j == 0:
+                stores.append(pltpu.make_async_copy(here.at[0], moved.at[e], load_sem.at[0]))
+                stores[0].start()
+                weights.wait()
+
+            def tile(at, columns):
+                tall = pl.ds(at, columns)
+                result = product(here[j], w_ref[tall, :] if turned else w_ref[:, tall])
+                part[j, :, :, tall] = result.reshape(n_ws, count, columns).astype(bf16)
+
+            column_tiles(width, tile)
+
+        def send_core(j):
+            for half, to in ((1, last), (0, twin)):
+                cores[half, j] = remote(
+                    part.at[j, to], core.at[half, j], c_s.at[half, j], c_r.at[half, j], (e, twin)
+                )
+                cores[half, j].start()
+
+        def add_core(j):
+            cores[1, j].wait_recv()
+            sum_y[j] = (part[j, other].astype(f32) + core[1, j].astype(f32)).astype(bf16)
+
+        def send_y(j):
+            over_y.append(remote(sum_y.at[j], from_y.at[j], y_s.at[j], y_r.at[j], (e, other)))
+            over_y[j].start()
+
+        def add_all(j):
+            cores[0, j].wait_recv()
+            over_y[j].wait_recv()
+            total[j] = (
+                part[j, w].astype(f32) + core[0, j].astype(f32) + from_y[j].astype(f32)
+            ).astype(bf16)
+
+        def send_back(j):
+            if j:
+                back.append(
+                    remote(total.at[j], out.at[e], b_s.at[j - 1], b_r.at[j - 1], (places[j], w))
+                )
+                back[j - 1].start()
+            else:
+                stores.append(pltpu.make_async_copy(total.at[0], out.at[e], load_sem.at[1]))
+                stores[1].start()
+
+        for t in range(n + 4):
+            for lag, stage in ((0, multiply), (1, add_core), (3, add_all), (0, send_core), (1, send_y), (4, send_back)):
+                if 0 <= t - lag < n:
+                    stage(t - lag)
+            yield
+        for copy in arrivals + list(cores.values()) + over_y:
+            copy.wait_send()
+        for copy in back + stores:
+            copy.wait()
+
+    return Job(
+        [rows, weight],
+        [jax.ShapeDtypeStruct(rows.shape, bf16), jax.ShapeDtypeStruct(block, bf16)],
+        [
+            pltpu.VMEM(weight.shape, bf16),
+            pltpu.VMEM(rows.shape, bf16),
+            pltpu.VMEM((n, n_ws, count, width), bf16),
+            pltpu.VMEM((2,) + block, bf16),
+            pltpu.VMEM(block, bf16),
+            pltpu.VMEM(block, bf16),
+            pltpu.VMEM(block, bf16),
+            DMA((n + 1,)),
+            DMA((n - 1,)),
+            DMA((n - 1,)),
+            DMA((2, n)),
+            DMA((2, n)),
+            DMA((n,)),
+            DMA((n,)),
+            DMA((n - 1,)),
+            DMA((n - 1,)),
+        ],
+        n + 4,
+        body,
+        [(k, 0) for k in range(1, n)] + [(0, 1), (0, 2)],
+    )
+
+
 def gather_weights_job(mine, normed, n, n_ws):
     rows, block = mine.shape
     routes = [(4, 0), (2, 0), (2, 4)]
@@ -1265,8 +1374,15 @@
             kept.append((q, probs))
             mixed_pieces.append(mixed.astype(bf16))
         mixed = to_experts(mixed_pieces)
-    owner_mixed = exchange(mixed)[0].reshape(-1, part)
-    attn_slots = combine(dot(owner_mixed, w_output[0]).astype(bf16), group, n_ep, n_ws, collective_id=11)[0]
+    if fused:
+        owner_mixed, attn_slots = run_jobs(
+            [exchange_combine_job(mixed, w_output[0], dot, n_ws)], [], 11, "exchange_output"
+        )
+        owner_mixed, attn_slots = owner_mixed.reshape(-1, part), attn_slots.reshape(-1, width)
+    else:
+        owner_mixed = exchange(mixed)[0].reshape(-1, part)
+        output_part = dot(owner_mixed, w_output[0]).astype(bf16)
+        attn_slots = combine(output_part, group, n_ep, n_ws)[0]
 
     def weighted(pairs, gates, slot_values):
         return sum(gates[:, k : k + 1] * t_dot(pairs[k], slot_values) for k in range(2))
@@ -1356,33 +1472,34 @@
         ).astype(bf16)
         query_grads = to_experts(query_pieces)
     if fused:
-        owner_grad_query, grad_kv_rows = run_jobs(
-            [exchange_job(query_grads), swap_job(grad_kv_rows)], [], 14, "exchange_grad_kv"
+        owner_grad_query, normed_back, grad_kv_rows = run_jobs(
+            [exchange_combine_job(query_grads, w_query[0], dot_t, n_ws), swap_job(grad_kv_rows)],
+            [],
+            14,
+            "exchange_back",
         )
         owner_grad_query = owner_grad_query.reshape(-1, part)
+        normed_back = normed_back.reshape(-1, width)
         grad_kv_rows = grad_kv_rows.reshape(2 * sequence, -1)
     else:
         owner_grad_query = exchange(query_grads)[0].reshape(-1, part)
     grad_kv = t_dot(normed_sequence, grad_kv_rows)
     from_kv = dot_t(grad_kv_rows, kv_own).astype(bf16)
-    back_normed = dot_t(owner_grad_query, w_query[0]).astype(bf16)
     if fused:
-        normed_back, piece, from_kv, grad_query = run_jobs(
+        piece, from_kv, grad_query = run_jobs(
             [
-                combine_job(back_normed.reshape(n_ep, n_ws, ROWS, width)),
                 reduce_weights_job(
                     grad_kv.astype(bf16), from_kv.reshape(2, n_ws, local_tokens, width), n_ep
-                ),
+                )
             ],
             [grad_job(rows_one, owner_grad_query)],
             9,
-            "combine_weights",
+            "reduce_weights",
         )
-        normed_back = normed_back.reshape(-1, width)
     else:
-        normed_back, grad_query = combine(
-            back_normed, group, n_ep, n_ws, (grad_job, rows_one, owner_grad_query)
-        )
+        back_normed = dot_t(owner_grad_query, w_query[0]).astype(bf16)
+        normed_back = combine(back_normed, group, n_ep, n_ws)[0]
+        grad_query = t_dot(rows_one, owner_grad_query)
     if fused:
         back = [(b, a) for a, b in there]
         grad_kv_shard = lax.ppermute(piece, ("ep", "ws"), back).astype(f32)

time: 743 us -> 726 us (0.977)
  matrix products: 54 us -> 45.9 us
    pallas_call x12 -> x11, Pallas kernels: 558 us -> 551 us  [run_jobs(): pl.pallas_call(kernel, out_shape=outs, in_specs=[ANY] * len(args), out_sp...]
    dot_general x9 -> x8, matrix products: 23.8 us -> 17.9 us  [dot(): return jnp.dot(a, b, preferred_element_type=f32)]
    dot_general x3 -> x2, matrix products: 16.9 us -> 13.6 us  [dot_t(): lax.dot_general(a, b, (((1,), (1,)), ((), ())), preferred_element_type=f32)]
    unnamed x52 -> x32, local copies, waits for them, and re-layouts: 34.3 us -> 33.5 us
where the time goes in v7:
time: 726 us; the launch traced here: 720 us
  Pallas kernels  611 us (84%)
  matrix products  45.9 us (6%)
  local copies, waits for them, and re-layouts  37.3 us (5%)
  other arithmetic  9.31 us (1%)
  starting transfers between devices  7.9 us (1%)
  waiting for transfers between devices  7.67 us (1%)
    pallas_call x11, Pallas kernels, run_jobs(): pl.pallas_call(kernel, out_shape=outs, in_specs=[ANY] * len(args), out_sp...  551 us
    unnamed x32, local copies, waits for them, and re-layouts  33.5 us
    pallas_call x1, Pallas kernels, attend_back_call(): pl.pallas_call(functools.partial(attend_back_kernel, spans), out_shape=[j...  18.4 us
    dot_general x8, matrix products, dot(): return jnp.dot(a, b, preferred_element_type=f32)  17.9 us
    pallas_call x1, Pallas kernels, gather_call(): pl.pallas_call(functools.partial(gather_kernel, n, n_ws), out_shape=jax.S...  16 us
  transfers between devices with their start and end apart: 2, of which 1 were waited for; matrix products, arithmetic and copies ran while one was open for 2% of the time, Pallas kernels for 2%

profile of v7, /device:TPU:1, one launch (start us, length us, event | category | flops | bytes accessed | tf_op | source)
XLA Modules:
  0.0 720.4 jit_solution(3800352288322682505)
XLA Ops:
  0.7 4.6 collective-permute-start
  6.5 16.0 %gather_gains.1 = f32[8,4,1,128]{3,2,1,0:T(1,128)} custom-call(f32[1,128]{1,0:T(1,128)} %maximum_convert_fusion.own), custom_call_target="tpu_custom_call" | custom-call | tf_op jit(solution)/shard_map/gather_gains/pallas_call | solution.py:1112
  34.1 71.6 %dispatch_weights.1 = (bf16[8,4,40,2048]{3,2,1,0:T(8,128)(2,1)}, bf16[2048,512]{1,0:T(8,128)(2,1)}, bf16[2,4,128,2048]{3,2,1,0:T(8,128)(2,1)}, bf16[2048,1408]{1,0:T(8,128)(2,1)}, bf16[2048,1408]{1,0:T(8,128)(2,1)}) custom-call(bf16[8,40,2048]{2,1,0:T(8,128)(2,1)} %bitcast.101, bf16[2048,128]{1,0:T(8,128)(2,1)} %copy-done.10, bf16[128,2048]{1,0:T(8,128)(2,1)} %copy-done.5, ...), custom_call_target="tpu_custom_call" | custom-call | tf_op jit(solution)/shard_map/dispatch_weights/pallas_call | solution.py:107
  105.8 6.3 convolution_convert_fusion.6
  112.1 4.0 convolution_convert_fusion.3
  116.0 28.8 %exchange_kv.1 = (bf16[8,160,512]{2,1,0:T(8,128)(2,1)}, bf16[2,512,512]{2,1,0:T(8,128)(2,1)}) custom-call(bf16[8,160,512]{2,1,0:T(8,128)(2,1)} %bitcast.112, bf16[2,512,512]{2,1,0:T(8,128)(2,1)} %bitcast.116), custom_call_target="tpu_custom_call" | custom-call | tf_op jit(solution)/shard_map/exchange_kv/pallas_call | solution.py:107
  144.9 13.4 %attend.1 = bf16[8,4,40,512]{3,2,1,0:T(8,128)(2,1)} custom-call(bf16[8,4,40,512]{3,2,1,0:T(8,128)(2,1)} %bitcast.91, bf16[2,512,512]{2,1,0:T(8,128)(2,1)} %get-tuple-element.45.kv_ref), custom_call_target="tpu_custom_call" | custom-call | tf_op jit(solution)/shard_map/attend/pallas_call | solution.py:1040
  158.3 62.9 %exchange_output.1 = (bf16[8,160,512]{2,1,0:T(8,128)(2,1)}, bf16[8,40,2048]{2,1,0:T(8,128)(2,1)}) custom-call(bf16[8,160,512]{2,1,0:T(8,128)(2,1)} %bitcast.93, bf16[512,2048]{1,0:T(8,128)(2,1)} %bitcast.107), custom_call_target="tpu_custom_call" | custom-call | tf_op jit(solution)/shard_map/exchange_output/pallas_call | solution.py:107
  225.4 46.9 %dispatch.1 = bf16[8,4,40,2048]{3,2,1,0:T(8,128)(2,1)} custom-call(bf16[8,40,2048]{2,1,0:T(8,128)(2,1)} %bitcast.100), custom_call_target="tpu_custom_call" | custom-call | tf_op jit(solution)/shard_map/dispatch/pallas_call | solution.py:107
  272.4 55.2 %dispatch_ffn.1 = (bf16[8,4,40,2048]{3,2,1,0:T(8,128)(2,1)}, f32[1280,1408]{1,0:T(8,128)}, f32[1280,1408]{1,0:T(8,128)}, bf16[1280,1408]{1,0:T(8,128)(2,1)}, bf16[1280,2048]{1,0:T(8,128)(2,1)}) custom-call(bf16[8,40,2048]{2,1,0:T(8,128)(2,1)} %bitcast.86, bf16[1280,2048]{1,0:T(8,128)(2,1)} %bitcast.77, bf16[2048,1408]{1,0:T(8,128)(2,1)} %get-tuple-element.47.refs_2_.refs_4_, ...), custom_call_target="tpu_custom_call" | custom-call | tf_op jit(solution)/shard_map/dispatch_ffn/pallas_call | solution.py:107
  327.6 54.8 %combine_ffn_back.1 = (bf16[8,40,2048]{2,1,0:T(8,128)(2,1)}, bf16[1280,1408]{1,0:T(8,128)(2,1)}, bf16[1280,1408]{1,0:T(8,128)(2,1)}, bf16[1280,2048]{1,0:T(8,128)(2,1)}) custom-call(bf16[8,4,40,2048]{3,2,1,0:T(8,128)(2,1)} %bitcast.90, bf16[1280,2048]{1,0:T(8,128)(2,1)} %bitcast.82, f32[1280,1408]{1,0:T(8,128)} %get-tuple-element.51.refs_2_, ...), custom_call_target="tpu_custom_call" | custom-call | tf_op jit(solution)/shard_map/combine_ffn_back/pallas_call | solution.py:107
  382.4 46.0 %combine_grad_out.1 = (bf16[8,40,2048]{2,1,0:T(8,128)(2,1)}, f32[1408,2048]{1,0:T(8,128)}) custom-call(bf16[8,4,40,2048]{3,2,1,0:T(8,128)(2,1)} %bitcast.89, bf16[1280,1408]{1,0:T(8,128)(2,1)} %get-tuple-element.55.refs_1_, bf16[1280,2048]{1,0:T(8,128)(2,1)} %bitcast.83), custom_call_target="tpu_custom_call" | custom-call | tf_op jit(solution)/shard_map/combine_grad_out/pallas_call | solution.py:107
  432.9 43.4 %dispatch_grad_in.1 = (bf16[8,4,40,2048]{3,2,1,0:T(8,128)(2,1)}, f32[2048,2,1408]{2,1,0:T(2,128)}) custom-call(bf16[8,40,2048]{2,1,0:T(8,128)(2,1)} %bitcast.102, bf16[1280,2048]{1,0:T(8,128)(2,1)} %bitcast.78, bf16[1280,1408]{1,0:T(8,128)(2,1)} %get-tuple-element.57.refs_2_, bf16[1280,1408]{1,0:T(8,128)(2,1)} %get-tuple-element.58.refs_3_), custom_call_target="tpu_custom_call" | custom-call | tf_op jit(solution)/shard_map/dispatch_grad_in/pallas_call | solution.py:107
  476.4 7.1 convolution_convert_fusion.2
  483.5 25.5 %exchange_grad_output.1 = (bf16[8,160,512]{2,1,0:T(8,128)(2,1)}, f32[512,2048]{1,0:T(8,128)}) custom-call(bf16[8,160,512]{2,1,0:T(8,128)(2,1)} %bitcast.115, bf16[1280,512]{1,0:T(8,128)(2,1)} %bitcast.114, bf16[1280,2048]{1,0:T(8,128)(2,1)} %bitcast.99), custom_call_target="tpu_custom_call" | custom-call | tf_op jit(solution)/shard_map/exchange_grad_output/pallas_call | solution.py:107
  509.0 18.4 %attend_back.1 = (bf16[8,4,40,512]{3,2,1,0:T(8,128)(2,1)}, bf16[2,512,512]{2,1,0:T(8,128)(2,1)}) custom-call(bf16[8,4,40,512]{3,2,1,0:T(8,128)(2,1)} %bitcast.92, bf16[8,4,40,512]{3,2,1,0:T(8,128)(2,1)} %bitcast.109, bf16[2,512,512]{2,1,0:T(8,128)(2,1)} %get-tuple-element.45.kv_ref), custom_call_target="tpu_custom_call" | custom-call | tf_op jit(solution)/shard_map/attend_back/pallas_call | solution.py:1075
  527.4 67.5 %exchange_back.1 = (bf16[8,160,512]{2,1,0:T(8,128)(2,1)}, bf16[8,40,2048]{2,1,0:T(8,128)(2,1)}, bf16[2,512,512]{2,1,0:T(8,128)(2,1)}) custom-call(bf16[8,160,512]{2,1,0:T(8,128)(2,1)} %bitcast.113, bf16[2048,512]{1,0:T(8,128)(2,1)} %bitcast.106, bf16[2,512,512]{2,1,0:T(8,128)(2,1)} %get-tuple-element.63.refs_2_), custom_call_target="tpu_custom_call" | custom-call | tf_op jit(solution)/shard_map/exchange_back/pallas_call | solution.py:107
  595.0 6.4 convolution_convert_fusion
  601.4 3.8 convolution_convert_fusion.1.refs_0_
  605.2 47.8 %reduce_weights.1 = (bf16[2048,128]{1,0:T(8,128)(2,1)}, bf16[128,2048]{1,0:T(8,128)(2,1)}, f32[2048,512]{1,0:T(8,128)}) custom-call(bf16[2048,512]{1,0:T(8,128)(2,1)} %convolution_convert_fusion.1.refs_0_, bf16[2,4,128,2048]{3,2,1,0:T(8,128)(2,1)} %bitcast.103, bf16[1280,2048]{1,0:T(8,128)(2,1)} %bitcast.87, bf16[1280,512]{1,0:T(8,128)(2,1)} %bitcast.108), custom_call_target="tpu_custom_call" | custom-call | tf_op jit(solution)/shard_map/reduce_weights/pallas_call | solution.py:107
  657.0 12.6 %reduce_gains.1 = f32[1,128]{1,0:T(1,128)} custom-call(f32[8,4,1,128]{3,2,1,0:T(1,128)} %reshape.182.parts), custom_call_target="tpu_custom_call" | custom-call | tf_op jit(solution)/shard_map/reduce_gains/pallas_call | solution.py:1151
  678.6 7.7 %collective-permute-done.1 = bf16[2048,128]{1,0:T(8,128)(2,1)S(1)} collective-permute-done((bf16[2048,128]{1,0:T(8,128)(2,1)}, bf16[2048,128]{1,0:T(8,128)(2,1)S(1)}, u32[]{:S(2)}, u32[]{:S(2)}) %collective-permute-start.1) | collective-permute-done | bytes 524320 | tf_op jit(solution)/shard_map/ppermute | solution.py:1505
  693.0 16.3 %copy.30 = f32[1,2048,2,1408]{3,2,1,0:T(2,128)} copy(f32[1,2048,2,1408]{3,2,1,0:T(2,128)} %bitcast.81) | data formatting | bytes 46137344
  709.4 10.6 %copy.31 = f32[1,1408,2048]{2,1,0:T(8,128)} copy(f32[1,1408,2048]{2,1,0:T(8,128)} %bitcast.84) | data formatting | bytes 23068672
  (71 shorter events, 41.2 us)
Async XLA Ops:
  0.6 30.4 %copy-start.4 = (bf16[128,2048]{1,0:T(8,128)(2,1)S(1)}, bf16[128,2048]{1,0:T(8,128)(2,1)}, u32[]{:S(2)}) copy-start(bf16[128,2048]{1,0:T(8,128)(2,1)} %param.29) | copy-start | bytes 1572868
  0.7 32.7 %collective-permute-start = (bf16[2048,128]{1,0:T(8,128)(2,1)}, bf16[2048,128]{1,0:T(8,128)(2,1)S(1)}, u32[]{:S(2)}, u32[]{:S(2)}) collective-permute-start(bf16[2048,128]{1,0:T(8,128)(2,1)} %param.18), channel_id=1, source_target_pairs={{0,0},{1,4},{2,8},{3,12},{4,1},{5,5},{6,9},{7,13},{8,2},{9,6},{10,... | collective-permute-start | bytes 1572872 | tf_op jit(solution)/shard_map/ppermute | solution.py:1294
  29.5 2.2 copy-start.5
  29.5 2.2 copy-start.11
  33.3 0.8 copy-start.10
  105.7 6.3 copy-start.1
  105.8 6.3 copy-start.9
  158.3 64.9 %copy-start = (bf16[128,2048]{1,0:T(8,128)(2,1)S(1)}, bf16[128,2048]{1,0:T(8,128)(2,1)}, u32[]{:S(2)}) copy-start(bf16[128,2048]{1,0:T(8,128)(2,1)} %param.15) | copy-start | bytes 1572868
  221.2 1.9 copy-start.3
  595.0 6.5 copy-start.12
  595.0 6.5 copy-start.13
  669.6 6.4 copy-start.2
  670.9 15.4 %collective-permute-start.1 = (bf16[2048,128]{1,0:T(8,128)(2,1)}, bf16[2048,128]{1,0:T(8,128)(2,1)S(1)}, u32[]{:S(2)}, u32[]{:S(2)}) collective-permute-start(bf16[2048,128]{1,0:T(8,128)(2,1)} %get-tuple-element.68), channel_id=1, source_target_pairs={{0,0},{4,1},{8,2},{12,3},{1,4},{5,5},{9,6},{13,7},{2,8},{6,9},{10,... | collective-permute-start | bytes 1572872 | tf_op jit(solution)/shard_map/ppermute | solution.py:1505
  676.0 1.3 copy-start.8
  677.3 10.0 %copy-start.7 = (f32[2048,512]{1,0:T(8,128)S(1)}, f32[2048,512]{1,0:T(8,128)}, u32[]{:S(2)}) copy-start(f32[2048,512]{1,0:T(8,128)} %get-tuple-element.69) | copy-start | bytes 12582916
  687.3 3.7 copy-start.6

commit v8 on v7

--- a/solution.py
+++ b/solution.py
@@ -763,6 +763,109 @@
     )
 
 
+def dispatch_exchange_job(rows, weight, product, n_ws):
+    n, count, width = rows.shape
+    turned = weight.shape[1] == width
+    narrow = weight.shape[0] if turned else weight.shape[1]
+
+    def body(
+        rows, w_hbm, out, moved, w_ref, own, here, flat, res, load_sem, ep_s, ep_r, y_s, y_r, c_s, c_r, x_s, x_r,
+        b_s, b_r
+    ):
+        e, w = lax.axis_index("ep"), lax.axis_index("ws")
+        twin, other = flip(w, 1), flip(w, 2)
+        places = [e] + [flip(e, k) for k in range(1, n)]
+        weights = pltpu.make_async_copy(w_hbm, w_ref, load_sem.at[2])
+        weights.start()
+        first, over_y, to_twin, relayed, back, stores = [], [], [], [], [], []
+        for i, s in enumerate(places[1:]):
+            first.append(remote(rows.at[s], out.at[e, w], ep_s.at[i], ep_r.at[i], (s, w)))
+            first[i].start()
+        load = pltpu.make_async_copy(rows.at[e], own, load_sem.at[0])
+        load.start()
+
+        def arrive(j):
+            place = out.at[places[j], w]
+            block = place if j else rows.at[e]
+            if j:
+                first[j - 1].wait_recv()
+            over_y.append(remote(block, place, y_s.at[j], y_r.at[j], (e, other)))
+            over_y[j].start()
+            to_twin.append(remote(block, place, c_s.at[j], c_r.at[j], (e, twin)))
+            to_twin[j].start()
+            if j == 0:
+                load.wait()
+                stores.append(pltpu.make_async_copy(own, place, load_sem.at[1]))
+                stores[0].start()
+
+        def relay(j):
+            over_y[j].wait_recv()
+            block = out.at[places[j], other]
+            relayed.append(remote(block, block, x_s.at[j], x_r.at[j], (e, twin)))
+            relayed[j].start()
+
+        def multiply(j):
+            to_twin[j].wait_recv()
+            relayed[j].wait_recv()
+            if j == 0:
+                stores[0].wait()
+                weights.wait()
+            source = pltpu.make_async_copy(out.at[places[j]], here, load_sem.at[0])
+            source.start()
+            source.wait()
+            flat[...] = here[...].astype(f32).reshape(n_ws * count, width).astype(bf16)
+
+            def tile(at, columns):
+                tall = pl.ds(at, columns)
+                part = product(flat[...], w_ref[tall, :] if turned else w_ref[:, tall])
+                res[j, :, tall] = part.astype(bf16)
+
+            column_tiles(narrow, tile)
+
+        def send(j):
+            if j:
+                back.append(
+                    remote(res.at[j], moved.at[e], b_s.at[j - 1], b_r.at[j - 1], (places[j], w))
+                )
+                back[j - 1].start()
+            else:
+                stores.append(pltpu.make_async_copy(res.at[0], moved.at[e], load_sem.at[1]))
+                stores[1].start()
+
+        for t in range(n + 3):
+            for lag, stage in enumerate((arrive, relay, multiply, send)):
+                if 0 <= t - lag < n:
+                    stage(t - lag)
+            yield
+        for copy in first + over_y + to_twin + relayed:
+            copy.wait_send()
+        for copy in back + stores[1:]:
+            copy.wait()
+
+    return Job(
+        [rows, weight],
+        [
+            jax.ShapeDtypeStruct((n, n_ws, count, width), bf16),
+            jax.ShapeDtypeStruct((n, n_ws * count, narrow), bf16),
+        ],
+        [
+            pltpu.VMEM(weight.shape, bf16),
+            pltpu.VMEM((count, width), bf16),
+            pltpu.VMEM((n_ws, count, width), bf16),
+            pltpu.VMEM((n_ws * count, width), bf16),
+            pltpu.VMEM((n, n_ws * count, narrow), bf16),
+            DMA((3,)),
+            DMA((n - 1,)),
+            DMA((n - 1,)),
+        ]
+        + [DMA((n,)) for _ in range(6)]
+        + [DMA((n - 1,)), DMA((n - 1,))],
+        n + 3,
+        body,
+        [(k, 0) for k in range(1, n)] + [(0, 1), (0, 2)],
+    )
+
+
 def gather_weights_job(mine, normed, n, n_ws):
     rows, block = mine.shape
     routes = [(4, 0), (2, 0), (2, 4)]
@@ -1086,38 +1189,45 @@
     )(queries, grads, kv)
 
 
-def gather_kernel(n, n_ws, own, out, load_sem, w_s, w_r, ep_s, ep_r):
-    e, w = lax.axis_index("ep"), lax.axis_index("ws")
-    beside = [flip(w, k) for k in range(1, n_ws)]
-    across = [flip(e, k) for k in far_first(n)]
-    greet([(e, p) for p in beside] + [(s, w) for s in across])
-    keep = pltpu.make_async_copy(own, out.at[e, w], load_sem)
-    keep.start()
-    first = []
-    for i, p in enumerate(beside):
-        first.append(remote(own, out.at[e, w], w_s.at[i], w_r.at[i], (e, p)))
-        first[-1].start()
-    keep.wait()
-    for copy in first:
-        copy.wait()
-    second = []
-    for i, s in enumerate(across):
-        second.append(remote(out.at[e], out.at[e], ep_s.at[i], ep_r.at[i], (s, w)))
-        second[-1].start()
-    for copy in second:
-        copy.wait()
-
-
-def gather_call(own, n, n_ws):
-    return pl.pallas_call(
-        functools.partial(gather_kernel, n, n_ws),
-        out_shape=jax.ShapeDtypeStruct((n, n_ws) + own.shape, own.dtype),
-        in_specs=[VM],
-        out_specs=VM,
-        scratch_shapes=[DMA, DMA((n_ws - 1,)), DMA((n_ws - 1,)), DMA((n - 1,)), DMA((n - 1,))],
-        compiler_params=pltpu.CompilerParams(collective_id=3, has_side_effects=True),
-        name="gather_gains",
-    )(own)
+def gather_gains_job(own, n, n_ws):
+    def body(own, out, held, load_sem, w_s, w_r, ep_s, ep_r):
+        e, w = lax.axis_index("ep"), lax.axis_index("ws")
+        first = []
+        for i in range(n_ws - 1):
+            place = (e, flip(w, i + 1))
+            first.append(remote(own, out.at[e, w], w_s.at[i], w_r.at[i], place))
+            first[i].start()
+        load = fetch(((own, held),), load_sem)[0]
+        load.wait()
+        store = fetch(((held, out.at[e, w]),), load_sem)[0]
+        yield
+        store.wait()
+        for copy in first:
+            copy.wait()
+        second = []
+        for i in range(n - 1):
+            place = (flip(e, i + 1), w)
+            second.append(remote(out.at[e], out.at[e], ep_s.at[i], ep_r.at[i], place))
+            second[i].start()
+        yield
+        for copy in second:
+            copy.wait()
+
+    return Job(
+        [own],
+        [jax.ShapeDtypeStruct((n, n_ws) + own.shape, own.dtype)],
+        [
+            pltpu.VMEM(own.shape, own.dtype),
+            DMA((1,)),
+            DMA((n_ws - 1,)),
+            DMA((n_ws - 1,)),
+            DMA((n - 1,)),
+            DMA((n - 1,)),
+        ],
+        2,
+        body,
+        [(k, 0) for k in range(1, n)] + [(0, k) for k in range(1, n_ws)],
+    )
 
 
 def reduce_kernel(n, n_ws, parts, out, held, all_parts, load_sem, w_s, w_r, ep_s, ep_r):
@@ -1274,12 +1384,9 @@
     place = lax.axis_index("ws")
     scale = HEAD_SIZE ** (-0.5)
 
-    fused = small(n_ep) and key_value_weight.shape[1] == HEAD_SIZE
-    short = fused and gain_attn.shape[0] == 64
-    if short:
-        gains = jnp.concatenate([gain_attn, gain_ffn], 0).astype(f32)[None]
-        gains = gather_call(gains, n_ep, n_ws).reshape(n_ep * n_ws, 2, -1)
-        gain_one, gain_two = gains[:, 0].reshape(-1), gains[:, 1].reshape(-1)
+    fused = small(n_ep) and key_value_weight.shape[1] == HEAD_SIZE and gain_attn.shape[0] == 64
+    if fused:
+        own_gains = jnp.concatenate([gain_attn, gain_ffn], 0).astype(f32)[None]
     else:
         gain_one = lax.all_gather(gain_attn, ("ep", "ws"), axis=0, tiled=True).astype(f32)
         gain_two = lax.all_gather(gain_ffn, ("ep", "ws"), axis=0, tiled=True).astype(f32)
@@ -1300,7 +1407,7 @@
     inputs = x_in.astype(f32)
     inverse_one = lax.rsqrt(jnp.mean(inputs * inputs, -1, keepdims=True) + EPS)
     unit_one = inputs * inverse_one
-    normed = (unit_one * gain_one).astype(bf16)
+    normed = (unit_one if fused else unit_one * gain_one).astype(bf16)
     attn_pairs = slot_tables(route_attn, slot_attn)
     ffn_pairs = slot_tables(route_ffn, slot_ffn)
     attn_tokens = attn_pairs[0] + attn_pairs[1]
@@ -1308,17 +1415,21 @@
 
     slots_one = dot(attn_tokens, normed).astype(bf16)
     if fused:
-        rows_one, kv_own, normed_sequence, gate_weight, up_weight = run_jobs(
+        rows_one, kv_own, normed_sequence, gains, gate_weight, up_weight = run_jobs(
             [
                 dispatch_job(slots_one.reshape(n_ep, ROWS, width), n_ws),
                 gather_weights_job(mine, normed, n_ep, n_ws),
+                gather_gains_job(own_gains, n_ep, n_ws),
             ],
             [split_job(w_in[0])],
             10,
             "dispatch_weights",
         )
-        rows_one = rows_one.reshape(-1, width)
-        normed_sequence = normed_sequence.reshape(2 * sequence, width)
+        gains = gains.reshape(n_ep * n_ws, 2, -1)
+        gain_one, gain_two = gains[:, 0].reshape(-1), gains[:, 1].reshape(-1)
+        rows_one = (rows_one.reshape(-1, width).astype(f32) * gain_one).astype(bf16)
+        normed_sequence = normed_sequence.reshape(2 * sequence, width).astype(f32) * gain_one
+        normed_sequence = normed_sequence.astype(bf16)
     else:
         if plain:
             kv_own = lax.all_gather(mine, "ep", axis=1, tiled=True)
@@ -1430,20 +1541,21 @@
     grad_normed_two = t_dot(ffn_tokens, back_slots)
     grad_hidden_norm, grad_gain_two = norm_back(grad_normed_two, unit_two, inverse_two, gain_two)
     grad_hidden = grad_out + grad_hidden_norm
-    owner_grad, grad_first = dispatch(
-        to_slots(attn_pairs, gate_attn, grad_hidden),
-        group,
-        (pair_grad_job, expert_rows, grad_gate, grad_up),
-        collective_id=7,
-        name="dispatch_grad_in",
-    )
-    back_mixed = dot_t(owner_grad, w_output[0]).astype(bf16)
-    mixed_grads, grad_output = exchange(
-        back_mixed.reshape(n_ep, n_ws * ROWS, part),
-        (grad_job, owner_mixed, owner_grad),
-        collective_id=8,
-        name="exchange_grad_output",
-    )
+    attn_grads = to_slots(attn_pairs, gate_attn, grad_hidden)
+    if fused:
+        owner_grad, mixed_grads, grad_first = run_jobs(
+            [dispatch_exchange_job(attn_grads.reshape(n_ep, ROWS, width), w_output[0], dot_t, n_ws)],
+            [pair_grad_job(expert_rows, grad_gate, grad_up)],
+            7,
+            "dispatch_exchange",
+        )
+        owner_grad = owner_grad.reshape(-1, width)
+    else:
+        owner_grad = dispatch(attn_grads, group)[0]
+        grad_first = jnp.stack([t_dot(expert_rows, grad_gate), t_dot(expert_rows, grad_up)], 1)
+        back_mixed = dot_t(owner_grad, w_output[0]).astype(bf16)
+        mixed_grads = exchange(back_mixed.reshape(n_ep, n_ws * ROWS, part))[0]
+        grad_output = t_dot(owner_mixed, owner_grad)
 
     if fused:
         mixed_grads = mixed_grads.reshape(n_ep, n_ws, ROWS, part)
@@ -1472,9 +1584,9 @@
         ).astype(bf16)
         query_grads = to_experts(query_pieces)
     if fused:
-        owner_grad_query, normed_back, grad_kv_rows = run_jobs(
+        owner_grad_query, normed_back, grad_kv_rows, grad_output = run_jobs(
             [exchange_combine_job(query_grads, w_query[0], dot_t, n_ws), swap_job(grad_kv_rows)],
-            [],
+            [grad_job(owner_mixed, owner_grad)],
             14,
             "exchange_back",
         )
@@ -1520,7 +1632,7 @@
     grad_input_norm, grad_gain_one = norm_back(grad_normed, unit_one, inverse_one, gain_one)
     grad_input = grad_hidden + grad_input_norm
     gain_grads = jnp.stack([grad_gain_one, grad_gain_two], 0)
-    if short:
+    if fused:
         parts = gain_grads.reshape(2, n_ep, n_ws, -1).transpose(1, 2, 0, 3)
         gain_shards = reduce_call(parts.reshape(n_ep, n_ws, 1, -1)).reshape(2, -1)
     else:

time: 726 us -> 733 us (level); the launches traced: 720 us -> 719 us
  other arithmetic: 9.31 us -> 25.9 us
  Pallas kernels: 611 us -> 596 us
    convert_element_type x2 -> x6, other arithmetic: 2.48 us -> 19.1 us  [the longest x2 8.91 us: local(): normed_sequence = normed_sequence.astype(bf16)]
    pallas_call x1 -> x0, Pallas kernels: 16 us -> none  [gather_call(): pl.pallas_call(functools.partial(gather_kernel, n, n_ws), out_shape=jax.S...]
    pallas_call x11 -> x10, Pallas kernels: 551 us -> 553 us  [run_jobs(): pl.pallas_call(kernel, out_shape=outs, in_specs=[ANY] * len(args), out_sp...]
    unnamed x32 -> x38, local copies, waits for them, and re-layouts: 33.5 us -> 33.5 us
  transfers between devices with their start and end apart: 2 -> 2, of which waited for: 1 -> 2; matrix products, arithmetic and copies ran while one was open for 2% -> 2% of each run, Pallas kernels for 2% -> 0%
where the time goes in v8:
time: 733 us; the launch traced here: 719 us
  Pallas kernels  596 us (81%)
  matrix products  39.5 us (5%)
  local copies, waits for them, and re-layouts  37.3 us (5%)
  other arithmetic  25.9 us (4%)
  waiting for transfers between devices  10.9 us (1%)
  starting transfers between devices  8.27 us (1%)
    pallas_call x10, Pallas kernels, run_jobs(): pl.pallas_call(kernel, out_shape=outs, in_specs=[ANY] * len(args), out_sp...  553 us
    unnamed x38, local copies, waits for them, and re-layouts  33.5 us
    pallas_call x1, Pallas kernels, attend_back_call(): pl.pallas_call(functools.partial(attend_back_kernel, spans), out_shape=[j...  18.4 us
    dot_general x8, matrix products, dot(): return jnp.dot(a, b, preferred_element_type=f32)  17.3 us
    dot_general x7, matrix products, t_dot(): lax.dot_general(a, b, (((0,), (0,)), ((), ())), preferred_element_type=f32)  15.8 us
  transfers between devices with their start and end apart: 2, of which 2 were waited for; matrix products, arithmetic and copies ran while one was open for 2% of the time, Pallas kernels for 0%

profile of v8, /device:TPU:1, one launch (start us, length us, event | category | flops | bytes accessed | tf_op | source)
XLA Modules:
  0.0 719.3 jit_solution(7547208846647887545)
XLA Ops:
  0.7 4.6 collective-permute-start
  16.9 74.9 %dispatch_weights.1 = (bf16[8,4,40,2048]{3,2,1,0:T(8,128)(2,1)}, bf16[2048,512]{1,0:T(8,128)(2,1)}, bf16[2,4,128,2048]{3,2,1,0:T(8,128)(2,1)}, f32[8,4,1,128]{3,...) custom-call(bf16[8,40,2048]{2,1,0:T(8,128)(2,1)} %bitcast.107, bf16[2048,128]{1,0:T(8,128)(2,1)} %copy-done.11, ...), custom_call_target="tpu_custom_call" | custom-call | tf_op jit(solution)/shard_map/dispatch_weights/pallas_call | solution.py:107
  94.1 5.7 multiply_convert_fusion.1
  103.0 3.8 fusion.refs_2_
  106.8 3.8 multiply_convert_fusion
  110.7 5.6 convolution_convert_fusion.5
  116.3 4.0 convolution_convert_fusion.2
  120.3 30.1 %exchange_kv.1 = (bf16[8,160,512]{2,1,0:T(8,128)(2,1)}, bf16[2,512,512]{2,1,0:T(8,128)(2,1)}) custom-call(bf16[8,160,512]{2,1,0:T(8,128)(2,1)} %bitcast.118, bf16[2,512,512]{2,1,0:T(8,128)(2,1)} %bitcast.121), custom_call_target="tpu_custom_call" | custom-call | tf_op jit(solution)/shard_map/exchange_kv/pallas_call | solution.py:107
  150.4 13.4 %attend.1 = bf16[8,4,40,512]{3,2,1,0:T(8,128)(2,1)} custom-call(bf16[8,4,40,512]{3,2,1,0:T(8,128)(2,1)} %bitcast.97, bf16[2,512,512]{2,1,0:T(8,128)(2,1)} %get-tuple-element.47.kv_ref), custom_call_target="tpu_custom_call" | custom-call | tf_op jit(solution)/shard_map/attend/pallas_call | solution.py:1143
  163.8 63.2 %exchange_output.1 = (bf16[8,160,512]{2,1,0:T(8,128)(2,1)}, bf16[8,40,2048]{2,1,0:T(8,128)(2,1)}) custom-call(bf16[8,160,512]{2,1,0:T(8,128)(2,1)} %bitcast.99, bf16[512,2048]{1,0:T(8,128)(2,1)} %bitcast.92), custom_call_target="tpu_custom_call" | custom-call | tf_op jit(solution)/shard_map/exchange_output/pallas_call | solution.py:107
  231.2 46.6 %dispatch.1 = bf16[8,4,40,2048]{3,2,1,0:T(8,128)(2,1)} custom-call(bf16[8,40,2048]{2,1,0:T(8,128)(2,1)} %bitcast.106), custom_call_target="tpu_custom_call" | custom-call | tf_op jit(solution)/shard_map/dispatch/pallas_call | solution.py:107
  277.9 54.1 %dispatch_ffn.1 = (bf16[8,4,40,2048]{3,2,1,0:T(8,128)(2,1)}, f32[1280,1408]{1,0:T(8,128)}, f32[1280,1408]{1,0:T(8,128)}, bf16[1280,1408]{1,0:T(8,128)(2,1)}, bf16[1280,2048]{1,0:T(8,128)(2,1)}) custom-call(bf16[8,40,2048]{2,1,0:T(8,128)(2,1)} %bitcast.94, bf16[1280,2048]{1,0:T(8,128)(2,1)} %bitcast.81, bf16[2048,1408]{1,0:T(8,128)(2,1)} %get-tuple-element.49.refs_2_.refs_4_, ...), custom_call_target="tpu_custom_call" | custom-call | tf_op jit(solution)/shard_map/dispatch_ffn/pallas_call | solution.py:107
  332.0 55.5 %combine_ffn_back.1 = (bf16[8,40,2048]{2,1,0:T(8,128)(2,1)}, bf16[1280,1408]{1,0:T(8,128)(2,1)}, bf16[1280,1408]{1,0:T(8,128)(2,1)}, bf16[1280,2048]{1,0:T(8,128)(2,1)}) custom-call(bf16[8,4,40,2048]{3,2,1,0:T(8,128)(2,1)} %bitcast.96, bf16[1280,2048]{1,0:T(8,128)(2,1)} %bitcast.86, f32[1280,1408]{1,0:T(8,128)} %get-tuple-element.53.refs_2_, ...), custom_call_target="tpu_custom_call" | custom-call | tf_op jit(solution)/shard_map/combine_ffn_back/pallas_call | solution.py:107
  387.5 45.7 %combine_grad_out.1 = (bf16[8,40,2048]{2,1,0:T(8,128)(2,1)}, f32[1408,2048]{1,0:T(8,128)}) custom-call(bf16[8,4,40,2048]{3,2,1,0:T(8,128)(2,1)} %bitcast.95, bf16[1280,1408]{1,0:T(8,128)(2,1)} %get-tuple-element.57.refs_1_, bf16[1280,2048]{1,0:T(8,128)(2,1)} %bitcast.87), custom_call_target="tpu_custom_call" | custom-call | tf_op jit(solution)/shard_map/combine_grad_out/pallas_call | solution.py:107
  443.2 66.5 %dispatch_exchange.1 = (bf16[8,4,40,2048]{3,2,1,0:T(8,128)(2,1)}, bf16[8,160,512]{2,1,0:T(8,128)(2,1)}, f32[2048,2,1408]{2,1,0:T(2,128)}) custom-call(bf16[8,40,2048]{2,1,0:T(8,128)(2,1)} %bitcast.108, bf16[512,2048]{1,0:T(8,128)(2,1)} %bitcast.93, bf16[1280,2048]{1,0:T(8,128)(2,1)} %bitcast.82, bf16[1280,1408]{1,0:T(8,128)(2,1)} %get-tuple-element.59.refs_3_, ...), custom_call_target="tpu_custom_call" | custom-call | tf_op jit(solution)/shard_map/dispatch_exchange/pallas_call | solution.py:107
  509.6 18.4 %attend_back.1 = (bf16[8,4,40,512]{3,2,1,0:T(8,128)(2,1)}, bf16[2,512,512]{2,1,0:T(8,128)(2,1)}) custom-call(bf16[8,4,40,512]{3,2,1,0:T(8,128)(2,1)} %bitcast.98, bf16[8,4,40,512]{3,2,1,0:T(8,128)(2,1)} %bitcast.115, bf16[2,512,512]{2,1,0:T(8,128)(2,1)} %get-tuple-element.47.kv_ref), custom_call_target="tpu_custom_call" | custom-call | tf_op jit(solution)/shard_map/attend_back/pallas_call | solution.py:1178
  528.0 67.7 %exchange_back.1 = (bf16[8,160,512]{2,1,0:T(8,128)(2,1)}, bf16[8,40,2048]{2,1,0:T(8,128)(2,1)}, bf16[2,512,512]{2,1,0:T(8,128)(2,1)}, f32[512,2048]{1,0:T(8,128)}) custom-call(bf16[8,160,512]{2,1,0:T(8,128)(2,1)} %bitcast.120, bf16[2048,512]{1,0:T(8,128)(2,1)} %bitcast.113, bf16[2,512,512]{2,1,0:T(8,128)(2,1)} %get-tuple-element.63.refs_2_, ...), custom_call_target="tpu_custom_call" | custom-call | tf_op jit(solution)/shard_map/exchange_back/pallas_call | solution.py:107
  595.8 6.4 convolution_convert_fusion
  602.2 3.8 convolution_convert_fusion.1.refs_0_
  606.0 48.9 %reduce_weights.1 = (bf16[2048,128]{1,0:T(8,128)(2,1)}, bf16[128,2048]{1,0:T(8,128)(2,1)}, f32[2048,512]{1,0:T(8,128)}) custom-call(bf16[2048,512]{1,0:T(8,128)(2,1)} %convolution_convert_fusion.1.refs_0_, bf16[2,4,128,2048]{3,2,1,0:T(8,128)(2,1)} %bitcast.109, bf16[1280,2048]{1,0:T(8,128)(2,1)} %fusion.refs_2_, bf16[1280,512]{1,0:T(8,128)(2,1)} %bitcast.114), custom_call_target="tpu_custom_call" | custom-call | tf_op jit(solution)/shard_map/reduce_weights/pallas_call | solution.py:107
  657.9 11.0 %reduce_gains.1 = f32[1,128]{1,0:T(1,128)} custom-call(f32[8,4,1,128]{3,2,1,0:T(1,128)} %reshape.192.parts), custom_call_target="tpu_custom_call" | custom-call | tf_op jit(solution)/shard_map/reduce_gains/pallas_call | solution.py:1261
  675.3 9.9 %collective-permute-done.1 = bf16[2048,128]{1,0:T(8,128)(2,1)S(1)} collective-permute-done((bf16[2048,128]{1,0:T(8,128)(2,1)}, bf16[2048,128]{1,0:T(8,128)(2,1)S(1)}, u32[]{:S(2)}, u32[]{:S(2)}) %collective-permute-start.1) | collective-permute-done | bytes 524320 | tf_op jit(solution)/shard_map/ppermute | solution.py:1617
  691.9 16.3 %copy.30 = f32[1,2048,2,1408]{3,2,1,0:T(2,128)} copy(f32[1,2048,2,1408]{3,2,1,0:T(2,128)} %bitcast.85) | data formatting | bytes 46137344
  708.2 10.6 %copy.31 = f32[1,1408,2048]{2,1,0:T(8,128)} copy(f32[1,1408,2048]{2,1,0:T(8,128)} %bitcast.90) | data formatting | bytes 23068672
  (79 shorter events, 47.2 us)
Async XLA Ops:
  0.6 12.2 %copy-start.5 = (bf16[128,2048]{1,0:T(8,128)(2,1)S(1)}, bf16[128,2048]{1,0:T(8,128)(2,1)}, u32[]{:S(2)}) copy-start(bf16[128,2048]{1,0:T(8,128)(2,1)} %param.29) | copy-start | bytes 1572868
  0.7 15.5 %collective-permute-start = (bf16[2048,128]{1,0:T(8,128)(2,1)}, bf16[2048,128]{1,0:T(8,128)(2,1)S(1)}, u32[]{:S(2)}, u32[]{:S(2)}) collective-permute-start(bf16[2048,128]{1,0:T(8,128)(2,1)} %param.18), channel_id=1, source_target_pairs={{0,0},{1,4},{2,8},{3,12},{4,1},{5,5},{6,9},{7,13},{8,2},{9,6},{10,... | collective-permute-start | bytes 1572872 | tf_op jit(solution)/shard_map/ppermute | solution.py:1401
  9.9 5.2 copy-start.4
  9.9 3.5 copy-start.12
  16.1 0.8 copy-start.11
  94.1 5.7 copy-start
  94.1 8.9 %slice-start = ((s8[5242880]{0:T(1024)(128)(4,1)}), s8[4194304]{0:T(1024)(128)(4,1)S(1)}, s32[]{:S(2)}) async-start(s8[5242880]{0:T(1024)(128)(4,1)} %bitcast.88), calls=%async_computation | async-start | bytes 8388608
  99.8 3.2 slice-start.1
  106.8 3.9 copy-start.13
  110.7 5.6 copy-start.3
  110.7 5.6 copy-start.10
  163.8 65.1 %copy-start.1 = (bf16[128,2048]{1,0:T(8,128)(2,1)S(1)}, bf16[128,2048]{1,0:T(8,128)(2,1)}, u32[]{:S(2)}) copy-start(bf16[128,2048]{1,0:T(8,128)(2,1)} %param.15) | copy-start | bytes 1572868
  227.0 1.9 copy-start.2
  436.1 4.5 copy-start.9
  595.8 6.5 copy-start.6
  595.8 6.5 copy-start.14
  670.3 14.9 %collective-permute-start.1 = (bf16[2048,128]{1,0:T(8,128)(2,1)}, bf16[2048,128]{1,0:T(8,128)(2,1)S(1)}, u32[]{:S(2)}, u32[]{:S(2)}) collective-permute-start(bf16[2048,128]{1,0:T(8,128)(2,1)} %get-tuple-element.70), channel_id=1, source_target_pairs={{0,0},{4,1},{8,2},{12,3},{1,4},{5,5},{9,6},{13,7},{2,8},{6,9},{10,... | collective-permute-start | bytes 1572872 | tf_op jit(solution)/shard_map/ppermute | solution.py:1617
  673.9 12.3 %copy-start.8 = (f32[2048,512]{1,0:T(8,128)S(1)}, f32[2048,512]{1,0:T(8,128)}, u32[]{:S(2)}) copy-start(f32[2048,512]{1,0:T(8,128)} %get-tuple-element.71) | copy-start | bytes 12582916
  686.2 3.7 copy-start.7

commit v9 on v8

--- a/solution.py
+++ b/solution.py
@@ -52,11 +52,29 @@
     return sorted(range(1, n), key=lambda k: (-((k // 2).bit_length()), k))
 
 
-def greet(partners):
+def crossed():
+    e, w, n_ws = lax.axis_index("ep"), lax.axis_index("ws"), lax.axis_size("ws")
+    return (w + n_ws * (e // n_ws), e % n_ws), e % n_ws != w
+
+
+def greet(partners, crossing=False):
     barrier = pltpu.get_barrier_semaphore()
     for partner in partners:
         pl.semaphore_signal(barrier, inc=1, device_id=partner, device_id_type=MESH)
-    pl.semaphore_wait(barrier, len(partners))
+    if crossing:
+        partner, another = crossed()
+
+        @pl.when(another)
+        def _():
+            pl.semaphore_signal(barrier, inc=1, device_id=partner, device_id_type=MESH)
+            pl.semaphore_wait(barrier, len(partners) + 1)
+
+        @pl.when(jnp.logical_not(another))
+        def _():
+            pl.semaphore_wait(barrier, len(partners))
+
+    else:
+        pl.semaphore_wait(barrier, len(partners))
 
 
 def remote(src, dst, send, recv, device):
@@ -66,9 +84,9 @@
 
 
 class Job:
-    def __init__(self, args, outs, scratch, steps, body, partners=()):
+    def __init__(self, args, outs, scratch, steps, body, partners=(), crossing=False):
         self.args, self.outs, self.scratch, self.steps, self.body = args, outs, scratch, steps, body
-        self.partners = partners
+        self.partners, self.crossing = partners, crossing
 
 
 def run_jobs(jobs, fills, collective_id, name):
@@ -78,6 +96,7 @@
     scratch = [x for job in whole for x in job.scratch]
     turns = sorted((k / job.steps, i) for i, job in enumerate(jobs) for k in range(job.steps))
     partners = sorted({p for job in jobs for p in job.partners})
+    crossing = any(job.crossing for job in jobs)
 
     def kernel(*refs):
         bodies, at = [], [0, len(args), len(args) + len(outs)]
@@ -92,7 +111,7 @@
         for g in work:
             next(g)
         e, w = lax.axis_index("ep"), lax.axis_index("ws")
-        greet([(flip(e, p), flip(w, q)) for p, q in partners])
+        greet([(flip(e, p), flip(w, q)) for p, q in partners], crossing)
         done = 0
         for k, (_, i) in enumerate(turns):
             next(moves[i])
@@ -1008,7 +1027,7 @@
 
     def body(
         pieces, part, out, out_rows, mine, from_z, fourth, last_z, total, own, core, sum_y, from_y, total_near,
-        from_near, total_rows, load_sem, z_s, z_r, w_load, c_s, c_r, y_s, y_r, x_s, x_r, sem
+        from_near, total_rows, load_sem, z_s, z_r, w_load, c_s, c_r, y_s, y_r, x_s, x_r, sem, h_s, h_r
     ):
         e, w = lax.axis_index("ep"), lax.axis_index("ws")
         twin, other, last, near = flip(w, 1), flip(w, 2), flip(w, 3), flip(e, 1)
@@ -1070,17 +1089,37 @@
         to_near = remote(total_near, from_near, x_s, x_r, (near, w))
         to_near.start()
         yield
-        to_near.wait_recv()
-        add_blocks(total_rows, own.at[1, 1], core.at[1, 1], from_y.at[1], from_near)
         loads[1].wait()
         over_z[1].wait_recv()
         far.wait_recv()
         add_blocks(total, mine.at[1], from_z.at[1], last_z)
-        stores = fetch(((total_rows, out_rows), (total, out)), sem)
+        to_near.wait_recv()
+        add_blocks(total_rows, own.at[1, 1], core.at[1, 1], from_y.at[1], from_near)
+        partner, another = crossed()
+        home = remote(total, out, h_s, h_r, partner)
+        keep = pltpu.make_async_copy(total, out, sem.at[1])
+        store = pltpu.make_async_copy(total_rows, out_rows, sem.at[0])
+
+        @pl.when(another)
+        def _():
+            home.start()
+
+        @pl.when(jnp.logical_not(another))
+        def _():
+            keep.start()
+
+        store.start()
         for copy in over_z + list(cores.values()) + over_y + [far, to_near]:
             copy.wait_send()
-        for store in stores:
-            store.wait()
+        store.wait()
+
+        @pl.when(another)
+        def _():
+            home.wait()
+
+        @pl.when(jnp.logical_not(another))
+        def _():
+            keep.wait()
 
     one, rows_one = (rows, block), part.shape[2:]
     return Job(
@@ -1092,10 +1131,11 @@
         + [pltpu.VMEM((2,) + rows_one, bf16) for _ in range(2)]
         + [pltpu.VMEM(rows_one, bf16) for _ in range(3)]
         + [DMA((2,)), DMA((3,)), DMA((3,)), DMA((2, 2)), DMA((2, 2)), DMA((2, 2))]
-        + [DMA((2,)), DMA((2,)), DMA, DMA, DMA((2,))],
+        + [DMA((2,)), DMA((2,)), DMA, DMA, DMA((2,)), DMA, DMA],
         5,
         body,
         [(1, 0), (2, 0), (4, 0), (0, 1), (0, 2)],
+        True,
     )
 
 
@@ -1386,7 +1426,10 @@
 
     fused = small(n_ep) and key_value_weight.shape[1] == HEAD_SIZE and gain_attn.shape[0] == 64
     if fused:
-        own_gains = jnp.concatenate([gain_attn, gain_ffn], 0).astype(f32)[None]
+        gains = jnp.concatenate([gain_attn, gain_ffn], 0).astype(f32)[None]
+        gains = run_jobs([gather_gains_job(gains, n_ep, n_ws)], [], 3, "gather_gains")[0]
+        gains = gains.reshape(n_ep * n_ws, 2, -1)
+        gain_one, gain_two = gains[:, 0].reshape(-1), gains[:, 1].reshape(-1)
     else:
         gain_one = lax.all_gather(gain_attn, ("ep", "ws"), axis=0, tiled=True).astype(f32)
         gain_two = lax.all_gather(gain_ffn, ("ep", "ws"), axis=0, tiled=True).astype(f32)
@@ -1407,7 +1450,7 @@
     inputs = x_in.astype(f32)
     inverse_one = lax.rsqrt(jnp.mean(inputs * inputs, -1, keepdims=True) + EPS)
     unit_one = inputs * inverse_one
-    normed = (unit_one if fused else unit_one * gain_one).astype(bf16)
+    normed = (unit_one * gain_one).astype(bf16)
     attn_pairs = slot_tables(route_attn, slot_attn)
     ffn_pairs = slot_tables(route_ffn, slot_ffn)
     attn_tokens = attn_pairs[0] + attn_pairs[1]
@@ -1415,21 +1458,17 @@
 
     slots_one = dot(attn_tokens, normed).astype(bf16)
     if fused:
-        rows_one, kv_own, normed_sequence, gains, gate_weight, up_weight = run_jobs(
+        rows_one, kv_own, normed_sequence, gate_weight, up_weight = run_jobs(
             [
                 dispatch_job(slots_one.reshape(n_ep, ROWS, width), n_ws),
                 gather_weights_job(mine, normed, n_ep, n_ws),
-                gather_gains_job(own_gains, n_ep, n_ws),
             ],
             [split_job(w_in[0])],
             10,
             "dispatch_weights",
         )
-        gains = gains.reshape(n_ep * n_ws, 2, -1)
-        gain_one, gain_two = gains[:, 0].reshape(-1), gains[:, 1].reshape(-1)
-        rows_one = (rows_one.reshape(-1, width).astype(f32) * gain_one).astype(bf16)
-        normed_sequence = normed_sequence.reshape(2 * sequence, width).astype(f32) * gain_one
-        normed_sequence = normed_sequence.astype(bf16)
+        rows_one = rows_one.reshape(-1, width)
+        normed_sequence = normed_sequence.reshape(2 * sequence, width)
     else:
         if plain:
             kv_own = lax.all_gather(mine, "ep", axis=1, tiled=True)
@@ -1613,8 +1652,7 @@
         normed_back = combine(back_normed, group, n_ep, n_ws)[0]
         grad_query = t_dot(rows_one, owner_grad_query)
     if fused:
-        back = [(b, a) for a, b in there]
-        grad_kv_shard = lax.ppermute(piece, ("ep", "ws"), back).astype(f32)
+        grad_kv_shard = piece.astype(f32)
     elif plain:
         pieces = grad_kv.reshape(width, n_ep, HEAD_SIZE).transpose(1, 0, 2).astype(bf16)
         piece = lax.psum_scatter(pieces, "ep", scatter_dimension=0, tiled=False)

time: 733 us -> 714 us (0.974); the launches traced: 719 us -> 708 us
  Pallas kernels: 596 us -> 617 us
  other arithmetic: 25.9 us -> 10.5 us
  waiting for transfers between devices: 10.9 us -> 0.01 us
    pallas_call x10 -> x11, Pallas kernels: 553 us -> 576 us  [run_jobs(): pl.pallas_call(kernel, out_shape=outs, in_specs=[ANY] * len(args), out_sp...]
    convert_element_type x7 -> x3, other arithmetic: 20.1 us -> 4.72 us  [the longest x1 2.23 us: local(): grad_kv_shard = piece.astype(f32)]
    ppermute x1 -> x0, waiting for transfers between devices: 9.87 us -> none  [local(): grad_kv_shard = lax.ppermute(piece, ('ep', 'ws'), back).astype(f32)]
    unnamed x38 -> x30, local copies, waits for them, and re-layouts: 33.5 us -> 32.7 us
  transfers between devices with their start and end apart: 2 -> 1, of which waited for: 2 -> 0; matrix products, arithmetic and copies ran while one was open for 2% -> 2% of each run, Pallas kernels for 0% -> 2%
where the time goes in v9:
time: 714 us; the launch traced here: 708 us
  Pallas kernels  617 us (86%)
  matrix products  38.1 us (5%)
  local copies, waits for them, and re-layouts  36.5 us (5%)
  other arithmetic  10.5 us (1%)
    pallas_call x11, Pallas kernels, run_jobs(): pl.pallas_call(kernel, out_shape=outs, in_specs=[ANY] * len(args), out_sp...  576 us
    unnamed x30, local copies, waits for them, and re-layouts  32.7 us
    pallas_call x1, Pallas kernels, attend_back_call(): pl.pallas_call(functools.partial(attend_back_kernel, spans), out_shape=[j...  18.4 us
    dot_general x8, matrix products, dot(): return jnp.dot(a, b, preferred_element_type=f32)  17.9 us
    dot_general x7, matrix products, t_dot(): lax.dot_general(a, b, (((0,), (0,)), ((), ())), preferred_element_type=f32)  15.8 us
  transfers between devices with their start and end apart: 1, of which 0 were waited for; matrix products, arithmetic and copies ran while one was open for 2% of the time, Pallas kernels for 2%

profile of v9, /device:TPU:1, one launch (start us, length us, event | category | flops | bytes accessed | tf_op | source)
XLA Modules:
  0.0 708.1 jit_solution(6277962368507786717)
XLA Ops:
  0.7 4.6 collective-permute-start
  10.0 12.3 %gather_gains.1 = f32[8,4,1,128]{3,2,1,0:T(1,128)} custom-call(f32[1,128]{1,0:T(1,128)} %maximum_convert_fusion.refs_0_), custom_call_target="tpu_custom_call" | custom-call | tf_op jit(solution)/shard_map/gather_gains/pallas_call | solution.py:126
  29.6 71.4 %dispatch_weights.1 = (bf16[8,4,40,2048]{3,2,1,0:T(8,128)(2,1)}, bf16[2048,512]{1,0:T(8,128)(2,1)}, bf16[2,4,128,2048]{3,2,1,0:T(8,128)(2,1)}, bf16[2048,1408]{1,0:T(8,128)(2,1)}, bf16[2048,1408]{1,0:T(8,128)(2,1)}) custom-call(bf16[8,40,2048]{2,1,0:T(8,128)(2,1)} %bitcast.98, bf16[2048,128]{1,0:T(8,128)(2,1)} %collective-permute-done.refs_1_, ...), custom_call_target="tpu_custom_call" | custom-call | tf_op jit(solution)/shard_map/dispatch_weights/pallas_call | solution.py:126
  101.1 6.3 convolution_convert_fusion.5
  107.4 4.0 convolution_convert_fusion.2
  111.4 29.0 %exchange_kv.1 = (bf16[8,160,512]{2,1,0:T(8,128)(2,1)}, bf16[2,512,512]{2,1,0:T(8,128)(2,1)}) custom-call(bf16[8,160,512]{2,1,0:T(8,128)(2,1)} %bitcast.108, bf16[2,512,512]{2,1,0:T(8,128)(2,1)} %bitcast.111), custom_call_target="tpu_custom_call" | custom-call | tf_op jit(solution)/shard_map/exchange_kv/pallas_call | solution.py:126
  140.5 13.4 %attend.1 = bf16[8,4,40,512]{3,2,1,0:T(8,128)(2,1)} custom-call(bf16[8,4,40,512]{3,2,1,0:T(8,128)(2,1)} %bitcast.89, bf16[2,512,512]{2,1,0:T(8,128)(2,1)} %get-tuple-element.45.kv_ref), custom_call_target="tpu_custom_call" | custom-call | tf_op jit(solution)/shard_map/attend/pallas_call | solution.py:1183
  153.9 63.3 %exchange_output.1 = (bf16[8,160,512]{2,1,0:T(8,128)(2,1)}, bf16[8,40,2048]{2,1,0:T(8,128)(2,1)}) custom-call(bf16[8,160,512]{2,1,0:T(8,128)(2,1)} %bitcast.91, bf16[512,2048]{1,0:T(8,128)(2,1)} %bitcast.82), custom_call_target="tpu_custom_call" | custom-call | tf_op jit(solution)/shard_map/exchange_output/pallas_call | solution.py:126
  221.4 47.1 %dispatch.1 = bf16[8,4,40,2048]{3,2,1,0:T(8,128)(2,1)} custom-call(bf16[8,40,2048]{2,1,0:T(8,128)(2,1)} %bitcast.97), custom_call_target="tpu_custom_call" | custom-call | tf_op jit(solution)/shard_map/dispatch/pallas_call | solution.py:126
  268.5 54.7 %dispatch_ffn.1 = (bf16[8,4,40,2048]{3,2,1,0:T(8,128)(2,1)}, f32[1280,1408]{1,0:T(8,128)}, f32[1280,1408]{1,0:T(8,128)}, bf16[1280,1408]{1,0:T(8,128)(2,1)}, bf16[1280,2048]{1,0:T(8,128)(2,1)}) custom-call(bf16[8,40,2048]{2,1,0:T(8,128)(2,1)} %bitcast.84, bf16[1280,2048]{1,0:T(8,128)(2,1)} %bitcast.73, bf16[2048,1408]{1,0:T(8,128)(2,1)} %get-tuple-element.47.refs_2_.refs_4_, ...), custom_call_target="tpu_custom_call" | custom-call | tf_op jit(solution)/shard_map/dispatch_ffn/pallas_call | solution.py:126
  323.2 55.1 %combine_ffn_back.1 = (bf16[8,40,2048]{2,1,0:T(8,128)(2,1)}, bf16[1280,1408]{1,0:T(8,128)(2,1)}, bf16[1280,1408]{1,0:T(8,128)(2,1)}, bf16[1280,2048]{1,0:T(8,128)(2,1)}) custom-call(bf16[8,4,40,2048]{3,2,1,0:T(8,128)(2,1)} %bitcast.88, bf16[1280,2048]{1,0:T(8,128)(2,1)} %bitcast.78, f32[1280,1408]{1,0:T(8,128)} %get-tuple-element.51.refs_2_, ...), custom_call_target="tpu_custom_call" | custom-call | tf_op jit(solution)/shard_map/combine_ffn_back/pallas_call | solution.py:126
  378.4 46.1 %combine_grad_out.1 = (bf16[8,40,2048]{2,1,0:T(8,128)(2,1)}, f32[1408,2048]{1,0:T(8,128)}) custom-call(bf16[8,4,40,2048]{3,2,1,0:T(8,128)(2,1)} %bitcast.87, bf16[1280,1408]{1,0:T(8,128)(2,1)} %get-tuple-element.55.refs_1_, bf16[1280,2048]{1,0:T(8,128)(2,1)} %bitcast.79), custom_call_target="tpu_custom_call" | custom-call | tf_op jit(solution)/shard_map/combine_grad_out/pallas_call | solution.py:126
  429.0 64.8 %dispatch_exchange.1 = (bf16[8,4,40,2048]{3,2,1,0:T(8,128)(2,1)}, bf16[8,160,512]{2,1,0:T(8,128)(2,1)}, f32[2048,2,1408]{2,1,0:T(2,128)}) custom-call(bf16[8,40,2048]{2,1,0:T(8,128)(2,1)} %bitcast.99, bf16[512,2048]{1,0:T(8,128)(2,1)} %bitcast.83, bf16[1280,2048]{1,0:T(8,128)(2,1)} %bitcast.74, bf16[1280,1408]{1,0:T(8,128)(2,1)} %get-tuple-element.57.refs_3_, ...), custom_call_target="tpu_custom_call" | custom-call | tf_op jit(solution)/shard_map/dispatch_exchange/pallas_call | solution.py:126
  493.8 18.4 %attend_back.1 = (bf16[8,4,40,512]{3,2,1,0:T(8,128)(2,1)}, bf16[2,512,512]{2,1,0:T(8,128)(2,1)}) custom-call(bf16[8,4,40,512]{3,2,1,0:T(8,128)(2,1)} %bitcast.90, bf16[8,4,40,512]{3,2,1,0:T(8,128)(2,1)} %bitcast.105, bf16[2,512,512]{2,1,0:T(8,128)(2,1)} %get-tuple-element.45.kv_ref), custom_call_target="tpu_custom_call" | custom-call | tf_op jit(solution)/shard_map/attend_back/pallas_call | solution.py:1218
  512.2 67.2 %exchange_back.1 = (bf16[8,160,512]{2,1,0:T(8,128)(2,1)}, bf16[8,40,2048]{2,1,0:T(8,128)(2,1)}, bf16[2,512,512]{2,1,0:T(8,128)(2,1)}, f32[512,2048]{1,0:T(8,128)}) custom-call(bf16[8,160,512]{2,1,0:T(8,128)(2,1)} %bitcast.110, bf16[2048,512]{1,0:T(8,128)(2,1)} %bitcast.103, bf16[2,512,512]{2,1,0:T(8,128)(2,1)} %get-tuple-element.61.refs_2_, ...), custom_call_target="tpu_custom_call" | custom-call | tf_op jit(solution)/shard_map/exchange_back/pallas_call | solution.py:126
  579.4 6.3 convolution_convert_fusion.1.refs_0_
  585.8 4.4 convolution_convert_fusion
  593.5 65.3 %reduce_weights.1 = (bf16[2048,128]{1,0:T(8,128)(2,1)}, bf16[128,2048]{1,0:T(8,128)(2,1)}, f32[2048,512]{1,0:T(8,128)}) custom-call(bf16[2048,512]{1,0:T(8,128)(2,1)} %convolution_convert_fusion.1.refs_0_, bf16[2,4,128,2048]{3,2,1,0:T(8,128)(2,1)} %bitcast.100, bf16[1280,2048]{1,0:T(8,128)(2,1)} %bitcast.85, bf16[1280,512]{1,0:T(8,128)(2,1)} %bitcast.104), custom_call_target="tpu_custom_call" | custom-call | tf_op jit(solution)/shard_map/reduce_weights/pallas_call | solution.py:126
  661.4 8.7 %reduce_gains.1 = f32[1,128]{1,0:T(1,128)} custom-call(f32[8,4,1,128]{3,2,1,0:T(1,128)} %reshape.182.parts), custom_call_target="tpu_custom_call" | custom-call | tf_op jit(solution)/shard_map/reduce_gains/pallas_call | solution.py:1301
  671.4 2.2 convert_element_type.102
  675.0 2.1 copy.28
  678.7 2.0 copy.29
  680.7 16.3 %copy.30 = f32[1,2048,2,1408]{3,2,1,0:T(2,128)} copy(f32[1,2048,2,1408]{3,2,1,0:T(2,128)} %bitcast.77) | data formatting | bytes 46137344
  697.0 10.6 %copy.31 = f32[1,1408,2048]{2,1,0:T(8,128)} copy(f32[1,1408,2048]{2,1,0:T(8,128)} %bitcast.80) | data formatting | bytes 23068672
  (65 shorter events, 30.8 us)
Async XLA Ops:
  0.6 26.7 %copy-start.4 = (bf16[128,2048]{1,0:T(8,128)(2,1)S(1)}, bf16[128,2048]{1,0:T(8,128)(2,1)}, u32[]{:S(2)}) copy-start(bf16[128,2048]{1,0:T(8,128)(2,1)} %param.29) | copy-start | bytes 1572868
  0.7 29.0 %collective-permute-start = (bf16[2048,128]{1,0:T(8,128)(2,1)}, bf16[2048,128]{1,0:T(8,128)(2,1)}, u32[]{:S(2)}, u32[]{:S(2)}) collective-permute-start(bf16[2048,128]{1,0:T(8,128)(2,1)} %param.18), channel_id=1, source_target_pairs={{0,0},{1,4},{2,8},{3,12},{4,1},{5,5},{6,9},{7,13},{8,2},{9,6},{10,... | collective-permute-start | bytes 1572872 | tf_op jit(solution)/shard_map/ppermute | solution.py:1444
  25.8 2.2 copy-start.5
  25.8 2.2 copy-start.10
  101.1 6.3 copy-start.1
  101.1 6.3 copy-start.8
  153.9 65.2 %copy-start = (bf16[128,2048]{1,0:T(8,128)(2,1)S(1)}, bf16[128,2048]{1,0:T(8,128)(2,1)}, u32[]{:S(2)}) copy-start(bf16[128,2048]{1,0:T(8,128)(2,1)} %param.15) | copy-start | bytes 1572868
  217.1 1.9 copy-start.3
  579.4 6.4 copy-start.11
  579.4 6.4 copy-start.12
  590.3 1.9 copy-start.2
  593.5 65.3 %copy-start.9 = (bf16[8,40,2048]{2,1,0:T(8,128)(2,1)S(1)}, bf16[8,40,2048]{2,1,0:T(8,128)(2,1)}, u32[]{:S(2)}) copy-start(bf16[8,40,2048]{2,1,0:T(8,128)(2,1)} %get-tuple-element.64) | copy-start | bytes 3932164
  671.4 3.6 copy-start.7
  675.0 3.7 copy-start.6

commit v10 on v9

--- a/solution.py
+++ b/solution.py
@@ -337,7 +337,7 @@
     ):
         loads = fetch(((x_hbm, x_ref), (g_hbm, g_ref), (u_hbm, u_ref), (d_hbm, d_ref)), load_sem)
         yield
-        for load in loads:
+        for load in loads[:3]:
             load.wait()
         copies = []
         for i, (start, size) in enumerate(blocks_of(rows)):
@@ -358,6 +358,8 @@
 
             column_tiles(hidden, tile)
             yield
+            if i == 0:
+                loads[3].wait()
 
             def last(at, columns, slot=slot):
                 part = pl.ds(at, columns)
@@ -423,7 +425,7 @@
         x_hbm, gp_hbm, up_hbm, g_hbm, u_hbm, d_hbm, gate_out, up_out, out, x_ref, g_ref, u_ref, d_ref, pre, hid,
         res, load_sem, pre_sem, sem
     ):
-        loads = fetch(((x_hbm, x_ref), (g_hbm, g_ref), (u_hbm, u_ref), (d_hbm, d_ref)), load_sem)
+        loads = fetch(((x_hbm, x_ref), (d_hbm, d_ref), (g_hbm, g_ref), (u_hbm, u_ref)), load_sem)
 
         def load_pre(i):
             here = pl.ds(i * STEP, STEP)
@@ -435,7 +437,7 @@
         for copy in load_pre(0):
             copy.start()
         yield
-        for load in loads:
+        for load in loads[:2]:
             load.wait()
         copies = []
         steps = rows // STEP
@@ -459,6 +461,9 @@
 
             column_tiles(hidden, tile)
             yield
+            if i == 0:
+                for load in loads[2:]:
+                    load.wait()
 
             def last(at, columns, slot=slot):
                 part = pl.ds(at, columns)
@@ -1270,51 +1275,51 @@
     )
 
 
-def reduce_kernel(n, n_ws, parts, out, held, all_parts, load_sem, w_s, w_r, ep_s, ep_r):
-    e, w = lax.axis_index("ep"), lax.axis_index("ws")
-    beside = [flip(w, k) for k in range(1, n_ws)]
-    across = [flip(e, k) for k in far_first(n)]
-    greet([(e, p) for p in beside] + [(s, w) for s in across])
-    keep = pltpu.make_async_copy(parts.at[:, w], held.at[:, w], load_sem.at[0])
-    keep.start()
-    first = []
-    for i, p in enumerate(beside):
-        first.append(remote(parts.at[:, p], held.at[:, w], w_s.at[i], w_r.at[i], (e, p)))
-        first[-1].start()
-    keep.wait()
-    for copy in first:
-        copy.wait()
-    keep = pltpu.make_async_copy(held.at[e], all_parts.at[e], load_sem.at[1])
-    keep.start()
-    second = []
-    for i, s in enumerate(across):
-        second.append(remote(held.at[s], all_parts.at[e], ep_s.at[i], ep_r.at[i], (s, w)))
-        second[-1].start()
-    keep.wait()
-    for copy in second:
-        copy.wait()
-    out[...] = jnp.sum(jnp.sum(all_parts[...], 0), 0)
-
-
-def reduce_call(parts):
+def reduce_gains_job(parts):
     n, n_ws = parts.shape[:2]
-    return pl.pallas_call(
-        functools.partial(reduce_kernel, n, n_ws),
-        out_shape=jax.ShapeDtypeStruct(parts.shape[2:], parts.dtype),
-        in_specs=[VM],
-        out_specs=VM,
-        scratch_shapes=[
+
+    def body(parts, out, held, every, total, load_sem, w_s, w_r, ep_s, ep_r):
+        e, w = lax.axis_index("ep"), lax.axis_index("ws")
+        first, second = [], []
+        for i in range(n_ws - 1):
+            p = flip(w, i + 1)
+            first.append(remote(parts.at[:, p], held.at[:, w], w_s.at[i], w_r.at[i], (e, p)))
+            first[i].start()
+        keep = fetch(((parts.at[:, w], held.at[:, w]),), load_sem)[0]
+        yield
+        keep.wait()
+        for copy in first:
+            copy.wait()
+        keep = fetch(((held.at[e], every.at[e]),), load_sem)[0]
+        for i in range(n - 1):
+            p = flip(e, i + 1)
+            second.append(remote(held.at[p], every.at[e], ep_s.at[i], ep_r.at[i], (p, w)))
+            second[i].start()
+        yield
+        keep.wait()
+        for copy in second:
+            copy.wait()
+        total[...] = jnp.sum(jnp.sum(every[...], 0), 0)
+        store = fetch(((total, out),), load_sem)[0]
+        store.wait()
+
+    return Job(
+        [parts],
+        [jax.ShapeDtypeStruct(parts.shape[2:], parts.dtype)],
+        [
             pltpu.VMEM(parts.shape, parts.dtype),
             pltpu.VMEM(parts.shape, parts.dtype),
-            DMA((2,)),
+            pltpu.VMEM(parts.shape[2:], parts.dtype),
+            DMA((1,)),
             DMA((n_ws - 1,)),
             DMA((n_ws - 1,)),
             DMA((n - 1,)),
             DMA((n - 1,)),
         ],
-        compiler_params=pltpu.CompilerParams(collective_id=4, has_side_effects=True),
-        name="reduce_gains",
-    )(parts)
+        2,
+        body,
+        [(k, 0) for k in range(1, n)] + [(0, k) for k in range(1, n_ws)],
+    )
 
 
 def small(n_ep):
@@ -1637,11 +1642,16 @@
     grad_kv = t_dot(normed_sequence, grad_kv_rows)
     from_kv = dot_t(grad_kv_rows, kv_own).astype(bf16)
     if fused:
-        piece, from_kv, grad_query = run_jobs(
+        slot_share = t_dot(attn_tokens, normed_back)
+        kv_share = jnp.sum(from_kv.astype(f32) * normed_sequence.astype(f32), 0) / gain_one
+        gain_parts = jnp.stack([jnp.sum(slot_share * unit_one, 0) + kv_share, grad_gain_two], 0)
+        gain_parts = gain_parts.reshape(2, n_ep, n_ws, -1).transpose(1, 2, 0, 3)
+        piece, from_kv, gain_shards, grad_query = run_jobs(
             [
                 reduce_weights_job(
                     grad_kv.astype(bf16), from_kv.reshape(2, n_ws, local_tokens, width), n_ep
-                )
+                ),
+                reduce_gains_job(gain_parts.reshape(n_ep, n_ws, 1, -1)),
             ],
             [grad_job(rows_one, owner_grad_query)],
             9,
@@ -1669,13 +1679,14 @@
     grad_normed = t_dot(attn_tokens, normed_back) + from_kv.astype(f32)
     grad_input_norm, grad_gain_one = norm_back(grad_normed, unit_one, inverse_one, gain_one)
     grad_input = grad_hidden + grad_input_norm
-    gain_grads = jnp.stack([grad_gain_one, grad_gain_two], 0)
     if fused:
-        parts = gain_grads.reshape(2, n_ep, n_ws, -1).transpose(1, 2, 0, 3)
-        gain_shards = reduce_call(parts.reshape(n_ep, n_ws, 1, -1)).reshape(2, -1)
+        gain_shards = gain_shards.reshape(2, -1)
     else:
         gain_shards = lax.psum_scatter(
-            gain_grads, ("ep", "ws"), scatter_dimension=1, tiled=True
+            jnp.stack([grad_gain_one, grad_gain_two], 0),
+            ("ep", "ws"),
+            scatter_dimension=1,
+            tiled=True,
         )
     return (
         result.astype(bf16),

time: 714 us -> 705 us (0.987)
  Pallas kernels: 617 us -> 609 us
    pallas_call x1 -> x0, Pallas kernels: 8.71 us -> none  [reduce_call(): pl.pallas_call(functools.partial(reduce_kernel, n, n_ws), out_shape=jax.S...]
    unnamed x30 -> x38, local copies, waits for them, and re-layouts: 32.7 us -> 33.5 us
where the time goes in v10:
time: 705 us; the launch traced here: 700 us
  Pallas kernels  609 us (86%)
  matrix products  36.9 us (5%)
  local copies, waits for them, and re-layouts  36.7 us (5%)
  other arithmetic  11.9 us (2%)
    pallas_call x11, Pallas kernels, run_jobs(): pl.pallas_call(kernel, out_shape=outs, in_specs=[ANY] * len(args), out_sp...  577 us
    unnamed x38, local copies, waits for them, and re-layouts  33.5 us
    pallas_call x1, Pallas kernels, attend_back_call(): pl.pallas_call(functools.partial(attend_back_kernel, spans), out_shape=[j...  18.4 us
    dot_general x8, matrix products, dot(): return jnp.dot(a, b, preferred_element_type=f32)  17.9 us
    dot_general x7, matrix products, t_dot(): lax.dot_general(a, b, (((0,), (0,)), ((), ())), preferred_element_type=f32)  14.6 us
  transfers between devices with their start and end apart: 1, of which 0 were waited for; matrix products, arithmetic and copies ran while one was open for 2% of the time, Pallas kernels for 2%

profile of v10, /device:TPU:1, one launch (start us, length us, event | category | flops | bytes accessed | tf_op | source)
XLA Modules:
  0.0 700.4 jit_solution(3140340589437932112)
XLA Ops:
  0.7 4.6 collective-permute-start
  10.0 12.2 %gather_gains.1 = f32[8,4,1,128]{3,2,1,0:T(1,128)} custom-call(f32[1,128]{1,0:T(1,128)} %maximum_convert_fusion.refs_0_), custom_call_target="tpu_custom_call" | custom-call | tf_op jit(solution)/shard_map/gather_gains/pallas_call | solution.py:126
  30.3 71.6 %dispatch_weights.1 = (bf16[8,4,40,2048]{3,2,1,0:T(8,128)(2,1)}, bf16[2048,512]{1,0:T(8,128)(2,1)}, bf16[2,4,128,2048]{3,2,1,0:T(8,128)(2,1)}, bf16[2048,1408]{1,0:T(8,128)(2,1)}, bf16[2048,1408]{1,0:T(8,128)(2,1)}) custom-call(bf16[8,40,2048]{2,1,0:T(8,128)(2,1)} %bitcast.100, bf16[2048,128]{1,0:T(8,128)(2,1)} %copy-done.11, bf16[128,2048]{1,0:T(8,128)(2,1)} %copy-done.5, ...), custom_call_target="tpu_custom_call" | custom-call | tf_op jit(solution)/shard_map/dispatch_weights/pallas_call | solution.py:126
  101.9 6.3 convolution_convert_fusion.5
  108.2 4.0 convolution_convert_fusion.2
  112.2 28.8 %exchange_kv.1 = (bf16[8,160,512]{2,1,0:T(8,128)(2,1)}, bf16[2,512,512]{2,1,0:T(8,128)(2,1)}) custom-call(bf16[8,160,512]{2,1,0:T(8,128)(2,1)} %bitcast.110, bf16[2,512,512]{2,1,0:T(8,128)(2,1)} %bitcast.113), custom_call_target="tpu_custom_call" | custom-call | tf_op jit(solution)/shard_map/exchange_kv/pallas_call | solution.py:126
  141.0 13.4 %attend.1 = bf16[8,4,40,512]{3,2,1,0:T(8,128)(2,1)} custom-call(bf16[8,4,40,512]{3,2,1,0:T(8,128)(2,1)} %bitcast.91, bf16[2,512,512]{2,1,0:T(8,128)(2,1)} %get-tuple-element.46.kv_ref), custom_call_target="tpu_custom_call" | custom-call | tf_op jit(solution)/shard_map/attend/pallas_call | solution.py:1188
  154.4 62.9 %exchange_output.1 = (bf16[8,160,512]{2,1,0:T(8,128)(2,1)}, bf16[8,40,2048]{2,1,0:T(8,128)(2,1)}) custom-call(bf16[8,160,512]{2,1,0:T(8,128)(2,1)} %bitcast.93, bf16[512,2048]{1,0:T(8,128)(2,1)} %bitcast.84), custom_call_target="tpu_custom_call" | custom-call | tf_op jit(solution)/shard_map/exchange_output/pallas_call | solution.py:126
  221.5 46.9 %dispatch.1 = bf16[8,4,40,2048]{3,2,1,0:T(8,128)(2,1)} custom-call(bf16[8,40,2048]{2,1,0:T(8,128)(2,1)} %bitcast.99), custom_call_target="tpu_custom_call" | custom-call | tf_op jit(solution)/shard_map/dispatch/pallas_call | solution.py:126
  268.4 55.3 %dispatch_ffn.1 = (bf16[8,4,40,2048]{3,2,1,0:T(8,128)(2,1)}, f32[1280,1408]{1,0:T(8,128)}, f32[1280,1408]{1,0:T(8,128)}, bf16[1280,1408]{1,0:T(8,128)(2,1)}, bf16[1280,2048]{1,0:T(8,128)(2,1)}) custom-call(bf16[8,40,2048]{2,1,0:T(8,128)(2,1)} %bitcast.86, bf16[1280,2048]{1,0:T(8,128)(2,1)} %bitcast.75, bf16[2048,1408]{1,0:T(8,128)(2,1)} %get-tuple-element.48.refs_2_.refs_4_, ...), custom_call_target="tpu_custom_call" | custom-call | tf_op jit(solution)/shard_map/dispatch_ffn/pallas_call | solution.py:126
  323.7 54.6 %combine_ffn_back.1 = (bf16[8,40,2048]{2,1,0:T(8,128)(2,1)}, bf16[1280,1408]{1,0:T(8,128)(2,1)}, bf16[1280,1408]{1,0:T(8,128)(2,1)}, bf16[1280,2048]{1,0:T(8,128)(2,1)}) custom-call(bf16[8,4,40,2048]{3,2,1,0:T(8,128)(2,1)} %bitcast.90, bf16[1280,2048]{1,0:T(8,128)(2,1)} %bitcast.80, f32[1280,1408]{1,0:T(8,128)} %get-tuple-element.52.refs_2_, ...), custom_call_target="tpu_custom_call" | custom-call | tf_op jit(solution)/shard_map/combine_ffn_back/pallas_call | solution.py:126
  378.3 46.3 %combine_grad_out.1 = (bf16[8,40,2048]{2,1,0:T(8,128)(2,1)}, f32[1408,2048]{1,0:T(8,128)}) custom-call(bf16[8,4,40,2048]{3,2,1,0:T(8,128)(2,1)} %bitcast.89, bf16[1280,1408]{1,0:T(8,128)(2,1)} %get-tuple-element.56.refs_1_, bf16[1280,2048]{1,0:T(8,128)(2,1)} %bitcast.81), custom_call_target="tpu_custom_call" | custom-call | tf_op jit(solution)/shard_map/combine_grad_out/pallas_call | solution.py:126
  424.6 2.0 multiply_reduce_fusion.1
  429.2 64.9 %dispatch_exchange.1 = (bf16[8,4,40,2048]{3,2,1,0:T(8,128)(2,1)}, bf16[8,160,512]{2,1,0:T(8,128)(2,1)}, f32[2048,2,1408]{2,1,0:T(2,128)}) custom-call(bf16[8,40,2048]{2,1,0:T(8,128)(2,1)} %bitcast.101, bf16[512,2048]{1,0:T(8,128)(2,1)} %bitcast.85, bf16[1280,2048]{1,0:T(8,128)(2,1)} %bitcast.76, bf16[1280,1408]{1,0:T(8,128)(2,1)} %get-tuple-element.58.refs_3_, ...), custom_call_target="tpu_custom_call" | custom-call | tf_op jit(solution)/shard_map/dispatch_exchange/pallas_call | solution.py:126
  494.1 18.4 %attend_back.1 = (bf16[8,4,40,512]{3,2,1,0:T(8,128)(2,1)}, bf16[2,512,512]{2,1,0:T(8,128)(2,1)}) custom-call(bf16[8,4,40,512]{3,2,1,0:T(8,128)(2,1)} %bitcast.92, bf16[8,4,40,512]{3,2,1,0:T(8,128)(2,1)} %bitcast.107, bf16[2,512,512]{2,1,0:T(8,128)(2,1)} %get-tuple-element.46.kv_ref), custom_call_target="tpu_custom_call" | custom-call | tf_op jit(solution)/shard_map/attend_back/pallas_call | solution.py:1223
  512.5 69.4 %exchange_back.1 = (bf16[8,160,512]{2,1,0:T(8,128)(2,1)}, bf16[8,40,2048]{2,1,0:T(8,128)(2,1)}, bf16[2,512,512]{2,1,0:T(8,128)(2,1)}, f32[512,2048]{1,0:T(8,128)}) custom-call(bf16[8,160,512]{2,1,0:T(8,128)(2,1)} %bitcast.112, bf16[2048,512]{1,0:T(8,128)(2,1)} %bitcast.105, bf16[2,512,512]{2,1,0:T(8,128)(2,1)} %get-tuple-element.62.refs_2_, ...), custom_call_target="tpu_custom_call" | custom-call | tf_op jit(solution)/shard_map/exchange_back/pallas_call | solution.py:126
  581.9 6.3 convolution_convert_fusion.1.refs_0_
  588.3 4.4 multiply_reduce_fusion
  597.5 64.1 %reduce_weights.1 = (bf16[2048,128]{1,0:T(8,128)(2,1)}, bf16[128,2048]{1,0:T(8,128)(2,1)}, f32[1,128]{1,0:T(1,128)}, f32[2048,512]{1,0:T(8,128)}) custom-call(bf16[2048,512]{1,0:T(8,128)(2,1)} %convolution_convert_fusion.1.refs_0_, bf16[2,4,128,2048]{3,2,1,0:T(8,128)(2,1)} %bitcast.103, f32[8,4,1,128]{3,2,1,0:T(1,128)} %reshape.210.refs_2_, ...), custom_call_target="tpu_custom_call" | custom-call | tf_op jit(solution)/shard_map/reduce_weights/pallas_call | solution.py:126
  663.0 2.6 fusion.16
  667.2 2.1 copy.28
  670.9 2.0 copy.29
  673.0 16.3 %copy.30 = f32[1,2048,2,1408]{3,2,1,0:T(2,128)} copy(f32[1,2048,2,1408]{3,2,1,0:T(2,128)} %bitcast.79) | data formatting | bytes 46137344
  689.3 10.6 %copy.31 = f32[1,1408,2048]{2,1,0:T(8,128)} copy(f32[1,1408,2048]{2,1,0:T(8,128)} %bitcast.82) | data formatting | bytes 23068672
  (75 shorter events, 28.9 us)
Async XLA Ops:
  0.6 26.6 %copy-start.4 = (bf16[128,2048]{1,0:T(8,128)(2,1)S(1)}, bf16[128,2048]{1,0:T(8,128)(2,1)}, u32[]{:S(2)}) copy-start(bf16[128,2048]{1,0:T(8,128)(2,1)} %param.29) | copy-start | bytes 1572868
  0.7 28.8 %collective-permute-start = (bf16[2048,128]{1,0:T(8,128)(2,1)}, bf16[2048,128]{1,0:T(8,128)(2,1)S(1)}, u32[]{:S(2)}, u32[]{:S(2)}) collective-permute-start(bf16[2048,128]{1,0:T(8,128)(2,1)} %param.18), channel_id=1, source_target_pairs={{0,0},{1,4},{2,8},{3,12},{4,1},{5,5},{6,9},{7,13},{8,2},{9,6},{10,... | collective-permute-start | bytes 1572872 | tf_op jit(solution)/shard_map/ppermute | solution.py:1449
  25.6 3.8 copy-start.5
  25.6 2.1 copy-start.13
  29.5 0.8 copy-start.11
  101.9 6.3 copy-start.1
  101.9 6.3 copy-start.8
  154.4 64.8 %copy-start = (bf16[128,2048]{1,0:T(8,128)(2,1)S(1)}, bf16[128,2048]{1,0:T(8,128)(2,1)}, u32[]{:S(2)}) copy-start(bf16[128,2048]{1,0:T(8,128)(2,1)} %param.15) | copy-start | bytes 1572868
  217.3 1.9 copy-start.3
  581.9 6.4 copy-start.14
  581.9 6.4 copy-start.15
  581.9 6.4 copy-start.16
  592.8 2.0 copy-start.2
  592.8 3.3 copy-start.9
  663.0 2.6 copy-start.12
  663.0 3.2 copy-start.10
  663.0 4.2 copy-start.7
  667.2 3.7 copy-start.6

commit v11 on v10

--- a/solution.py
+++ b/solution.py
@@ -1093,13 +1093,11 @@
         over_y[1].wait_recv()
         to_near = remote(total_near, from_near, x_s, x_r, (near, w))
         to_near.start()
-        yield
         loads[1].wait()
         over_z[1].wait_recv()
         far.wait_recv()
         add_blocks(total, mine.at[1], from_z.at[1], last_z)
-        to_near.wait_recv()
-        add_blocks(total_rows, own.at[1, 1], core.at[1, 1], from_y.at[1], from_near)
+        yield
         partner, another = crossed()
         home = remote(total, out, h_s, h_r, partner)
         keep = pltpu.make_async_copy(total, out, sem.at[1])
@@ -1113,6 +1111,8 @@
         def _():
             keep.start()
 
+        to_near.wait_recv()
+        add_blocks(total_rows, own.at[1, 1], core.at[1, 1], from_y.at[1], from_near)
         store.start()
         for copy in over_z + list(cores.values()) + over_y + [far, to_near]:
             copy.wait_send()

time: 705 us -> 706 us (level)
  no operation moved by 1% of the time
where the time goes in v11:
time: 706 us; the launch traced here: 700 us
  Pallas kernels  609 us (86%)
  matrix products  36.9 us (5%)
  local copies, waits for them, and re-layouts  36.7 us (5%)
  other arithmetic  11.9 us (2%)
    pallas_call x11, Pallas kernels, run_jobs(): pl.pallas_call(kernel, out_shape=outs, in_specs=[ANY] * len(args), out_sp...  577 us
    unnamed x38, local copies, waits for them, and re-layouts  33.5 us
    pallas_call x1, Pallas kernels, attend_back_call(): pl.pallas_call(functools.partial(attend_back_kernel, spans), out_shape=[j...  18.4 us
    dot_general x8, matrix products, dot(): return jnp.dot(a, b, preferred_element_type=f32)  17.9 us
    dot_general x7, matrix products, t_dot(): lax.dot_general(a, b, (((0,), (0,)), ((), ())), preferred_element_type=f32)  14.6 us
  transfers between devices with their start and end apart: 1, of which 0 were waited for; matrix products, arithmetic and copies ran while one was open for 2% of the time, Pallas kernels for 2%

profile of v11, /device:TPU:1, one launch (start us, length us, event | category | flops | bytes accessed | tf_op | source)
XLA Modules:
  0.0 700.4 jit_solution(3617324810880820445)
XLA Ops:
  0.7 4.6 collective-permute-start
  10.0 12.2 %gather_gains.1 = f32[8,4,1,128]{3,2,1,0:T(1,128)} custom-call(f32[1,128]{1,0:T(1,128)} %maximum_convert_fusion.refs_0_), custom_call_target="tpu_custom_call" | custom-call | tf_op jit(solution)/shard_map/gather_gains/pallas_call | solution.py:126
  30.3 71.6 %dispatch_weights.1 = (bf16[8,4,40,2048]{3,2,1,0:T(8,128)(2,1)}, bf16[2048,512]{1,0:T(8,128)(2,1)}, bf16[2,4,128,2048]{3,2,1,0:T(8,128)(2,1)}, bf16[2048,1408]{1,0:T(8,128)(2,1)}, bf16[2048,1408]{1,0:T(8,128)(2,1)}) custom-call(bf16[8,40,2048]{2,1,0:T(8,128)(2,1)} %bitcast.100, bf16[2048,128]{1,0:T(8,128)(2,1)} %copy-done.11, bf16[128,2048]{1,0:T(8,128)(2,1)} %copy-done.5, ...), custom_call_target="tpu_custom_call" | custom-call | tf_op jit(solution)/shard_map/dispatch_weights/pallas_call | solution.py:126
  101.9 6.3 convolution_convert_fusion.5
  108.2 4.0 convolution_convert_fusion.2
  112.2 28.8 %exchange_kv.1 = (bf16[8,160,512]{2,1,0:T(8,128)(2,1)}, bf16[2,512,512]{2,1,0:T(8,128)(2,1)}) custom-call(bf16[8,160,512]{2,1,0:T(8,128)(2,1)} %bitcast.110, bf16[2,512,512]{2,1,0:T(8,128)(2,1)} %bitcast.113), custom_call_target="tpu_custom_call" | custom-call | tf_op jit(solution)/shard_map/exchange_kv/pallas_call | solution.py:126
  141.0 13.4 %attend.1 = bf16[8,4,40,512]{3,2,1,0:T(8,128)(2,1)} custom-call(bf16[8,4,40,512]{3,2,1,0:T(8,128)(2,1)} %bitcast.91, bf16[2,512,512]{2,1,0:T(8,128)(2,1)} %get-tuple-element.46.kv_ref), custom_call_target="tpu_custom_call" | custom-call | tf_op jit(solution)/shard_map/attend/pallas_call | solution.py:1188
  154.4 62.9 %exchange_output.1 = (bf16[8,160,512]{2,1,0:T(8,128)(2,1)}, bf16[8,40,2048]{2,1,0:T(8,128)(2,1)}) custom-call(bf16[8,160,512]{2,1,0:T(8,128)(2,1)} %bitcast.93, bf16[512,2048]{1,0:T(8,128)(2,1)} %bitcast.84), custom_call_target="tpu_custom_call" | custom-call | tf_op jit(solution)/shard_map/exchange_output/pallas_call | solution.py:126
  221.5 46.9 %dispatch.1 = bf16[8,4,40,2048]{3,2,1,0:T(8,128)(2,1)} custom-call(bf16[8,40,2048]{2,1,0:T(8,128)(2,1)} %bitcast.99), custom_call_target="tpu_custom_call" | custom-call | tf_op jit(solution)/shard_map/dispatch/pallas_call | solution.py:126
  268.4 55.3 %dispatch_ffn.1 = (bf16[8,4,40,2048]{3,2,1,0:T(8,128)(2,1)}, f32[1280,1408]{1,0:T(8,128)}, f32[1280,1408]{1,0:T(8,128)}, bf16[1280,1408]{1,0:T(8,128)(2,1)}, bf16[1280,2048]{1,0:T(8,128)(2,1)}) custom-call(bf16[8,40,2048]{2,1,0:T(8,128)(2,1)} %bitcast.86, bf16[1280,2048]{1,0:T(8,128)(2,1)} %bitcast.75, bf16[2048,1408]{1,0:T(8,128)(2,1)} %get-tuple-element.48.refs_2_.refs_4_, ...), custom_call_target="tpu_custom_call" | custom-call | tf_op jit(solution)/shard_map/dispatch_ffn/pallas_call | solution.py:126
  323.7 54.6 %combine_ffn_back.1 = (bf16[8,40,2048]{2,1,0:T(8,128)(2,1)}, bf16[1280,1408]{1,0:T(8,128)(2,1)}, bf16[1280,1408]{1,0:T(8,128)(2,1)}, bf16[1280,2048]{1,0:T(8,128)(2,1)}) custom-call(bf16[8,4,40,2048]{3,2,1,0:T(8,128)(2,1)} %bitcast.90, bf16[1280,2048]{1,0:T(8,128)(2,1)} %bitcast.80, f32[1280,1408]{1,0:T(8,128)} %get-tuple-element.52.refs_2_, ...), custom_call_target="tpu_custom_call" | custom-call | tf_op jit(solution)/shard_map/combine_ffn_back/pallas_call | solution.py:126
  378.3 46.3 %combine_grad_out.1 = (bf16[8,40,2048]{2,1,0:T(8,128)(2,1)}, f32[1408,2048]{1,0:T(8,128)}) custom-call(bf16[8,4,40,2048]{3,2,1,0:T(8,128)(2,1)} %bitcast.89, bf16[1280,1408]{1,0:T(8,128)(2,1)} %get-tuple-element.56.refs_1_, bf16[1280,2048]{1,0:T(8,128)(2,1)} %bitcast.81), custom_call_target="tpu_custom_call" | custom-call | tf_op jit(solution)/shard_map/combine_grad_out/pallas_call | solution.py:126
  424.6 2.0 multiply_reduce_fusion.1
  429.2 64.9 %dispatch_exchange.1 = (bf16[8,4,40,2048]{3,2,1,0:T(8,128)(2,1)}, bf16[8,160,512]{2,1,0:T(8,128)(2,1)}, f32[2048,2,1408]{2,1,0:T(2,128)}) custom-call(bf16[8,40,2048]{2,1,0:T(8,128)(2,1)} %bitcast.101, bf16[512,2048]{1,0:T(8,128)(2,1)} %bitcast.85, bf16[1280,2048]{1,0:T(8,128)(2,1)} %bitcast.76, bf16[1280,1408]{1,0:T(8,128)(2,1)} %get-tuple-element.58.refs_3_, ...), custom_call_target="tpu_custom_call" | custom-call | tf_op jit(solution)/shard_map/dispatch_exchange/pallas_call | solution.py:126
  494.1 18.4 %attend_back.1 = (bf16[8,4,40,512]{3,2,1,0:T(8,128)(2,1)}, bf16[2,512,512]{2,1,0:T(8,128)(2,1)}) custom-call(bf16[8,4,40,512]{3,2,1,0:T(8,128)(2,1)} %bitcast.92, bf16[8,4,40,512]{3,2,1,0:T(8,128)(2,1)} %bitcast.107, bf16[2,512,512]{2,1,0:T(8,128)(2,1)} %get-tuple-element.46.kv_ref), custom_call_target="tpu_custom_call" | custom-call | tf_op jit(solution)/shard_map/attend_back/pallas_call | solution.py:1223
  512.5 69.4 %exchange_back.1 = (bf16[8,160,512]{2,1,0:T(8,128)(2,1)}, bf16[8,40,2048]{2,1,0:T(8,128)(2,1)}, bf16[2,512,512]{2,1,0:T(8,128)(2,1)}, f32[512,2048]{1,0:T(8,128)}) custom-call(bf16[8,160,512]{2,1,0:T(8,128)(2,1)} %bitcast.112, bf16[2048,512]{1,0:T(8,128)(2,1)} %bitcast.105, bf16[2,512,512]{2,1,0:T(8,128)(2,1)} %get-tuple-element.62.refs_2_, ...), custom_call_target="tpu_custom_call" | custom-call | tf_op jit(solution)/shard_map/exchange_back/pallas_call | solution.py:126
  581.9 6.3 convolution_convert_fusion.1.refs_0_
  588.3 4.4 multiply_reduce_fusion
  597.5 64.1 %reduce_weights.1 = (bf16[2048,128]{1,0:T(8,128)(2,1)}, bf16[128,2048]{1,0:T(8,128)(2,1)}, f32[1,128]{1,0:T(1,128)}, f32[2048,512]{1,0:T(8,128)}) custom-call(bf16[2048,512]{1,0:T(8,128)(2,1)} %convolution_convert_fusion.1.refs_0_, bf16[2,4,128,2048]{3,2,1,0:T(8,128)(2,1)} %bitcast.103, f32[8,4,1,128]{3,2,1,0:T(1,128)} %reshape.210.refs_2_, ...), custom_call_target="tpu_custom_call" | custom-call | tf_op jit(solution)/shard_map/reduce_weights/pallas_call | solution.py:126
  663.1 2.6 fusion.16
  667.3 2.1 copy.28
  671.0 2.0 copy.29
  673.0 16.3 %copy.30 = f32[1,2048,2,1408]{3,2,1,0:T(2,128)} copy(f32[1,2048,2,1408]{3,2,1,0:T(2,128)} %bitcast.79) | data formatting | bytes 46137344
  689.3 10.6 %copy.31 = f32[1,1408,2048]{2,1,0:T(8,128)} copy(f32[1,1408,2048]{2,1,0:T(8,128)} %bitcast.82) | data formatting | bytes 23068672
  (75 shorter events, 28.9 us)
Async XLA Ops:
  0.6 26.6 %copy-start.4 = (bf16[128,2048]{1,0:T(8,128)(2,1)S(1)}, bf16[128,2048]{1,0:T(8,128)(2,1)}, u32[]{:S(2)}) copy-start(bf16[128,2048]{1,0:T(8,128)(2,1)} %param.29) | copy-start | bytes 1572868
  0.7 28.8 %collective-permute-start = (bf16[2048,128]{1,0:T(8,128)(2,1)}, bf16[2048,128]{1,0:T(8,128)(2,1)S(1)}, u32[]{:S(2)}, u32[]{:S(2)}) collective-permute-start(bf16[2048,128]{1,0:T(8,128)(2,1)} %param.18), channel_id=1, source_target_pairs={{0,0},{1,4},{2,8},{3,12},{4,1},{5,5},{6,9},{7,13},{8,2},{9,6},{10,... | collective-permute-start | bytes 1572872 | tf_op jit(solution)/shard_map/ppermute | solution.py:1449
  25.6 3.8 copy-start.5
  25.6 2.1 copy-start.13
  29.5 0.8 copy-start.11
  101.9 6.3 copy-start.1
  101.9 6.3 copy-start.8
  154.4 64.8 %copy-start = (bf16[128,2048]{1,0:T(8,128)(2,1)S(1)}, bf16[128,2048]{1,0:T(8,128)(2,1)}, u32[]{:S(2)}) copy-start(bf16[128,2048]{1,0:T(8,128)(2,1)} %param.15) | copy-start | bytes 1572868
  217.3 1.9 copy-start.3
  581.9 6.4 copy-start.14
  581.9 6.4 copy-start.15
  581.9 6.4 copy-start.16
  592.8 2.0 copy-start.2
  592.8 3.3 copy-start.9
  663.0 2.6 copy-start.12
  663.0 3.2 copy-start.10
  663.0 4.2 copy-start.7
  667.2 3.7 copy-start.6
